TPU v7x, 32 devices: a whole 2x2x4 slice. The times are simulated.
32 devices in a mesh: dp: 8 (over z, x), mp: 4 (over y, core).
Axes of the slice: x: 2, y: 2, z: 4, core: 2. Of those that a mesh axis runs over, the one named last changes fastest.
Arguments:
- table: float32 [25088, 512], P(('dp', 'mp')), may hold values from -6 to 6
- row_acc: float32 [25088], P(('dp', 'mp')), may hold values from 3.637979e-12 to 5.820766e-11
- uvqk_weight: float32 [512, 2048], replicated, may hold values from -0.25 to 0.25
- out_weight: float32 [512, 512], replicated, may hold values from -0.25 to 0.25
- time_bias: float32 [8, 32], replicated, may hold values from -0.6 to 0.6
- gains: float32 [3, 512], replicated, may hold values from 0.5 to 1.5
- uvqk_m: float32 [512, 2048], replicated, may hold values from -0.00032552084 to 0.00032552084
- uvqk_v: float32 [512, 2048], replicated, may hold values from 3.1370866e-09 to 5.0193385e-08
- out_m: float32 [512, 512], replicated, may hold values from -0.00032552084 to 0.00032552084
- out_v: float32 [512, 512], replicated, may hold values from 3.1370866e-09 to 5.0193385e-08
- bias_m: float32 [8, 32], replicated, may hold values from -0.00032552084 to 0.00032552084
- bias_v: float32 [8, 32], replicated, may hold values from 3.1370866e-09 to 5.0193385e-08
- gain_m: float32 [3, 512], replicated, may hold values from -0.00032552084 to 0.00032552084
- gain_v: float32 [3, 512], replicated, may hold values from 3.1370866e-09 to 5.0193385e-08
- lengths: int32 [32], P(('dp', 'mp')), may hold values from 1 to 1024, as said below
- time_buckets: int32 [32, 1024], P(('dp', 'mp')), may hold values from 0 to 31
- item_rows: int32 [49152], P(('dp', 'mp')), may hold values from 0 to 783
- row_owner: int32 [49152, 1], P(('dp', 'mp')), may hold values from 0 to 31; in each aligned block of 1536 rows (0 to 1535, 1536 to 3071, ...) at most 96 rows name the same one
Outputs:
- new_table: float32 [25088, 512], P(('dp', 'mp'))
- new_acc: float32 [25088], P(('dp', 'mp'))
- uvqk_step: float32 [512, 2048], replicated
- uvqk_m_new: float32 [512, 2048], replicated
- uvqk_v_new: float32 [512, 2048], replicated
- out_step: float32 [512, 512], replicated
- out_m_new: float32 [512, 512], replicated
- out_v_new: float32 [512, 512], replicated
- bias_step: float32 [8, 32], replicated
- bias_m_new: float32 [8, 32], replicated
- bias_v_new: float32 [8, 32], replicated
- gain_step: float32 [3, 512], replicated
- gain_m_new: float32 [3, 512], replicated
- gain_v_new: float32 [3, 512], replicated
- summary: float32 [3], replicated
- attention_rms: float32 [1], replicated
Inputs may be any that keep to these rules, and one draw needn't show every extreme that they name: `lengths`: events of a history fill its first positions, the rest is padding. `row_owner`: among the 1536 requests of one device no owner is named more than 96 times.
All inputs are finite; a program needn't handle non-finite values.
Results may differ from a plain program's by a relative error of at most 0.0083.
Values may be sent and summed in bfloat16 or wider, within the bound.
No kernel may reach another device: no remote copies, remote signals or barrier semaphores. Data moves between devices by JAX's collectives and lax.ppermute only.
A program may use at most 128 MiB of HBM per device.

v0:
```python
import math

import jax
import jax.numpy as jnp
from jax import lax
from jax.sharding import PartitionSpec as P

D = 512
H = 8
NB = 32


EPSILON = 1e-06
ROW_RATE = 0.2
LEARN_RATE = 0.01
BETA_ONE = 0.9
BETA_TWO = 0.95
ADAM_EPSILON = 1e-08
WEIGHT_DECAY = 0.1


def silu_grad(values):
    sigma = jax.nn.sigmoid(values)
    return sigma * (1.0 + values * (1.0 - sigma))


def rms_norm(values, gain_row):
    recip_norm = lax.rsqrt(jnp.mean(values * values, -1, keepdims=True) + EPSILON)
    return (values * recip_norm * gain_row, recip_norm)


def norm_back(grad_n, values, recip_norm, gain_row):
    grad_gain = jnp.sum(grad_n * values * recip_norm, 0)
    scaled = grad_n * gain_row
    grad_in = recip_norm * scaled - values * recip_norm**3 * jnp.mean(
        scaled * values, -1, keepdims=True
    )
    return (grad_in, grad_gain)


def root_mean(values):
    return jnp.sqrt(jnp.mean(values * values, -1) + EPSILON)


def attend_scores(query_blk, key_seq, bias_seq, block_start, length):
    score_scale = query_blk.shape[-1] ** (-0.5)
    raw_scores = jnp.einsum("qhd,khd->hqk", query_blk, key_seq, preferred_element_type=jnp.float32)
    scores = raw_scores * score_scale + bias_seq[:, None, :]
    query_pos = block_start + jnp.arange(query_blk.shape[0], dtype=jnp.int32)
    key_pos = jnp.arange(key_seq.shape[0], dtype=jnp.int32)
    keep_mask = (key_pos[None, :] <= query_pos[:, None]) & (key_pos[None, :] < length)
    weight = jnp.where(keep_mask, 1.0, 0.0).astype(jnp.float32) / length.astype(jnp.float32)
    return (scores, weight)


def pick_block(array_four, sequence, block_start, block_rows):
    whole_seq = lax.dynamic_index_in_dim(array_four, sequence, 0, keepdims=False)
    return lax.dynamic_slice_in_dim(whole_seq, block_start, block_rows, 0)


def adam_update(weight, gradient, first, second, decay):
    first_new = BETA_ONE * first + (1.0 - BETA_ONE) * gradient
    second_new = BETA_TWO * second + (1.0 - BETA_TWO) * gradient * gradient
    update = -LEARN_RATE * (first_new / (jnp.sqrt(second_new) + ADAM_EPSILON) + decay * weight)
    return (update, first_new, second_new)


def per_device(
    table,
    row_acc,
    uvqk_weight,
    out_weight,
    time_bias,
    gains,
    uvqk_m,
    uvqk_v,
    out_m,
    out_v,
    bias_m,
    bias_v,
    gain_m,
    gain_v,
    lengths,
    time_buckets,
    item_rows,
    row_owner,
):
    devices = lax.axis_size(("dp", "mp"))
    requests = item_rows.shape[0]
    capacity = max(2, 2 * requests // devices)
    sequences, seq_len = time_buckets.shape
    tokens = sequences * seq_len
    model_width = table.shape[1]
    head_dim = model_width // H
    block_rows = min(512, seq_len)
    blocks = seq_len // block_rows
    owners = row_owner[:, 0]
    owner_hits = (owners[:, None] == jnp.arange(devices, dtype=jnp.int32)[None, :]).astype(
        jnp.int32
    )
    slot_rank = jnp.sum((jnp.cumsum(owner_hits, axis=0) - 1) * owner_hits, axis=1)
    slot_index = owners * capacity + slot_rank
    send_ids = jnp.zeros((devices * capacity,), jnp.int32).at[slot_index].set(item_rows)
    recv_ids = lax.all_to_all(
        send_ids.reshape(devices, capacity), ("dp", "mp"), split_axis=0, concat_axis=0, tiled=True
    ).reshape(-1)
    served = table[recv_ids].astype(jnp.bfloat16)
    returned = lax.all_to_all(
        served.reshape(devices, capacity, model_width),
        ("dp", "mp"),
        split_axis=0,
        concat_axis=0,
        tiled=True,
    )
    fetched = returned.reshape(-1, model_width)[slot_index]
    token_rows = fetched[:tokens]
    neg_rows = fetched[tokens:]
    inputs = token_rows.astype(jnp.float32)
    normed_one, recip_one = rms_norm(inputs, gains[0])
    normed_low = normed_one.astype(jnp.bfloat16)
    uvqk_low = uvqk_weight.astype(jnp.bfloat16)
    project = jnp.dot(normed_low, uvqk_low, preferred_element_type=jnp.float32)
    active = jax.nn.silu(project)
    gate_u = active[:, :model_width]
    value_qk = active[:, model_width:].astype(jnp.bfloat16)
    value4 = value_qk[:, :model_width].reshape(sequences, seq_len, H, head_dim)
    query4 = value_qk[:, model_width : 2 * model_width].reshape(sequences, seq_len, H, head_dim)
    key4 = value_qk[:, 2 * model_width :].reshape(sequences, seq_len, H, head_dim)
    bucket_hits = (
        time_buckets[:, :, None] == jnp.arange(NB, dtype=jnp.int32)[None, None, :]
    ).astype(jnp.float32)
    key_bias = jnp.einsum("snb,hb->shn", bucket_hits, time_bias, precision=lax.Precision.HIGHEST)

    def block_inputs(block_id):
        sequence = block_id // blocks
        block_start = block_id % blocks * block_rows
        query_blk = pick_block(query4, sequence, block_start, block_rows)
        key_seq = lax.dynamic_index_in_dim(key4, sequence, 0, keepdims=False)
        value_seq = lax.dynamic_index_in_dim(value4, sequence, 0, keepdims=False)
        bias_seq = lax.dynamic_index_in_dim(key_bias, sequence, 0, keepdims=False)
        length = lax.dynamic_index_in_dim(lengths, sequence, 0, keepdims=False)
        scores, weight = attend_scores(query_blk, key_seq, bias_seq, block_start, length)
        attn_low = (jax.nn.silu(scores) * weight[None]).astype(jnp.bfloat16)
        return (sequence, block_start, query_blk, key_seq, value_seq, scores, weight, attn_low)

    def forward_block(block_id):
        parts_here = block_inputs(block_id)
        attn_low, value_seq = (parts_here[7], parts_here[4])
        result = jnp.einsum("hqk,khd->qhd", attn_low, value_seq, preferred_element_type=jnp.float32)
        return result.reshape(block_rows, model_width)

    attended = lax.map(forward_block, jnp.arange(sequences * blocks, dtype=jnp.int32)).reshape(
        tokens, model_width
    )
    normed_two, recip_two = rms_norm(attended, gains[1])
    gated_low = (normed_two * gate_u).astype(jnp.bfloat16)
    out_low = out_weight.astype(jnp.bfloat16)
    branch = jnp.dot(gated_low, out_low, preferred_element_type=jnp.float32)
    mixed = inputs + branch
    normed_three, recip_three = rms_norm(mixed, gains[2])
    final_low = normed_three.astype(jnp.bfloat16)
    rows_three = token_rows.reshape(sequences, seq_len, model_width)
    next_rows = jnp.concatenate(
        [rows_three[:, 1:], jnp.zeros((sequences, 1, model_width), jnp.bfloat16)], 1
    ).reshape(tokens, model_width)
    logit_scale = 2.0 / math.sqrt(D)
    final_f = final_low.astype(jnp.float32)
    next_f = next_rows.astype(jnp.float32)
    target = jnp.sum(final_f * next_f, -1) * logit_scale
    negative = (
        lax.dot_general(
            final_low, neg_rows, (((1,), (1,)), ((), ())), preferred_element_type=jnp.float32
        )
        * logit_scale
    )
    top_logit = jnp.maximum(jnp.max(negative, -1), target)
    log_total = top_logit + jnp.log(
        jnp.exp(target - top_logit) + jnp.sum(jnp.exp(negative - top_logit[:, None]), -1)
    )
    token_pos = jnp.arange(seq_len, dtype=jnp.int32)[None, :].reshape(-1)
    token_len = jnp.broadcast_to(lengths[:, None], (sequences, seq_len)).reshape(-1)
    valid_rows = token_pos < token_len - 1
    live_rows = token_pos < token_len
    local_sums = jnp.stack(
        [
            jnp.sum(jnp.where(valid_rows, log_total - target, 0.0)),
            jnp.sum(jnp.where(live_rows, root_mean(inputs), 0.0)),
            jnp.sum(jnp.where(live_rows, root_mean(attended), 0.0)),
            jnp.sum(jnp.where(live_rows, root_mean(branch), 0.0)),
        ]
    )
    total_tokens = float(tokens * devices)
    summed_stats = lax.psum(local_sums, ("dp", "mp")) / total_tokens
    summary = jnp.stack([summed_stats[0], summed_stats[1], summed_stats[3]])
    attention_rms = summed_stats[2:3]
    row_weight = jnp.where(valid_rows, 1.0 / total_tokens, 0.0).astype(jnp.float32)
    grad_target = row_weight * (jnp.exp(target - log_total) - 1.0)
    grad_neg = (row_weight[:, None] * jnp.exp(negative - log_total[:, None])).astype(jnp.bfloat16)
    grad_final = (grad_target * logit_scale)[:, None] * next_f + logit_scale * jnp.dot(
        grad_neg, neg_rows, preferred_element_type=jnp.float32
    )
    grad_negs = logit_scale * lax.dot_general(
        grad_neg, final_low, (((0,), (0,)), ((), ())), preferred_element_type=jnp.float32
    )
    grad_next = ((grad_target * logit_scale)[:, None] * final_f).reshape(
        sequences, seq_len, model_width
    )
    grad_shift = jnp.concatenate(
        [jnp.zeros((sequences, 1, model_width), jnp.float32), grad_next[:, :-1]], 1
    ).reshape(tokens, model_width)
    grad_mixed, grad_g3 = norm_back(grad_final, mixed, recip_three, gains[2])
    grad_branch = grad_mixed.astype(jnp.bfloat16)
    grad_out = lax.dot_general(
        gated_low, grad_branch, (((0,), (0,)), ((), ())), preferred_element_type=jnp.float32
    )
    grad_gated = lax.dot_general(
        grad_branch, out_low, (((1,), (1,)), ((), ())), preferred_element_type=jnp.float32
    )
    grad_u = grad_gated * normed_two
    grad_attended, grad_g2 = norm_back(grad_gated * gate_u, attended, recip_two, gains[1])
    out_grad4 = grad_attended.astype(jnp.bfloat16).reshape(sequences, seq_len, H, head_dim)

    def backward_block(block_id, running):
        grad_query, grad_key, grad_value, grad_bias = running
        sequence, block_start, query_blk, key_seq, value_seq, scores, weight, attn_low = (
            block_inputs(block_id)
        )
        score_scale = head_dim ** (-0.5)
        out_grad_blk = pick_block(out_grad4, sequence, block_start, block_rows)
        grad_attn = jnp.einsum(
            "qhd,khd->hqk", out_grad_blk, value_seq, preferred_element_type=jnp.float32
        )
        grad_scores = (grad_attn * weight[None] * silu_grad(scores)).astype(jnp.bfloat16)
        query_add = (
            jnp.einsum("hqk,khd->qhd", grad_scores, key_seq, preferred_element_type=jnp.float32)
            * score_scale
        )
        key_add = (
            jnp.einsum("hqk,qhd->khd", grad_scores, query_blk, preferred_element_type=jnp.float32)
            * score_scale
        )
        value_add = jnp.einsum(
            "hqk,qhd->khd", attn_low, out_grad_blk, preferred_element_type=jnp.float32
        )
        bias_add = jnp.sum(grad_scores, axis=1, dtype=jnp.float32)
        grad_query = lax.dynamic_update_slice(
            grad_query, query_add[None], (sequence, block_start, 0, 0)
        )
        grad_key = grad_key.at[sequence].add(key_add)
        grad_value = grad_value.at[sequence].add(value_add)
        grad_bias = grad_bias.at[sequence].add(bias_add)
        return (grad_query, grad_key, grad_value, grad_bias)

    zeros_four = jnp.zeros((sequences, seq_len, H, head_dim), jnp.float32)
    grad_query, grad_key, grad_value, grad_keybias = lax.fori_loop(
        0,
        sequences * blocks,
        backward_block,
        (zeros_four, zeros_four, zeros_four, jnp.zeros((sequences, H, seq_len), jnp.float32)),
    )
    grad_timebias = jnp.einsum(
        "shn,snb->hb", grad_keybias, bucket_hits, precision=lax.Precision.HIGHEST
    )
    grad_active = jnp.concatenate(
        [
            grad_u,
            grad_value.reshape(tokens, model_width),
            grad_query.reshape(tokens, model_width),
            grad_key.reshape(tokens, model_width),
        ],
        1,
    )
    grad_project = (grad_active * silu_grad(project)).astype(jnp.bfloat16)
    grad_uvqk = lax.dot_general(
        normed_low, grad_project, (((0,), (0,)), ((), ())), preferred_element_type=jnp.float32
    )
    grad_normed = lax.dot_general(
        grad_project, uvqk_low, (((1,), (1,)), ((), ())), preferred_element_type=jnp.float32
    )
    grad_inputs, grad_g1 = norm_back(grad_normed, inputs, recip_one, gains[0])
    grad_tokens = grad_inputs + grad_mixed + grad_shift
    row_grads = jnp.concatenate([grad_tokens, grad_negs], 0)
    send_grads = (
        jnp.zeros((devices * capacity, model_width), jnp.float32).at[slot_index].set(row_grads)
    )
    recv_grads = lax.all_to_all(
        send_grads.reshape(devices, capacity, model_width),
        ("dp", "mp"),
        split_axis=0,
        concat_axis=0,
        tiled=True,
    )
    summed_rows = jnp.zeros_like(table).at[recv_ids].add(recv_grads.reshape(-1, model_width))
    new_acc = row_acc + jnp.mean(summed_rows * summed_rows, -1)
    new_table = table - ROW_RATE * summed_rows * lax.rsqrt(new_acc)[:, None]
    grad_gains = jnp.stack([grad_g1, grad_g2, grad_g3])
    sum_uvqk, sum_out, sum_bias, sum_gains = lax.psum(
        (grad_uvqk, grad_out, grad_timebias, grad_gains), ("dp", "mp")
    )
    uvqk_step, uvqk_m_new, uvqk_v_new = adam_update(
        uvqk_weight, sum_uvqk, uvqk_m, uvqk_v, WEIGHT_DECAY
    )
    out_step, out_m_new, out_v_new = adam_update(out_weight, sum_out, out_m, out_v, WEIGHT_DECAY)
    bias_step, bias_m_new, bias_v_new = adam_update(time_bias, sum_bias, bias_m, bias_v, 0.0)
    gain_step, gain_m_new, gain_v_new = adam_update(gains, sum_gains, gain_m, gain_v, 0.0)
    return (
        new_table,
        new_acc,
        uvqk_step,
        uvqk_m_new,
        uvqk_v_new,
        out_step,
        out_m_new,
        out_v_new,
        bias_step,
        bias_m_new,
        bias_v_new,
        gain_step,
        gain_m_new,
        gain_v_new,
        summary,
        attention_rms,
    )


def solution(mesh):
    return jax.shard_map(
        per_device,
        mesh=mesh,
        in_specs=(
            P(("dp", "mp"), None),
            P(("dp", "mp")),
            P(),
            P(),
            P(),
            P(),
            P(),
            P(),
            P(),
            P(),
            P(),
            P(),
            P(),
            P(),
            P(("dp", "mp")),
            P(("dp", "mp"), None),
            P(("dp", "mp")),
            P(("dp", "mp"), None),
        ),
        out_specs=(
            P(("dp", "mp"), None),
            P(("dp", "mp")),
            P(),
            P(),
            P(),
            P(),
            P(),
            P(),
            P(),
            P(),
            P(),
            P(),
            P(),
            P(),
            P(),
            P(),
        ),
        check_vma=False,
    )
```

profile of v0, /device:TPU:0, one launch (start us, length us, event | category | flops | bytes accessed | tf_op | source)
XLA Modules:
  0.0 615.0 jit_solution(13958703298946148381)
XLA Ops:
  8.1 9.1 %reduce-window.6 = s32[32,12,128]{2,1,0:T(8,128)S(1)} reduce-window(s32[32,12,128]{2,1,0:T(8,128)S(1)} %fusion.82, s32[]{:T(128)} %constant.415.clone.1), window={size=1x1x128 pad=0_0x0_0x127_0}, to_apply=%region_0.0 | reduce-window | flops 6242304 | bytes 393220 | tf_op jit(solution)/shard_map/reduce-window
  17.9 6.4 %scatter_custom_fusion = s32[3072]{0:T(1024)S(1)} fusion(s32[1536]{0:T(1024)S(1)} %fusion.91, s32[1536]{0:T(1024)} %param.44, s32[]{:T(128)} %constant.415.clone.1), kind=kCustom, calls=%fused_computation.168 | custom fusion | bytes 12800 | tf_op jit(solution)/shard_map/scatter | solution.py:103
  24.3 14.3 %all_to_all.19 = s32[32,1,96]{2,1,0:T(1,128)S(1)} all-to-all(s32[32,1,96]{2,1,0:T(1,128)S(1)} %all_to_all.12), channel_id=1, replica_groups=mesh['dp'=8,'mp'=4] {'dp','mp'}, dimensions={0} | all-to-all | bytes 24576 | tf_op jit(solution)/shard_map/all_to_all | solution.py:104
  40.0 12.4 %gather_fusion = bf16[3072,512]{1,0:T(8,128)(2,1)} fusion(f32[784,512]{1,0:T(8,128)S(1)} %copy-done.1, s32[3072]{0:T(1024)S(1)} %broadcast_clamp_fusion), kind=kCustom, calls=%fused_computation | custom fusion | bytes 6303744 | tf_op jit(solution)/shard_map/gather | solution.py:107
  57.2 69.9 %all-to-all-done.1 = bf16[32,96,512]{2,1,0:T(8,128)(2,1)S(1)} async-done(((bf16[32,96,512]{2,1,0:T(8,128)(2,1)}), bf16[32,96,512]{2,1,0:T(8,128)(2,1)S(1)}, u32[]{:S(2)}, u32[]{:S(2)}) %all-to-all-start.1) | async-done | bytes 3145760 | tf_op jit(solution)/shard_map/all_to_all | solution.py:108
  127.1 5.4 gather_fusion.1
  135.8 9.9 %fusion.104 = (bf16[1024,2048]{1,0:T(8,128)(2,1)S(1)}, f32[1024,2048]{1,0:T(8,128)}, f32[1024,2048]{1,0:T(8,128)}) fusion(f32[512,2048]{1,0:T(8,128)} %param.30, bf16[1024,512]{0,1:T(8,128)(2,1)S(1)} %copy.92, f32[512]{0:T(512)S(1)} %bitcast.240, f32[1024]{0:T(1024)S(1)} %get-tuple-element.616), kind=kOutput, calls=%fused_computation.198 | convolution fusion | flops 2161115136 | bytes 26220544 | tf_op jit(solution)/shard_map/dot_general | solution.py:122
  149.2 33.1 %while.37 = (s32[]{:T(128)}, f32[2,512,512]{1,2,0:T(8,128)}, s32[2]{0:T(128)S(1)}, bf16[1,1024,8,64]{1,3,2,0:T(8,128)(2,1)}, bf16[1,1024,8,64]{1,3,2,0:T(8,128)(...) while((s32[]{:T(128)}, f32[2,512,512]{1,2,0:T(8,128)}, ...), condition=%wide.region_6.7_spmd, body=%wide.region_5.6_spmd.sunk | while | flops 1109394944 | bytes 10000712 | solution.py:152
  153.2 10.4 %fusion.134 = f32[8,512,64]{1,2,0:T(8,128)} fusion(f32[512,1024]{1,0:T(8,128)S(1)} %select_divide_fusion.4, f32[8,1024]{1,0:T(8,128)S(1)} %bitcast.249, bf16[1,1024,8,64]{1,3,2,0:T(8,128)(2,1)} %get-tuple-element.800, bf16[1,1024,8,64]{1,3,2,0:T(8,128)(2,1)S(1)} %get-tuple-element.796, bf16[1,1024,8,64]{1,3,2,0:T(8,128)(2,1)} %get-tuple-element.795, ...), kind=kOutput, calls=%fused_computation.9.clone.1 | convolution fusion | flops 1107296256 | bytes 5799940 | tf_op jit(solution)/shard_map/while/body/eval_jaxpr/hqk,khd->qhd/dot_general | solution.py:149
  169.6 10.4 %fusion.134 = f32[8,512,64]{1,2,0:T(8,128)} fusion(f32[512,1024]{1,0:T(8,128)S(1)} %select_divide_fusion.4, f32[8,1024]{1,0:T(8,128)S(1)} %bitcast.249, bf16[1,1024,8,64]{1,3,2,0:T(8,128)(2,1)} %get-tuple-element.800, bf16[1,1024,8,64]{1,3,2,0:T(8,128)(2,1)S(1)} %get-tuple-element.796, bf16[1,1024,8,64]{1,3,2,0:T(8,128)(2,1)} %get-tuple-element.795, ...), kind=kOutput, calls=%fused_computation.9.clone.1 | convolution fusion | flops 1107296256 | bytes 5799940 | tf_op jit(solution)/shard_map/while/body/eval_jaxpr/hqk,khd->qhd/dot_general | solution.py:149
  211.0 75.1 %while.38 = (s32[]{:T(128)}, f32[1,1024,8,64]{1,3,2,0:T(8,128)}, f32[1,1024,8,64]{1,3,2,0:T(8,128)S(1)}, f32[1,1024,8,64]{1,3,2,0:T(8,128)}, f32[1,8,1024]{2,1,0...) while((s32[]{:T(128)}, f32[1,1024,8,64]{1,3,2,0:T(8,128)}, ...), condition=%wide.region_18.19_spmd.clone, body=%wide.region_14.18_spmd.clone.sunk | while | flops 2782676480 | bytes 193141392 | solution.py:255
  216.3 5.7 copy-done
  222.0 7.3 %add_select_fusion.7 = f32[1,1024,8,64]{1,3,2,0:T(8,128)} fusion(f32[1,1024,8,64]{1,3,2,0:T(8,128)} %get-tuple-element.828, f32[8,512,1024]{2,1,0:T(8,128)S(1)} %fusion.142, f32[8,1024]{1,0:T(8,128)S(1)} %bitcast.250, f32[512,1024]{1,0:T(8,128)S(1)} %select_divide_fusion.5, pred[]{:T(512)S(6)} %compare.90, pred[]{:T(512)} %and_reduce_fusion.4, ...), kind=kOutput, calls=%fused_computation.26.clone.1 | convolution fusion | flops 571998208 | bytes 23625734 | tf_op jit(solution)/shard_map/while/body/eval_jaxpr/hqk,qhd->khd/dot_general | solution.py:242
  229.3 11.5 %convert_reduce_fusion.2 = (f32[8,1024]{1,0:T(8,128)S(1)}, bf16[8,512,1024]{2,1,0:T(8,128)(2,1)S(1)}) fusion(f32[8,1024]{1,0:T(8,128)S(1)} %bitcast.251, f32[8,512,1024]{2,1,0:T(8,128)} %copy-done, f32[512,1024]{1,0:T(8,128)S(1)} %select_divide_fusion.5, bf16[1,1024,8,64]{1,3,2,0:T(8,128)(2,1)S(1)} %copy-done.27, ...), kind=kOutput, calls=%fused_computation.20.clone.1 | convolution fusion | flops 595582976 | bytes 28901380 | tf_op jit(solution)/shard_map/while/body/eval_jaxpr/qhd,khd->hqk/dot_general | solution.py:230
  253.2 5.7 copy-done
  258.9 8.3 %add_select_fusion.7 = f32[1,1024,8,64]{1,3,2,0:T(8,128)} fusion(f32[1,1024,8,64]{1,3,2,0:T(8,128)} %get-tuple-element.828, f32[8,512,1024]{2,1,0:T(8,128)S(1)} %fusion.142, f32[8,1024]{1,0:T(8,128)S(1)} %bitcast.250, f32[512,1024]{1,0:T(8,128)S(1)} %select_divide_fusion.5, pred[]{:T(512)S(6)} %compare.90, pred[]{:T(512)} %and_reduce_fusion.4, ...), kind=kOutput, calls=%fused_computation.26.clone.1 | convolution fusion | flops 571998208 | bytes 23625734 | tf_op jit(solution)/shard_map/while/body/eval_jaxpr/hqk,qhd->khd/dot_general | solution.py:242
  267.2 11.4 %convert_reduce_fusion.2 = (f32[8,1024]{1,0:T(8,128)S(1)}, bf16[8,512,1024]{2,1,0:T(8,128)(2,1)S(1)}) fusion(f32[8,1024]{1,0:T(8,128)S(1)} %bitcast.251, f32[8,512,1024]{2,1,0:T(8,128)} %copy-done, f32[512,1024]{1,0:T(8,128)S(1)} %select_divide_fusion.5, bf16[1,1024,8,64]{1,3,2,0:T(8,128)(2,1)S(1)} %copy-done.27, ...), kind=kOutput, calls=%fused_computation.20.clone.1 | convolution fusion | flops 595582976 | bytes 28901380 | tf_op jit(solution)/shard_map/while/body/eval_jaxpr/qhd,khd->hqk/dot_general | solution.py:230
  293.8 7.1 %fusion.35 = bf16[1024,2048]{1,0:T(8,128)(2,1)S(1)} fusion(f32[1024,512]{1,0:T(8,128)} %copy.83, f32[1024,512]{1,0:T(8,128)S(1)} %copy-done.15, f32[1024,512]{1,0:T(8,128)} %copy.81, f32[1024,512]{1,0:T(8,128)} %get-tuple-element.607, f32[1024,2048]{1,0:T(8,128)} %get-tuple-element.623), kind=kLoop, calls=%fused_computation.58 | loop fusion | flops 25165824 | bytes 20971520 | tf_op jit(solution)/shard_map/convert_element_type | solution.py:273
  311.4 10.6 %scatter_custom_fusion.1 = f32[3072,512]{1,0:T(8,128)} fusion(s32[1536]{0:T(1024)} %copy-done.32, f32[1536,512]{1,0:T(8,128)} %copy.86, f32[]{:T(128)} %constant.414.clone.1), kind=kCustom, calls=%fused_computation.72 | custom fusion | bytes 6291968 | tf_op jit(solution)/shard_map/scatter | solution.py:284
  322.0 4.7 all-to-all-start.2
  338.4 179.5 %all-reduce.2 = (f32[8,32]{1,0:T(8,128)S(1)}, f32[3,512]{1,0:T(4,128)S(1)}, f32[4]{0:T(128)S(1)}) all-reduce(f32[8,32]{1,0:T(8,128)S(1)} %fusion.86, f32[3,512]{1,0:T(4,128)S(1)} %pad_maximum_fusion.1, f32[4]{0:T(128)S(1)} %pad_maximum_fusion.2), channel_id=1, replica_groups=mesh['dp'=8,'mp'=4] {'dp','mp'}, use_global_device_ids=true, to_apply=%region_25.26 | all-reduce | flops 1796 | bytes 14368 | tf_op jit(solution)/shard_map/psum | solution.py:297
  521.0 48.4 %all-reduce.6.cloned.1.call-done = (f32[512,2048]{1,0:T(8,128)}, f32[512,512]{1,0:T(8,128)}) async-done(((f32[512,2048]{1,0:T(8,128)}, f32[512,512]{1,0:T(8,128)}), (f32[512,2048]{1,0:T(8,128)}, f32[512,512]{1,0:T(8,128)})) %all-reduce.6.cloned.1.call-update) | async-done | bytes 5242896 | tf_op jit(solution)/shard_map/psum | solution.py:297
  573.0 8.7 %add_multiply_fusion = (f32[512,2048]{1,0:T(8,128)}, f32[512,2048]{1,0:T(8,128)}, f32[512,2048]{1,0:T(8,128)}) fusion(f32[512,2048]{1,0:T(8,128)S(1)} %copy-done.21, f32[512,2048]{1,0:T(8,128)} %get-tuple-element.583, f32[512,2048]{1,0:T(8,128)} %param.35, f32[512,2048]{1,0:T(8,128)} %param.34), kind=kLoop, calls=%fused_computation.69 | loop fusion | flops 12582912 | bytes 29360128 | tf_op jit(solution)/shard_map/mul | solution.py:64
  581.7 22.2 %scatter_custom_fusion.2 = f32[784,512]{1,0:T(8,128)} fusion(s32[3072]{0:T(1024)} %bitcast.230, f32[3072,512]{1,0:T(8,128)} %bitcast.34, f32[]{:T(128)} %constant.414.clone.1), kind=kCustom, calls=%fused_computation.126 | custom fusion | flops 1572864 | bytes 1606144 | tf_op jit(solution)/shard_map/scatter-add | solution.py:293
  (235 shorter events, 115.2 us)
Async XLA Ops:
  7.2 10.6 %copy-start.35 = (s32[1536,1]{0,1:T(1,128)S(1)}, s32[1536,1]{0,1:T(1,128)}, u32[]{:S(2)}) copy-start(s32[1536,1]{0,1:T(1,128)} %param.45) | copy-start | bytes 18436
  7.2 32.8 %copy-start.1 = (f32[784,512]{1,0:T(8,128)S(1)}, f32[784,512]{1,0:T(8,128)}, u32[]{:S(2)}) copy-start(f32[784,512]{1,0:T(8,128)} %param.28) | copy-start | bytes 4816900
  17.9 38.2 %copy-start.32 = (s32[1536]{0:T(1024)}, s32[1536]{0:T(1024)S(1)}, u32[]{:S(2)}) copy-start(s32[1536]{0:T(1024)S(1)} %fusion.91) | copy-start | bytes 18436
  40.0 12.5 %copy-start.30 = (s32[3072,1]{0,1:T(1,128)}, s32[3072,1]{0,1:T(1,128)S(1)}, u32[]{:S(2)}) copy-start(s32[3072,1]{0,1:T(1,128)S(1)} %compare_select_fusion) | copy-start | bytes 36868
  52.5 74.6 %all-to-all-start.1 = ((bf16[32,96,512]{2,1,0:T(8,128)(2,1)}), bf16[32,96,512]{2,1,0:T(8,128)(2,1)S(1)}, u32[]{:S(2)}, u32[]{:S(2)}) async-start(bf16[32,96,512]{2,1,0:T(8,128)(2,1)} %bitcast.216), calls=%async_computation.1 | async-start | bytes 6291456 | tf_op jit(solution)/shard_map/all_to_all | solution.py:108
  57.2 78.6 %copy-start.43 = (f32[1,512]{1,0:T(1,128)}, f32[1,512]{1,0:T(1,128)S(1)}, u32[]{:S(2)}) copy-start(f32[1,512]{1,0:T(1,128)S(1)} %get-tuple-element.612) | copy-start | bytes 6148
  134.3 11.5 %copy-start.4 = (bf16[1024,512]{0,1:T(8,128)(2,1)}, bf16[1024,512]{0,1:T(8,128)(2,1)S(1)}, u32[]{:S(2)}) copy-start(bf16[1024,512]{0,1:T(8,128)(2,1)S(1)} %copy.92) | copy-start | bytes 3145732
  135.8 9.9 %copy-start.37 = (f32[1024]{0:T(1024)}, f32[1024]{0:T(1024)S(1)}, u32[]{:S(2)}) copy-start(f32[1024]{0:T(1024)S(1)} %get-tuple-element.616) | copy-start | bytes 12292
  213.9 8.1 %copy-start.28 = (bf16[1,1024,8,64]{1,3,2,0:T(8,128)(2,1)S(1)}, bf16[1,1024,8,64]{1,3,2,0:T(8,128)(2,1)}, u32[]{:S(2)}) copy-start(bf16[1,1024,8,64]{1,3,2,0:T(8,128)(2,1)} %get-tuple-element.849) | copy-start | bytes 3145732 | tf_op jit(solution)/shard_map/while
  250.8 8.1 %copy-start.28 = (bf16[1,1024,8,64]{1,3,2,0:T(8,128)(2,1)S(1)}, bf16[1,1024,8,64]{1,3,2,0:T(8,128)(2,1)}, u32[]{:S(2)}) copy-start(bf16[1,1024,8,64]{1,3,2,0:T(8,128)(2,1)} %get-tuple-element.849) | copy-start | bytes 3145732 | tf_op jit(solution)/shard_map/while
  258.9 8.3 %copy-start.27 = (bf16[1,1024,8,64]{1,3,2,0:T(8,128)(2,1)S(1)}, bf16[1,1024,8,64]{1,3,2,0:T(8,128)(2,1)}, u32[]{:S(2)}) copy-start(bf16[1,1024,8,64]{1,3,2,0:T(8,128)(2,1)} %get-tuple-element.850) | copy-start | bytes 3145732 | tf_op jit(solution)/shard_map/while
  322.0 259.7 %all-to-all-start.2 = ((f32[32,96,512]{2,1,0:T(8,128)}), f32[32,96,512]{2,1,0:T(8,128)}, u32[]{:S(2)}, u32[]{:S(2)}) async-start(f32[32,96,512]{2,1,0:T(8,128)} %bitcast.215), calls=%async_computation.2 | async-start | bytes 12582912 | tf_op jit(solution)/shard_map/all_to_all | solution.py:286
  326.6 242.8 %all-reduce.6.cloned.1.call-start = ((), (), s32[]{:S(2)}) async-start(), calls=%async_computation.3 | async-start | bytes 10485760 | tf_op jit(solution)/shard_map/psum | solution.py:297
  334.3 185.5 %copy-start.48 = (f32[8,32]{1,0:T(8,128)S(1)}, f32[8,32]{1,0:T(8,128)}, u32[]{:S(2)}) copy-start(f32[8,32]{1,0:T(8,128)} %param.32) | copy-start | bytes 3076
  334.3 185.5 %copy-start.49 = (f32[8,32]{1,0:T(8,128)S(1)}, f32[8,32]{1,0:T(8,128)}, u32[]{:S(2)}) copy-start(f32[8,32]{1,0:T(8,128)} %param.39) | copy-start | bytes 3076
  334.3 185.4 %copy-start.50 = (f32[8,32]{1,0:T(8,128)S(1)}, f32[8,32]{1,0:T(8,128)}, u32[]{:S(2)}) copy-start(f32[8,32]{1,0:T(8,128)} %param.38) | copy-start | bytes 3076
  334.3 186.1 %copy-start.34 = (f32[3,512]{1,0:T(4,128)S(1)}, f32[3,512]{1,0:T(4,128)}, u32[]{:S(2)}) copy-start(f32[3,512]{1,0:T(4,128)} %param.33) | copy-start | bytes 18436
  334.3 186.0 %copy-start.41 = (f32[3,512]{1,0:T(4,128)S(1)}, f32[3,512]{1,0:T(4,128)}, u32[]{:S(2)}) copy-start(f32[3,512]{1,0:T(4,128)} %param.41) | copy-start | bytes 18436
  334.3 186.0 %copy-start.42 = (f32[3,512]{1,0:T(4,128)S(1)}, f32[3,512]{1,0:T(4,128)}, u32[]{:S(2)}) copy-start(f32[3,512]{1,0:T(4,128)} %param.40) | copy-start | bytes 18436
  334.4 235.1 %copy-start.13 = (f32[512,512]{1,0:T(8,128)S(1)}, f32[512,512]{1,0:T(8,128)}, u32[]{:S(2)}) copy-start(f32[512,512]{1,0:T(8,128)} %param.31) | copy-start | bytes 3145732
  334.4 235.1 %copy-start.25 = (f32[512,512]{1,0:T(8,128)S(1)}, f32[512,512]{1,0:T(8,128)}, u32[]{:S(2)}) copy-start(f32[512,512]{1,0:T(8,128)} %param.37) | copy-start | bytes 3145732
  334.4 235.1 %copy-start.26 = (f32[512,512]{1,0:T(8,128)S(1)}, f32[512,512]{1,0:T(8,128)}, u32[]{:S(2)}) copy-start(f32[512,512]{1,0:T(8,128)} %param.36) | copy-start | bytes 3145732
  581.7 24.0 %copy-start.52 = (f32[784]{0:T(1024)S(1)}, f32[784]{0:T(1024)}, u32[]{:S(2)}) copy-start(f32[784]{0:T(1024)} %param.29) | copy-start | bytes 9412
  581.7 24.6 %copy-start.2 = (f32[784,512]{1,0:T(8,128)S(1)}, f32[784,512]{1,0:T(8,128)}, u32[]{:S(2)}) copy-start(f32[784,512]{1,0:T(8,128)} %param.28) | copy-start | bytes 4816900
  (42 other events, 148.0 us)
Sparse Core Ops, SparseCore 0:
  334.5 234.8 all-reduce.5
where the time goes:
time: 621 us; the launch traced here: 615 us
  blocking collectives  194 us (31%)
  waiting for transfers between devices  118 us (19%)
  matrix products  105 us (17%)
  other arithmetic  85.7 us (14%)
  local copies, waits for them, and re-layouts  84.5 us (14%)
  between operations  15.8 us (3%)
  starting transfers between devices  7.66 us (1%)
    psum x1, blocking collectives, per_device(): lax.psum((grad_uvqk, grad_out, grad_timebias, grad_gains), ('dp', 'mp'))  180 us
    all_to_all x1, waiting for transfers between devices, per_device(): lax.all_to_all(served.reshape(devices, capacity, model_width), ('dp', 'mp...  69.9 us
    psum x1, waiting for transfers between devices, per_device(): lax.psum((grad_uvqk, grad_out, grad_timebias, grad_gains), ('dp', 'mp'))  48.4 us
    dot_general x2, matrix products, backward_block(): jnp.einsum('qhd,khd->hqk', out_grad_blk, value_seq, preferred_element_typ...  22.9 us
    scatter-add x1, other arithmetic, per_device(): jnp.zeros_like(table).at[recv_ids].add(recv_grads.reshape(-1, model_width))  22.2 us
    dot_general x2, matrix products, forward_block(): jnp.einsum('hqk,khd->qhd', attn_low, value_seq, preferred_element_type=jn...  20.9 us
    dot_general x2, matrix products, backward_block(): jnp.einsum('hqk,qhd->khd', attn_low, out_grad_blk, preferred_element_type...  15.6 us
    all_to_all x1, blocking collectives, per_device(): lax.all_to_all(send_ids.reshape(devices, capacity), ('dp', 'mp'), split_a...  14.3 us
  transfers between devices with their start and end apart: 3, of which 2 were waited for; matrix products, arithmetic and copies ran while one was open for 4% of the time, Pallas kernels for 0%

commit v1 on v0

v1 whole, which is shorter than its diff:
```python
import functools
import math

import jax
import jax.numpy as jnp
from jax import lax
from jax.experimental import pallas as pl
from jax.experimental.pallas import tpu as pltpu
from jax.sharding import Mesh
from jax.sharding import PartitionSpec as P

D = 512
H = 8
NB = 32

EPSILON = 1e-06
ROW_RATE = 0.2
LEARN_RATE = 0.01
BETA_ONE = 0.9
BETA_TWO = 0.95
ADAM_EPSILON = 1e-08
WEIGHT_DECAY = 0.1

ALL = ("zh", "b", "y", "c")
HALF = ("b", "y", "c")
CHIPS = ("zh", "b", "y")
SWAP = [(0, 1), (1, 0)]
BLK = 256
F32 = jnp.float32
BF16 = jnp.bfloat16
HIGH = lax.Precision.HIGHEST
PARAMS = pltpu.CompilerParams(vmem_limit_bytes=60 * 1024 * 1024)
NT = (((1,), (1,)), ((), ()))
TN = (((0,), (0,)), ((), ()))


def dot(left, right):
    return jnp.dot(left, right, preferred_element_type=F32)


def dot_nt(left, right):
    return lax.dot_general(left, right, NT, preferred_element_type=F32)


def dot_tn(left, right):
    return lax.dot_general(left, right, TN, preferred_element_type=F32)


def iota(shape, dim):
    return lax.broadcasted_iota(jnp.int32, shape, dim)


def one_hot(mask):
    return jnp.where(mask, 1.0, 0.0).astype(BF16)


def at(block):
    return pl.ds(pl.multiple_of(block * BLK, BLK), BLK)


def root_mean(mean_square):
    return jnp.sqrt(mean_square + EPSILON)


def mean_last(values):
    return jnp.mean(values, -1, keepdims=True)


def sds(*shape, dtype=BF16):
    return jax.ShapeDtypeStruct(shape, dtype)


def adam_update(weight, gradient, first, second, decay):
    first_new = BETA_ONE * first + (1.0 - BETA_ONE) * gradient
    second_new = BETA_TWO * second + (1.0 - BETA_TWO) * gradient * gradient
    update = -LEARN_RATE * (first_new / (jnp.sqrt(second_new) + ADAM_EPSILON) + decay * weight)
    return (update, first_new, second_new)


def slots_kernel(devices, capacity, half_ref, ownc_ref, ownr_ref, rows_ref, slotc_ref, slotr_ref, ids_ref):
    requests = ownc_ref.shape[0]
    peers = devices // 2
    shift = half_ref[0] * peers
    relc = ownc_ref[...] - shift
    relc = jnp.where(relc < 0, relc + devices, relc)
    relr = ownr_ref[...] - shift
    relr = jnp.where(relr < 0, relr + devices, relr)
    lower = one_hot(iota((BLK, BLK), 0) > iota((BLK, BLK), 1))
    upper = one_hot(iota((BLK, BLK), 0) < iota((BLK, BLK), 1))
    run_c = jnp.zeros((1, devices), F32)
    run_r = jnp.zeros((devices, 1), F32)
    acc_hi = jnp.zeros((peers, 2 * capacity), F32)
    acc_lo = jnp.zeros((peers, 2 * capacity), F32)
    for block in range(requests // BLK):
        part = slice(block * BLK, (block + 1) * BLK)
        rc = relc[part]
        hits = jnp.where(rc == iota((BLK, devices), 1), 1.0, 0.0)
        before = dot(lower, hits.astype(BF16)) + run_c
        rank = jnp.sum(before * hits, 1, keepdims=True).astype(jnp.int32)
        run_c = run_c + jnp.sum(hits, 0, keepdims=True)
        slotc_ref[part, :] = rc * capacity + rank
        rr = relr[:, part]
        hits_r = jnp.where(rr == iota((devices, BLK), 0), 1.0, 0.0)
        before_r = dot(hits_r.astype(BF16), upper) + run_r
        rank_r = jnp.sum(before_r * hits_r, 0, keepdims=True).astype(jnp.int32)
        run_r = run_r + jnp.sum(hits_r, 1, keepdims=True)
        slotr_ref[:, part] = rr * capacity + rank_r
        far = rc >= peers
        where = one_hot(iota((BLK, 2 * capacity), 1) == rank + jnp.where(far, capacity, 0))
        near_peer = jnp.where(rr >= peers, rr - peers, rr)
        mine = near_peer == iota((peers, BLK), 0)
        rows = rows_ref[:, part]
        hi = rows // 32
        lo = rows - hi * 32
        acc_hi = acc_hi + dot(jnp.where(mine, hi.astype(F32), 0.0).astype(BF16), where)
        acc_lo = acc_lo + dot(jnp.where(mine, lo.astype(F32), 0.0).astype(BF16), where)
    ids_ref[...] = (acc_hi * 32.0 + acc_lo).astype(jnp.int32)


def request_slots(half, owners, item_rows, devices, capacity):
    requests = item_rows.shape[0]
    vmem = pl.BlockSpec(memory_space=pltpu.VMEM)
    return pl.pallas_call(
        functools.partial(slots_kernel, devices, capacity),
        out_shape=(
            sds(requests, 1, dtype=jnp.int32),
            sds(1, requests, dtype=jnp.int32),
            sds(devices // 2, 2 * capacity, dtype=jnp.int32),
        ),
        in_specs=[pl.BlockSpec(memory_space=pltpu.SMEM)] + [vmem] * 3,
        out_specs=[vmem] * 3,
        compiler_params=PARAMS,
        name="request_slots",
    )(half, owners.reshape(requests, 1), owners.reshape(1, requests), item_rows.reshape(1, requests))


def serve_kernel(ids_ref, table_ref, out_ref):
    rows = table_ref.shape[0]
    for block in range(out_ref.shape[0] // BLK):
        part = slice(block * BLK, (block + 1) * BLK)
        hits = one_hot(ids_ref[part, :] == iota((BLK, rows), 1))
        out_ref[part, :] = dot(hits, table_ref[...]).astype(BF16)


def serve(ids, table):
    return pl.pallas_call(
        serve_kernel,
        out_shape=sds(ids.shape[0], table.shape[1]),
        compiler_params=PARAMS,
        name="serve",
    )(ids, table)


def place_kernel(slotc_ref, got_ref, out_ref):
    slots = got_ref.shape[0]
    for block in range(out_ref.shape[0] // BLK):
        part = slice(block * BLK, (block + 1) * BLK)
        hits = one_hot(slotc_ref[part, :] == iota((BLK, slots), 1))
        out_ref[part, :] = dot(hits, got_ref[...]).astype(BF16)


def place(slotc, got):
    return pl.pallas_call(
        place_kernel,
        out_shape=sds(slotc.shape[0], got.shape[1]),
        compiler_params=PARAMS,
        name="place",
    )(slotc, got)


def forward_kernel(
    total_tokens,
    len_ref,
    own_ref,
    far_ref,
    slotc_ref,
    w_ref,
    wo_ref,
    gains_ref,
    tb_ref,
    bucket_ref,
    x_ref,
    n1_ref,
    v_ref,
    q_ref,
    k_ref,
    sp_ref,
    bias_ref,
    dpu_ref,
    do_ref,
    gm_ref,
    dneg_ref,
    dout_ref,
    stats_ref,
    dgain_ref,
    xs,
    neg,
    gate,
    gate_d,
    att,
    dnacc,
    dwo,
    carry,
):
    seq_len = n1_ref.shape[0]
    negs = dneg_ref.shape[0]
    slots = far_ref.shape[0]
    blocks = seq_len // BLK
    length = len_ref[0]
    inv_len = 1.0 / (jnp.zeros((1, 1), jnp.int32) + length).astype(F32)

    def fetch(block):
        hits = one_hot(slotc_ref[at(block), :] - slots == iota((BLK, slots), 1))
        return own_ref[at(block), :].astype(F32) + dot(hits, far_ref[...])

    buckets = jnp.where(bucket_ref[...] == iota((NB, seq_len), 0), 1.0, 0.0)
    bias_ref[...] = 0.5 * jnp.dot(tb_ref[...], buckets, precision=HIGH, preferred_element_type=F32)
    xs[pl.ds(seq_len, 8), :] = jnp.zeros((8, D), F32)

    def project(block, sum_x):
        x = fetch(block)
        xs[at(block), :] = x
        x_ref[at(block), :] = x.astype(BF16)
        mean_sq = mean_last(x * x)
        pos = block * BLK + iota((BLK, 1), 0)
        live = pos < length
        n1 = (x * lax.rsqrt(mean_sq + EPSILON) * gains_ref[0:1, :]).astype(BF16)
        n1_ref[at(block), :] = n1
        for part in range(4):
            half_pre = 0.5 * dot(n1, w_ref[:, part * D : (part + 1) * D])
            th = jnp.tanh(half_pre)
            act = half_pre + half_pre * th
            deriv = 0.5 * (1.0 + th) * (1.0 + half_pre * (1.0 - th))
            if part == 0:
                gate[at(block), :] = act
                gate_d[at(block), :] = deriv
            else:
                sp_ref[at(block), (part - 1) * D : part * D] = deriv.astype(BF16)
                low = act.astype(BF16)
                if part == 1:
                    v_ref[at(block), :] = jnp.where(live, low.astype(F32), 0.0).astype(BF16)
                elif part == 2:
                    q_ref[at(block), :] = (low.astype(F32) * (0.5 * (D // H) ** -0.5)).astype(BF16)
                else:
                    k_ref[at(block), :] = low
        return sum_x + jnp.sum(jnp.where(live, root_mean(mean_sq), 0.0), keepdims=True)

    sum_x = lax.fori_loop(0, blocks, project, jnp.zeros((1, 1), F32))
    for block in range(negs // BLK):
        neg[block * BLK : (block + 1) * BLK, :] = fetch(blocks + block).astype(BF16)

    lower = iota((BLK, BLK), 0) >= iota((BLK, BLK), 1)

    def attend(pair, _):
        lanes = pl.ds(pl.multiple_of(pair * 128, 128), 128)
        lane = iota((1, 128), 1)
        sides = [jnp.where(lane < 64, 1.0, 0.0).astype(BF16), jnp.where(lane < 64, 0.0, 1.0).astype(BF16)]
        keys = [k_ref[:, lanes] * side for side in sides]
        vals = [v_ref[:, lanes] * side for side in sides]
        bias = [bias_ref[pl.ds(2 * pair + hh, 1), :] for hh in range(2)]
        for qb in range(blocks):
            query = q_ref[qb * BLK : (qb + 1) * BLK, lanes]
            total = jnp.zeros((BLK, 128), F32)
            for hh in range(2):
                for kb in range(qb + 1):
                    span = slice(kb * BLK, (kb + 1) * BLK)
                    half_s = dot_nt(query, keys[hh][span]) + bias[hh][:, span]
                    score = half_s + half_s * jnp.tanh(half_s)
                    if kb == qb:
                        score = jnp.where(lower, score, 0.0)
                    total = total + dot(score.astype(BF16), vals[hh][span])
            att[qb * BLK : (qb + 1) * BLK, lanes] = total * inv_len
        return 0

    lax.fori_loop(0, H // 2, attend, 0)

    scale = 2.0 / math.sqrt(D)
    dnacc[...] = jnp.zeros_like(dnacc)
    dwo[...] = jnp.zeros_like(dwo)
    carry[...] = jnp.zeros_like(carry)
    first_row = iota((BLK, 1), 0) == 0
    last_row = iota((BLK, 1), 0) == BLK - 1

    def head(block, sums):
        sum_loss, sum_o, sum_b, dg1, dg2 = sums
        rows = at(block)
        x = xs[rows, :]
        pos = block * BLK + iota((BLK, 1), 0)
        live = pos < length
        valid = pos < length - 1
        o = att[rows, :]
        u = gate[rows, :]
        ms_o = mean_last(o * o)
        r2 = lax.rsqrt(ms_o + EPSILON)
        n2 = o * r2 * gains_ref[1:2, :]
        g = (n2 * u).astype(BF16)
        branch = dot(g, wo_ref[...])
        ms_b = mean_last(branch * branch)
        mixed = x + branch
        r3 = lax.rsqrt(mean_last(mixed * mixed) + EPSILON)
        final = (mixed * r3 * gains_ref[2:3, :]).astype(BF16)
        final_f = final.astype(F32)
        after = xs[pl.ds(pl.multiple_of(block * BLK + BLK, 8), 8), :][0:1, :]
        nxt = jnp.where(last_row, after, pltpu.roll(x, BLK - 1, 0))
        target = jnp.sum(final_f * nxt, -1, keepdims=True) * scale
        logits = dot_nt(final, neg[...]) * scale
        top = jnp.maximum(jnp.max(logits, -1, keepdims=True), target)
        lse = top + jnp.log(jnp.exp(target - top) + jnp.sum(jnp.exp(logits - top), -1, keepdims=True))
        weight = jnp.where(valid, 1.0 / total_tokens, 0.0)
        dt = weight * (jnp.exp(target - lse) - 1.0) * scale
        dz = (weight * jnp.exp(logits - lse)).astype(BF16)
        dfin = dt * nxt + scale * dot(dz, neg[...])
        dnacc[...] += dot_tn(dz, final)
        dnext = dt * final_f
        shifted = jnp.where(first_row, carry[0:1, :], pltpu.roll(dnext, 1, 0))
        carry[...] = jnp.broadcast_to(dnext[BLK - 1 : BLK, :], carry.shape)
        dg2 = dg2 + jnp.sum(dfin * mixed * r3, 0, keepdims=True)
        scaled = dfin * gains_ref[2:3, :]
        dy = r3 * scaled - mixed * (r3 * r3 * r3) * mean_last(scaled * mixed)
        gm_ref[rows, :] = dy + shifted
        db = dy.astype(BF16)
        dwo[...] += dot_tn(g, db)
        dg = dot_nt(db, wo_ref[...])
        dpu_ref[rows, :] = (dg * n2 * gate_d[rows, :]).astype(BF16)
        dn2 = dg * u
        dg1 = dg1 + jnp.sum(dn2 * o * r2, 0, keepdims=True)
        scaled2 = dn2 * gains_ref[1:2, :]
        do = r2 * scaled2 - o * (r2 * r2 * r2) * mean_last(scaled2 * o)
        do_ref[rows, :] = (do * inv_len).astype(BF16)
        return (
            sum_loss + jnp.sum(jnp.where(valid, lse - target, 0.0), keepdims=True),
            sum_o + jnp.sum(jnp.where(live, root_mean(ms_o), 0.0), keepdims=True),
            sum_b + jnp.sum(jnp.where(live, root_mean(ms_b), 0.0), keepdims=True),
            dg1,
            dg2,
        )

    zero = jnp.zeros((1, 1), F32)
    zrow = jnp.zeros((1, D), F32)
    sum_loss, sum_o, sum_b, dg1, dg2 = lax.fori_loop(0, blocks, head, (zero, zero, zero, zrow, zrow))
    dneg_ref[...] = (dnacc[...] * scale).astype(BF16)
    dout_ref[...] = dwo[...].astype(BF16)
    which = iota((8, 128), 0)
    stats = jnp.where(which == 0, sum_loss, 0.0) + jnp.where(which == 1, sum_x, 0.0)
    stats_ref[...] = stats + jnp.where(which == 2, sum_o, 0.0) + jnp.where(which == 3, sum_b, 0.0)
    row = iota((8, D), 0)
    dgain_ref[...] = jnp.where(row == 1, dg1, 0.0) + jnp.where(row == 2, dg2, 0.0)


def forward(length, own, far, slotc, w, wo, gains, time_bias, buckets, total_tokens):
    seq_len = buckets.shape[1]
    negs = slotc.shape[0] - seq_len
    vmem = pl.BlockSpec(memory_space=pltpu.VMEM)
    outs = (
        sds(seq_len, D),
        sds(seq_len, D),
        sds(seq_len, D),
        sds(seq_len, D),
        sds(seq_len, D),
        sds(seq_len, 3 * D),
        sds(H, seq_len, dtype=F32),
        sds(seq_len, D),
        sds(seq_len, D),
        sds(seq_len, D, dtype=F32),
        sds(negs, D),
        sds(D, D),
        sds(8, 128, dtype=F32),
        sds(8, D, dtype=F32),
    )
    return pl.pallas_call(
        functools.partial(forward_kernel, total_tokens),
        out_shape=outs,
        in_specs=[pl.BlockSpec(memory_space=pltpu.SMEM)] + [vmem] * 8,
        out_specs=[vmem] * len(outs),
        scratch_shapes=[
            pltpu.VMEM((seq_len + 8, D), F32),
            pltpu.VMEM((negs, D), BF16),
            pltpu.VMEM((seq_len, D), F32),
            pltpu.VMEM((seq_len, D), F32),
            pltpu.VMEM((seq_len, D), F32),
            pltpu.VMEM((negs, D), F32),
            pltpu.VMEM((D, D), F32),
            pltpu.VMEM((8, D), F32),
        ],
        compiler_params=PARAMS,
        name="forward",
    )(length, own, far, slotc, w, wo, gains, time_bias, buckets)


def backward_kernel(
    len_ref,
    x_ref,
    v_ref,
    q_ref,
    k_ref,
    sp_ref,
    bias_ref,
    dpu_ref,
    do_ref,
    gm_ref,
    dneg_ref,
    slotr_ref,
    w_ref,
    gains_ref,
    bucket_ref,
    far_ref,
    own_ref,
    dp_ref,
    dbias_ref,
    dgain_ref,
    qt,
    dt,
    kt,
    vt,
    dkb,
    rows_ref,
):
    seq_len = x_ref.shape[0]
    requests = slotr_ref.shape[1]
    slots = far_ref.shape[0]
    blocks = seq_len // BLK
    length = len_ref[0]
    lower = iota((BLK, BLK), 0) >= iota((BLK, BLK), 1)
    live = iota((seq_len, 1), 0) < length
    ones = jnp.where(iota((16, seq_len), 0) == 0, 1.0, 0.0).astype(BF16)

    def pair_step(pair, _):
        lanes = pl.ds(pl.multiple_of(pair * 128, 128), 128)
        lane = iota((1, 128), 1)
        sides = [jnp.where(lane < 64, 1.0, 0.0).astype(BF16), jnp.where(lane < 64, 0.0, 1.0).astype(BF16)]
        keys = [k_ref[:, lanes] * side for side in sides]
        vals = [v_ref[:, lanes] * side for side in sides]
        bias = [bias_ref[pl.ds(2 * pair + hh, 1), :] for hh in range(2)]
        queries = q_ref[:, lanes]
        grads = do_ref[:, lanes]
        qtr = queries.astype(F32).T.astype(BF16)
        dtr = grads.astype(F32).T.astype(BF16)
        for hh in range(2):
            qt[hh, 0:64, :] = qtr[hh * 64 : hh * 64 + 64, :]
            qt[hh, 64:80, :] = ones
            dt[hh] = dtr[hh * 64 : hh * 64 + 64, :]
        kt[...] = jnp.zeros_like(kt)
        vt[...] = jnp.zeros_like(vt)
        for qb in range(blocks):
            qs = slice(qb * BLK, (qb + 1) * BLK)
            dq = jnp.zeros((BLK, 128), F32)
            for hh in range(2):
                for kb in range(qb + 1):
                    span = slice(kb * BLK, (kb + 1) * BLK)
                    half_s = dot_nt(queries[qs], keys[hh][span]) + bias[hh][:, span]
                    th = jnp.tanh(half_s)
                    score = half_s + half_s * th
                    deriv = (0.5 + 0.5 * th) * (1.0 + half_s - half_s * th)
                    ds = dot_nt(grads[qs], vals[hh][span]) * deriv
                    if kb == qb:
                        score = jnp.where(lower, score, 0.0)
                        ds = jnp.where(lower, ds, 0.0)
                    ds = ds.astype(BF16)
                    dq = dq + dot(ds, keys[hh][span])
                    kt[hh, :, span] += dot(qt[hh, :, qs], ds)
                    vt[hh, :, span] += dot(dt[hh, :, qs], score.astype(BF16))
            head_scale = (D // H) ** -0.5
            dql = pl.ds(pl.multiple_of(D + pair * 128, 128), 128)
            dp_ref[qs, dql] = (dq * head_scale * sp_ref[qs, dql].astype(F32)).astype(BF16)
        dkl = pl.ds(pl.multiple_of(2 * D + pair * 128, 128), 128)
        dk = jnp.concatenate([kt[0, 0:64, :], kt[1, 0:64, :]], 0).T
        dv = jnp.concatenate([vt[0], vt[1]], 0).T
        dp_ref[:, dkl] = (dk * 2.0 * sp_ref[:, dkl].astype(F32)).astype(BF16)
        dp_ref[:, lanes] = (jnp.where(live, dv, 0.0) * sp_ref[:, lanes].astype(F32)).astype(BF16)
        for hh in range(2):
            dkb[pl.ds(2 * pair + hh, 1), :] = kt[hh, 64:65, :]
        return 0

    lax.fori_loop(0, H // 2, pair_step, 0)
    buckets = jnp.where(bucket_ref[...] == iota((NB, seq_len), 0), 1.0, 0.0)
    dbias_ref[...] = lax.dot_general(dkb[...], buckets, NT, precision=HIGH, preferred_element_type=F32)

    def tail(block, dg0):
        rows = at(block)
        x = x_ref[rows, :].astype(F32)
        r1 = lax.rsqrt(mean_last(x * x) + EPSILON)
        dn1 = dot_nt(dpu_ref[rows, :], w_ref[:, 0:D]) + dot_nt(dp_ref[rows, :], w_ref[:, D : 4 * D])
        dg0 = dg0 + jnp.sum(dn1 * x * r1, 0, keepdims=True)
        scaled = dn1 * gains_ref[0:1, :]
        dx = r1 * scaled - x * (r1 * r1 * r1) * mean_last(scaled * x) + gm_ref[rows, :]
        rows_ref[rows, :] = dx.astype(BF16)
        return dg0

    dg0 = lax.fori_loop(0, blocks, tail, jnp.zeros((1, D), F32))
    rows_ref[seq_len:requests, :] = dneg_ref[...]
    dgain_ref[...] = jnp.where(iota((8, D), 0) == 0, dg0, 0.0)

    def put(block, _):
        slot = block * BLK + iota((BLK, 1), 0)
        hits = one_hot(slotr_ref[...] - slots == slot)
        far_ref[at(block), :] = dot(hits, rows_ref[...]).astype(BF16)
        hits = one_hot(slotr_ref[...] == slot)
        own_ref[at(block), :] = dot(hits, rows_ref[...]).astype(BF16)
        return 0

    lax.fori_loop(0, slots // BLK, put, 0)


def backward(length, x, v, q, k, sp, bias, dpu, do, gm, dneg, slotr, w, gains, buckets, slots):
    seq_len = x.shape[0]
    vmem = pl.BlockSpec(memory_space=pltpu.VMEM)
    outs = (
        sds(slots, D),
        sds(slots, D),
        sds(seq_len, 3 * D),
        sds(H, NB, dtype=F32),
        sds(8, D, dtype=F32),
    )
    return pl.pallas_call(
        backward_kernel,
        out_shape=outs,
        in_specs=[pl.BlockSpec(memory_space=pltpu.SMEM)] + [vmem] * 14,
        out_specs=[vmem] * len(outs),
        scratch_shapes=[
            pltpu.VMEM((2, 80, seq_len), BF16),
            pltpu.VMEM((2, 64, seq_len), BF16),
            pltpu.VMEM((2, 80, seq_len), F32),
            pltpu.VMEM((2, 64, seq_len), F32),
            pltpu.VMEM((H, seq_len), F32),
            pltpu.VMEM((slotr.shape[1], D), BF16),
        ],
        compiler_params=PARAMS,
        name="backward",
    )(length, x, v, q, k, sp, bias, dpu, do, gm, dneg, slotr, w, gains, buckets)


def weight_kernel(n1_ref, dp_ref, out_ref):
    for part in range(dp_ref.shape[1] // D):
        columns = slice(part * D, (part + 1) * D)
        out_ref[columns, :] = dot_tn(n1_ref[...], dp_ref[:, columns]).astype(BF16)


def weight_grad(n1, dp):
    return pl.pallas_call(
        weight_kernel,
        out_shape=sds(dp.shape[1], D),
        compiler_params=PARAMS,
        name="weight_grad",
    )(n1, dp)


def gather_kernel(ids_ref, got_ref, out_ref):
    rows, slots = (out_ref.shape[0], got_ref.shape[0])
    hits = one_hot(ids_ref[...] == iota((rows, slots), 0))
    out_ref[...] = dot(hits, got_ref[...]).astype(BF16)


def row_sums(ids, got, rows):
    return pl.pallas_call(
        gather_kernel,
        out_shape=sds(rows, got.shape[1]),
        compiler_params=PARAMS,
        name="row_sums",
    )(ids, got)


def update_kernel(ids_ref, got_ref, far_ref, table_ref, acc_ref, table_out, acc_out):
    rows, slots = (table_ref.shape[0], got_ref.shape[0])
    hits = one_hot(ids_ref[...] == iota((rows, slots), 0))
    sums = dot(hits, got_ref[...]) + far_ref[...].astype(F32)
    acc = acc_ref[...] + mean_last(sums * sums)
    acc_out[...] = acc
    table_out[...] = table_ref[...] - ROW_RATE * sums * lax.rsqrt(acc)


def update_rows(ids, got, far, table, row_acc):
    rows = table.shape[0]
    new_table, new_acc = pl.pallas_call(
        update_kernel,
        out_shape=(sds(*table.shape, dtype=F32), sds(rows, 1, dtype=F32)),
        compiler_params=PARAMS,
        name="update_rows",
    )(ids, got, far, table, row_acc.reshape(rows, 1))
    return new_table, new_acc.reshape(rows)


def sum_dense(grad):
    rows, width = grad.shape
    core = lax.axis_index("c")
    half = rows // 2
    chips = lax.axis_size(CHIPS)
    keep = lax.dynamic_slice_in_dim(grad, core * half, half, 0)
    give = lax.dynamic_slice_in_dim(grad, (1 - core) * half, half, 0)
    pair = (keep.astype(F32) + lax.ppermute(give, "c", SWAP).astype(F32)).astype(BF16)
    parts = lax.all_to_all(pair.reshape(chips, half // chips, width), CHIPS, 0, 0, tiled=True)
    mine = jnp.sum(parts.astype(F32), 0).astype(BF16)
    spread = lax.all_to_all(jnp.broadcast_to(mine[None], parts.shape), CHIPS, 0, 0, tiled=True)
    whole = spread.reshape(half, width)
    other = lax.ppermute(whole, "c", SWAP)
    return jnp.where(core == 0, jnp.concatenate([whole, other], 0), jnp.concatenate([other, whole], 0))


def per_device(
    table,
    row_acc,
    uvqk_weight,
    out_weight,
    time_bias,
    gains,
    uvqk_m,
    uvqk_v,
    out_m,
    out_v,
    bias_m,
    bias_v,
    gain_m,
    gain_v,
    lengths,
    time_buckets,
    item_rows,
    row_owner,
):
    devices = lax.axis_size(ALL)
    peers = devices // 2
    requests = item_rows.shape[0]
    capacity = max(2, 2 * requests // devices)
    rows = table.shape[0]
    slots = peers * capacity
    total_tokens = float(time_buckets.size * devices)
    half = lax.axis_index("zh").reshape(1)

    table_low = table.astype(BF16)
    table_far = lax.ppermute(table_low, "zh", SWAP)
    slotc, slotr, ids = request_slots(half, row_owner, item_rows, devices, capacity)
    ids = lax.all_to_all(ids, HALF, 0, 0, tiled=True)
    ids_own = ids[:, :capacity]
    ids_far = ids[:, capacity:]

    def exchange(values):
        return lax.all_to_all(
            values.reshape(peers, capacity, D), HALF, 0, 0, tiled=True
        ).reshape(slots, D)

    got_own = exchange(serve(ids_own.reshape(slots, 1), table_low))
    got_far = exchange(serve(ids_far.reshape(slots, 1), table_far))
    own = place(slotc, got_own)

    w_low = uvqk_weight.astype(BF16)
    wo_low = out_weight.astype(BF16)
    (x, n1, v, q, k, sp, bias, dpu, do, gm, dneg, dout, stats, dgain) = forward(
        lengths, own, got_far, slotc, w_low, wo_low, gains, time_bias, time_buckets, total_tokens
    )
    early = jnp.concatenate([dout, weight_grad(n1, dpu)], 0)
    send_far, send_own, dp, dbias, dgain0 = backward(
        lengths, x, v, q, k, sp, bias, dpu, do, gm, dneg, slotr, w_low, gains, time_buckets, slots
    )
    back_far = exchange(send_far)
    sums_far = row_sums(ids_far.reshape(1, slots), back_far, rows)
    sums_far = lax.ppermute(sums_far, "zh", SWAP)
    back_own = exchange(send_own)
    new_table, new_acc = update_rows(ids_own.reshape(1, slots), back_own, sums_far, table, row_acc)

    sum_early = sum_dense(early)
    sum_late = sum_dense(weight_grad(n1, dp))
    small = jnp.concatenate(
        [
            dbias.reshape(-1),
            (dgain + dgain0)[:3].reshape(-1),
            stats[:4, 0],
            jnp.zeros((2048 - H * NB - 3 * D - 4,), F32),
        ]
    ).reshape(1, 8, 256)
    small = lax.all_to_all(jnp.broadcast_to(small, (devices, 8, 256)), ALL, 0, 0, tiled=True)
    small = jnp.sum(small, 0).reshape(-1)
    sum_bias = small[: H * NB].reshape(H, NB)
    sum_gains = small[H * NB : H * NB + 3 * D].reshape(3, D)
    sums = small[H * NB + 3 * D : H * NB + 3 * D + 4] / total_tokens
    summary = jnp.stack([sums[0], sums[1], sums[3]])
    attention_rms = sums[2:3]

    sum_out = sum_early[:D].astype(F32)
    sum_uvqk = jnp.concatenate(
        [sum_early[D:], sum_late[:D], sum_late[D : 2 * D], sum_late[2 * D :]], 1
    ).astype(F32)
    uvqk_step, uvqk_m_new, uvqk_v_new = adam_update(
        uvqk_weight, sum_uvqk, uvqk_m, uvqk_v, WEIGHT_DECAY
    )
    out_step, out_m_new, out_v_new = adam_update(out_weight, sum_out, out_m, out_v, WEIGHT_DECAY)
    bias_step, bias_m_new, bias_v_new = adam_update(time_bias, sum_bias, bias_m, bias_v, 0.0)
    gain_step, gain_m_new, gain_v_new = adam_update(gains, sum_gains, gain_m, gain_v, 0.0)
    return (
        new_table,
        new_acc,
        uvqk_step,
        uvqk_m_new,
        uvqk_v_new,
        out_step,
        out_m_new,
        out_v_new,
        bias_step,
        bias_m_new,
        bias_v_new,
        gain_step,
        gain_m_new,
        gain_v_new,
        summary,
        attention_rms,
    )


def solution(mesh):
    n_dp, n_mp = (mesh.shape["dp"], mesh.shape["mp"])
    fine = Mesh(mesh.devices.reshape(2, n_dp // 2, n_mp // 2, 2), ALL)
    split = P(ALL)
    whole = P()
    return jax.shard_map(
        per_device,
        mesh=fine,
        in_specs=(split, split) + (whole,) * 12 + (split,) * 4,
        out_specs=(split, split) + (whole,) * 14,
        check_vma=False,
    )
```

time: 621 us -> 386 us (0.62)
  blocking collectives: 194 us -> 43.8 us
  Pallas kernels: 0 us -> 110 us
  matrix products: 105 us -> 0 us
  local copies, waits for them, and re-layouts: 84.5 us -> 19.4 us
  other arithmetic: 85.7 us -> 32.1 us
  starting transfers between devices: 7.66 us -> 44.1 us
  waiting for transfers between devices: 118 us -> 133 us
  between operations: 15.8 us -> 1.64 us
    psum x1 -> x0, blocking collectives: 180 us -> none  [per_device(): lax.psum((grad_uvqk, grad_out, grad_timebias, grad_gains), ('dp', 'mp'))]
    pallas_call x0 -> x10, Pallas kernels: none -> 110 us  [the longest x1 39.9 us: backward(): pl.pallas_call(backward_kernel, out_shape=outs, in_specs=[pl.BlockSpec(me...]
    dot_general x23 -> x0, matrix products: 105 us -> none  [the longest x2 22.9 us: backward_block(): jnp.einsum('qhd,khd->hqk', out_grad_blk, value_seq, preferred_element_typ...]
    psum x1 -> x0, waiting for transfers between devices: 48.4 us -> none  [per_device(): lax.psum((grad_uvqk, grad_out, grad_timebias, grad_gains), ('dp', 'mp'))]
    ppermute x0 -> x6, waiting for transfers between devices: none -> 46.5 us  [the longest x1 31.1 us: per_device(): table_far = lax.ppermute(table_low, 'zh', SWAP)]
    all_to_all x2 -> x8, starting transfers between devices: 7.62 us -> 40.7 us  [the longest x4 20.1 us: exchange(): lax.all_to_all(values.reshape(peers, capacity, D), HALF, 0, 0, tiled=True)]
    all_to_all x1 -> x2, blocking collectives: 14.3 us -> 43.8 us  [sum_dense(): lax.all_to_all(jnp.broadcast_to(mine[None], parts.shape), CHIPS, 0, 0, ti...]
    scatter-add x3 -> x0, other arithmetic: 23.5 us -> none  [the longest x1 22.2 us: per_device(): jnp.zeros_like(table).at[recv_ids].add(recv_grads.reshape(-1, model_width))]
  transfers between devices with their start and end apart: 3 -> 14, of which waited for: 2 -> 9; matrix products, arithmetic and copies ran while one was open for 4% -> 7% of each run, Pallas kernels for 0% -> 17%
where the time goes in v1:
time: 386 us; the launch traced here: 385 us
  waiting for transfers between devices  133 us (34%)
  Pallas kernels  110 us (28%)
  starting transfers between devices  44.1 us (11%)
  blocking collectives  43.8 us (11%)
  other arithmetic  32.1 us (8%)
  local copies, waits for them, and re-layouts  19.4 us (5%)
    all_to_all x4, waiting for transfers between devices, exchange(): lax.all_to_all(values.reshape(peers, capacity, D), HALF, 0, 0, tiled=True)  50.3 us
    all_to_all x2, blocking collectives, sum_dense(): lax.all_to_all(jnp.broadcast_to(mine[None], parts.shape), CHIPS, 0, 0, ti...  43.8 us
    pallas_call x1, Pallas kernels, backward(): pl.pallas_call(backward_kernel, out_shape=outs, in_specs=[pl.BlockSpec(me...  39.9 us
    pallas_call x1, Pallas kernels, forward(): pl.pallas_call(functools.partial(forward_kernel, total_tokens), out_shape...  34.6 us
    all_to_all x2, waiting for transfers between devices, sum_dense(): lax.all_to_all(pair.reshape(chips, half // chips, width), CHIPS, 0, 0, ti...  33.3 us
    ppermute x1, waiting for transfers between devices, per_device(): table_far = lax.ppermute(table_low, 'zh', SWAP)  31.1 us
    all_to_all x4, starting transfers between devices, exchange(): lax.all_to_all(values.reshape(peers, capacity, D), HALF, 0, 0, tiled=True)  20.1 us
    ppermute x1, waiting for transfers between devices, per_device(): sums_far = lax.ppermute(sums_far, 'zh', SWAP)  15.4 us
  transfers between devices with their start and end apart: 14, of which 9 were waited for; matrix products, arithmetic and copies ran while one was open for 7% of the time, Pallas kernels for 17%

profile of v1, /device:TPU:0, one launch (start us, length us, event | category | flops | bytes accessed | tf_op | source)
XLA Modules:
  0.0 384.9 jit_solution(13206544310314743856)
XLA Ops:
  3.8 3.9 %request_slots.1 = (s32[1536,1]{1,0:T(8,128)}, s32[1,1536]{1,0:T(1,128)}, s32[16,192]{1,0:T(8,128)}) custom-call(s32[1]{0:T(128)} %bitcast.half_ref, s32[1536,1]{1,0:T(8,128)} %copy.44.ownc_ref, s32[1,1536]{1,0:T(1,128)} %bitcast.35, s32[1,1536]{1,0:T(1,128)} %reshape.122.rows_ref), custom_call_target="tpu_custom_call" | custom-call | tf_op jit(solution)/shard_map/request_slots/pallas_call | solution.py:123
  9.1 6.3 %all-to-all-start = ((s32[16,1,192]{2,1,0:T(1,128)}), s32[16,1,192]{2,1,0:T(1,128)S(1)}, u32[]{:S(2)}, u32[]{:S(2)}) async-start(s32[16,1,192]{2,1,0:T(1,128)} %copy.45), calls=%async_computation | async-start | bytes 32768 | tf_op jit(solution)/shard_map/all_to_all | solution.py:630
  22.6 4.4 %serve.2 = bf16[1536,512]{1,0:T(8,128)(2,1)} custom-call(s32[1536,1]{1,0:T(8,128)} %reshape.146.ids_ref, bf16[784,512]{1,0:T(8,128)(2,1)} %convert_element_type.37.table_ref), custom_call_target="tpu_custom_call" | custom-call | tf_op jit(solution)/shard_map/serve/pallas_call | solution.py:146
  35.0 31.1 %collective-permute-done.table_ref = bf16[784,512]{1,0:T(8,128)(2,1)S(1)} collective-permute-done((bf16[784,512]{1,0:T(8,128)(2,1)S(1)}, bf16[784,512]{1,0:T(8,128)(2,1)S(1)}, u32[]{:S(2)}, u32[]{:S(2)}) %collective-permute-start) | collective-permute-done | bytes 802848 | tf_op jit(solution)/shard_map/ppermute | solution.py:628
  67.0 4.4 %serve.3 = bf16[1536,512]{1,0:T(8,128)(2,1)} custom-call(s32[1536,1]{1,0:T(8,128)} %reshape.147.ids_ref, bf16[784,512]{1,0:T(8,128)(2,1)} %copy-done.16), custom_call_target="tpu_custom_call" | custom-call | tf_op jit(solution)/shard_map/serve/pallas_call | solution.py:146
  71.3 8.6 %all-to-all-start.2 = ((bf16[16,96,512]{2,1,0:T(8,128)(2,1)}), bf16[16,96,512]{2,1,0:T(8,128)(2,1)S(1)}, u32[]{:S(2)}, u32[]{:S(2)}) async-start(bf16[16,96,512]{2,1,0:T(8,128)(2,1)} %bitcast.22), calls=%async_computation.2 | async-start | bytes 3145728 | tf_op jit(solution)/shard_map/all_to_all | solution.py:635
  80.6 3.9 %convert_element_type.38.w_ref = bf16[512,2048]{1,0:T(8,128)(2,1)} convert(f32[512,2048]{1,0:T(8,128)} %param.20) | non-fusion elementwise | flops 1048576 | bytes 6291456 | tf_op jit(solution)/shard_map/convert_element_type | solution.py:643
  85.4 5.4 %place.1.own_ref = bf16[1536,512]{1,0:T(8,128)(2,1)} custom-call(s32[1536,1]{1,0:T(8,128)} %get-tuple-element.41.slotc_ref, bf16[1536,512]{1,0:T(8,128)(2,1)} %bitcast.25), custom_call_target="tpu_custom_call" | custom-call | tf_op jit(solution)/shard_map/place/pallas_call | solution.py:163
  90.8 11.8 %all-to-all-done.2 = bf16[16,96,512]{2,1,0:T(8,128)(2,1)S(1)} async-done(((bf16[16,96,512]{2,1,0:T(8,128)(2,1)}), bf16[16,96,512]{2,1,0:T(8,128)(2,1)S(1)}, u32[]{:S(2)}, u32[]{:S(2)}) %all-to-all-start.2) | async-done | bytes 1572896 | tf_op jit(solution)/shard_map/all_to_all | solution.py:635
  103.8 34.6 %forward.1 = (bf16[1024,512]{1,0:T(8,128)(2,1)}, bf16[1024,512]{1,0:T(8,128)(2,1)}, bf16[1024,512]{1,0:T(8,128)(2,1)}, bf16[1024,512]{1,0:T(8,128)(2,1)}, bf16[1...) custom-call(s32[1]{0:T(128)S(6)} %copy.53.len_ref, ...), custom_call_target="tpu_custom_call" | custom-call | tf_op jit(solution)/shard_map/forward/pallas_call | solution.py:370
  143.8 39.9 %backward.1 = (bf16[1536,512]{1,0:T(8,128)(2,1)}, bf16[1536,512]{1,0:T(8,128)(2,1)}, bf16[1024,1536]{1,0:T(8,128)(2,1)}, f32[8,32]{1,0:T(8,128)}, f32[8,512]{1,0:T(8,128)}) custom-call(s32[1]{0:T(128)S(6)} %copy.53.len_ref, bf16[1024,512]{1,0:T(8,128)(2,1)} %get-tuple-element.42.x_ref, bf16[1024,512]{1,0:T(8,128)(2,1)} %get-tuple-element.43.v_ref, ...), custom_call_target="tpu_custom_call" | custom-call | tf_op jit(solution)/shard_map/backward/pallas_call | solution.py:514
  189.7 5.3 %weight_grad.3 = bf16[1536,512]{1,0:T(8,128)(2,1)} custom-call(bf16[1024,512]{1,0:T(8,128)(2,1)} %get-tuple-element.58.n1_ref, bf16[1024,1536]{1,0:T(8,128)(2,1)} %get-tuple-element.59.dp_ref), custom_call_target="tpu_custom_call" | custom-call | tf_op jit(solution)/shard_map/weight_grad/pallas_call | solution.py:539
  200.3 6.6 %all-to-all-start.5 = ((bf16[16,32,512]{2,1,0:T(8,128)(2,1)}), bf16[16,32,512]{2,1,0:T(8,128)(2,1)S(1)}, u32[]{:S(2)}, u32[]{:S(2)}) async-start(bf16[16,32,512]{2,1,0:T(8,128)(2,1)} %bitcast.11), calls=%async_computation.5 | async-start | bytes 1048576 | tf_op jit(solution)/shard_map/all_to_all | solution.py:590
  207.9 14.4 %all-to-all-done.5 = bf16[16,32,512]{2,1,0:T(8,128)(2,1)S(1)} async-done(((bf16[16,32,512]{2,1,0:T(8,128)(2,1)}), bf16[16,32,512]{2,1,0:T(8,128)(2,1)S(1)}, u32[]{:S(2)}, u32[]{:S(2)}) %all-to-all-start.5) | async-done | bytes 524320 | tf_op jit(solution)/shard_map/all_to_all | solution.py:590
  222.3 4.1 %all-to-all-start.7 = ((bf16[16,48,512]{2,1,0:T(8,128)(2,1)}), bf16[16,48,512]{2,1,0:T(8,128)(2,1)S(1)}, u32[]{:S(2)}, u32[]{:S(2)}) async-start(bf16[16,48,512]{2,1,0:T(8,128)(2,1)} %bitcast.13), calls=%async_computation.7 | async-start | bytes 1572864 | tf_op jit(solution)/shard_map/all_to_all | solution.py:590
  226.5 18.9 %all-to-all-done.7 = bf16[16,48,512]{2,1,0:T(8,128)(2,1)S(1)} async-done(((bf16[16,48,512]{2,1,0:T(8,128)(2,1)}), bf16[16,48,512]{2,1,0:T(8,128)(2,1)S(1)}, u32[]{:S(2)}, u32[]{:S(2)}) %all-to-all-start.7) | async-done | bytes 786464 | tf_op jit(solution)/shard_map/all_to_all | solution.py:590
  245.4 19.0 %all_to_all.57 = bf16[16,32,512]{2,1,0:T(8,128)(2,1)} all-to-all(bf16[16,32,512]{2,1,0:T(8,128)(2,1)S(1)} %broadcast_in_dim.10), channel_id=1, replica_groups=mesh['zh'=2,'b'=4,'y'=2,'c'=2] {'zh','b','y'}, dimensions={0} | all-to-all | bytes 1048576 | tf_op jit(solution)/shard_map/all_to_all | solution.py:592
  268.3 22.6 %all-to-all-done.4 = bf16[16,96,512]{2,1,0:T(8,128)(2,1)S(1)} async-done(((bf16[16,96,512]{2,1,0:T(8,128)(2,1)}), bf16[16,96,512]{2,1,0:T(8,128)(2,1)S(1)}, u32[]{:S(2)}, u32[]{:S(2)}) %all-to-all-start.4) | async-done | bytes 1572896 | tf_op jit(solution)/shard_map/all_to_all | solution.py:635
  290.9 24.8 %all_to_all.58 = bf16[16,48,512]{2,1,0:T(8,128)(2,1)} all-to-all(bf16[16,48,512]{2,1,0:T(8,128)(2,1)S(1)} %broadcast_in_dim.11), channel_id=1, replica_groups=mesh['zh'=2,'b'=4,'y'=2,'c'=2] {'zh','b','y'}, dimensions={0} | all-to-all | bytes 1572864 | tf_op jit(solution)/shard_map/all_to_all | solution.py:592
  315.8 4.1 %all-to-all-start.3 = ((bf16[16,96,512]{2,1,0:T(8,128)(2,1)}), bf16[16,96,512]{2,1,0:T(8,128)(2,1)S(1)}, u32[]{:S(2)}, u32[]{:S(2)}) async-start(bf16[16,96,512]{2,1,0:T(8,128)(2,1)} %bitcast.31), calls=%async_computation.3 | async-start | bytes 3145728 | tf_op jit(solution)/shard_map/all_to_all | solution.py:635
  334.7 15.9 %all-to-all-done.3 = bf16[16,96,512]{2,1,0:T(8,128)(2,1)S(1)} async-done(((bf16[16,96,512]{2,1,0:T(8,128)(2,1)}), bf16[16,96,512]{2,1,0:T(8,128)(2,1)S(1)}, u32[]{:S(2)}, u32[]{:S(2)}) %all-to-all-start.3) | async-done | bytes 1572896 | tf_op jit(solution)/shard_map/all_to_all | solution.py:635
  350.6 15.4 %collective-permute-done.1.far_ref = bf16[784,512]{1,0:T(8,128)(2,1)S(1)} collective-permute-done((bf16[784,512]{1,0:T(8,128)(2,1)}, bf16[784,512]{1,0:T(8,128)(2,1)S(1)}, u32[]{:S(2)}, u32[]{:S(2)}) %collective-permute-start.1) | collective-permute-done | bytes 802848 | tf_op jit(solution)/shard_map/ppermute | solution.py:654
  366.8 5.7 %update_rows.1 = (f32[784,512]{1,0:T(8,128)}, f32[784,1]{1,0:T(8,128)}) custom-call(s32[1,1536]{1,0:T(1,128)} %reshape.123.ids_ref, bf16[1536,512]{1,0:T(8,128)(2,1)} %bitcast.21, bf16[784,512]{1,0:T(8,128)(2,1)} %copy-done.15, f32[784,512]{1,0:T(8,128)} %table_ref.1, f32[784,1]{1,0:T(8,128)} %reshape.148.acc_ref), custom_call_target="tpu_custom_call" | custom-call | tf_op jit(solution)/shard_map/update_rows/pallas_call | solution.py:573
  377.2 7.7 %add_multiply_fusion = (f32[512,2048]{1,0:T(8,128)}, f32[512,2048]{1,0:T(8,128)}, f32[512,2048]{1,0:T(8,128)}) fusion(f32[512,2048]{1,0:T(8,128)S(1)} %copy-done, bf16[512,512]{1,0:T(8,128)(2,1)S(1)} %get-tuple-element.77, bf16[512,512]{1,0:T(8,128)(2,1)S(1)} %get-tuple-element.78, bf16[512,512]{1,0:T(8,128)(2,1)S(1)} %get-tuple-element.76, ...), kind=kLoop, calls=%fused_computation.4 | loop fusion | flops 20971520 | bytes 27262976 | tf_op jit(solution)/shard_map/mul | solution.py:76
  (116 shorter events, 64.4 us)
Async XLA Ops:
  9.1 11.9 %all-to-all-start = ((s32[16,1,192]{2,1,0:T(1,128)}), s32[16,1,192]{2,1,0:T(1,128)S(1)}, u32[]{:S(2)}, u32[]{:S(2)}) async-start(s32[16,1,192]{2,1,0:T(1,128)} %copy.45), calls=%async_computation | async-start | bytes 32768 | tf_op jit(solution)/shard_map/all_to_all | solution.py:630
  27.0 44.3 %all-to-all-start.1 = ((bf16[16,96,512]{2,1,0:T(8,128)(2,1)}), bf16[16,96,512]{2,1,0:T(8,128)(2,1)S(1)}, u32[]{:S(2)}, u32[]{:S(2)}) async-start(bf16[16,96,512]{2,1,0:T(8,128)(2,1)} %bitcast.23), calls=%async_computation.1 | async-start | bytes 3145728 | tf_op jit(solution)/shard_map/all_to_all | solution.py:635
  30.8 35.3 %collective-permute-start = (bf16[784,512]{1,0:T(8,128)(2,1)S(1)}, bf16[784,512]{1,0:T(8,128)(2,1)S(1)}, u32[]{:S(2)}, u32[]{:S(2)}) collective-permute-start(bf16[784,512]{1,0:T(8,128)(2,1)S(1)} %copy-done.10), channel_id=1, source_target_pairs={{0,16},{16,0},{1,17},{17,1},{2,18},{18,2},{3,19},{19,3},{4,20},{20... | collective-permute-start | bytes 2408456 | tf_op jit(solution)/shard_map/ppermute | solution.py:628
  71.3 31.3 %all-to-all-start.2 = ((bf16[16,96,512]{2,1,0:T(8,128)(2,1)}), bf16[16,96,512]{2,1,0:T(8,128)(2,1)S(1)}, u32[]{:S(2)}, u32[]{:S(2)}) async-start(bf16[16,96,512]{2,1,0:T(8,128)(2,1)} %bitcast.22), calls=%async_computation.2 | async-start | bytes 3145728 | tf_op jit(solution)/shard_map/all_to_all | solution.py:635
  143.7 53.7 %collective-permute-start.2 = (bf16[512,512]{1,0:T(8,128)(2,1)}, bf16[512,512]{1,0:T(8,128)(2,1)}, u32[]{:S(2)}, u32[]{:S(2)}) collective-permute-start(bf16[512,512]{1,0:T(8,128)(2,1)} %fusion.4), channel_id=1, source_target_pairs={{0,1},{1,0},{2,3},{3,2},{4,5},{5,4},{6,7},{7,6},{8,9},{9,8},{10,11... | collective-permute-start | bytes 1572872 | tf_op jit(solution)/shard_map/ppermute | solution.py:589
  143.7 40.6 %copy-start.22 = (f32[8,512]{1,0:T(8,128)S(1)}, f32[8,512]{1,0:T(8,128)}, u32[]{:S(2)}) copy-start(f32[8,512]{1,0:T(8,128)} %get-tuple-element.61) | copy-start | bytes 49156
  143.7 41.4 %copy-start.25 = (f32[8,128]{1,0:T(8,128)S(1)}, f32[8,128]{1,0:T(8,128)}, u32[]{:S(2)}) copy-start(f32[8,128]{1,0:T(8,128)} %get-tuple-element.63) | copy-start | bytes 12292
  186.1 14.2 %all-to-all-start.9 = ((f32[32,8,256]{2,1,0:T(8,128)}), f32[32,8,256]{2,1,0:T(8,128)S(1)}, u32[]{:S(2)}, u32[]{:S(2)}) async-start(f32[32,8,256]{2,1,0:T(8,128)} %broadcast_in_dim.26), calls=%async_computation.9 | async-start | bytes 524288 | tf_op jit(solution)/shard_map/all_to_all | solution.py:668
  197.1 9.7 %collective-permute-start.4 = (bf16[768,512]{1,0:T(8,128)(2,1)}, bf16[768,512]{1,0:T(8,128)(2,1)S(1)}, u32[]{:S(2)}, u32[]{:S(2)}) collective-permute-start(bf16[768,512]{1,0:T(8,128)(2,1)} %constant_dynamic-slice_fusion), channel_id=1, source_target_pairs={{0,1},{1,0},{2,3},{3,2},{4,5},{5,4},{6,7},{7,6},{8,9},{9,8},{10,11... | collective-permute-start | bytes 2359304 | tf_op jit(solution)/shard_map/ppermute | solution.py:589
  200.3 22.1 %all-to-all-start.5 = ((bf16[16,32,512]{2,1,0:T(8,128)(2,1)}), bf16[16,32,512]{2,1,0:T(8,128)(2,1)S(1)}, u32[]{:S(2)}, u32[]{:S(2)}) async-start(bf16[16,32,512]{2,1,0:T(8,128)(2,1)} %bitcast.11), calls=%async_computation.5 | async-start | bytes 1048576 | tf_op jit(solution)/shard_map/all_to_all | solution.py:590
  222.3 23.1 %all-to-all-start.7 = ((bf16[16,48,512]{2,1,0:T(8,128)(2,1)}), bf16[16,48,512]{2,1,0:T(8,128)(2,1)S(1)}, u32[]{:S(2)}, u32[]{:S(2)}) async-start(bf16[16,48,512]{2,1,0:T(8,128)(2,1)} %bitcast.13), calls=%async_computation.7 | async-start | bytes 1572864 | tf_op jit(solution)/shard_map/all_to_all | solution.py:590
  264.4 26.5 %all-to-all-start.4 = ((bf16[16,96,512]{2,1,0:T(8,128)(2,1)}), bf16[16,96,512]{2,1,0:T(8,128)(2,1)S(1)}, u32[]{:S(2)}, u32[]{:S(2)}) async-start(bf16[16,96,512]{2,1,0:T(8,128)(2,1)} %bitcast.32), calls=%async_computation.4 | async-start | bytes 3145728 | tf_op jit(solution)/shard_map/all_to_all | solution.py:635
  268.1 51.8 %copy-start.21 = (f32[784]{0:T(1024)S(1)}, f32[784]{0:T(1024)}, u32[]{:S(2)}) copy-start(f32[784]{0:T(1024)} %param.19) | copy-start | bytes 9412
  268.2 54.7 %copy-start.18 = (f32[8,32]{1,0:T(8,128)S(1)}, f32[8,32]{1,0:T(8,128)}, u32[]{:S(2)}) copy-start(f32[8,32]{1,0:T(8,128)} %tb_ref.1) | copy-start | bytes 3076
  268.3 54.7 %copy-start.23 = (f32[8,32]{1,0:T(8,128)S(1)}, f32[8,32]{1,0:T(8,128)}, u32[]{:S(2)}) copy-start(f32[8,32]{1,0:T(8,128)} %param.29) | copy-start | bytes 3076
  268.3 54.7 %copy-start.24 = (f32[8,32]{1,0:T(8,128)S(1)}, f32[8,32]{1,0:T(8,128)}, u32[]{:S(2)}) copy-start(f32[8,32]{1,0:T(8,128)} %param.28) | copy-start | bytes 3076
  290.9 31.5 %copy-start.3 = (bf16[16,96,512]{2,1,0:T(8,128)(2,1)}, bf16[16,96,512]{2,1,0:T(8,128)(2,1)S(1)}, u32[]{:S(2)}) copy-start(bf16[16,96,512]{2,1,0:T(8,128)(2,1)S(1)} %all-to-all-done.4) | copy-start | bytes 4718596
  315.8 13.3 %copy-start.20 = (f32[3,512]{1,0:T(4,128)S(1)}, f32[3,512]{1,0:T(4,128)}, u32[]{:S(2)}) copy-start(f32[3,512]{1,0:T(4,128)} %param.30) | copy-start | bytes 18436
  315.8 34.8 %all-to-all-start.3 = ((bf16[16,96,512]{2,1,0:T(8,128)(2,1)}), bf16[16,96,512]{2,1,0:T(8,128)(2,1)S(1)}, u32[]{:S(2)}, u32[]{:S(2)}) async-start(bf16[16,96,512]{2,1,0:T(8,128)(2,1)} %bitcast.31), calls=%async_computation.3 | async-start | bytes 3145728 | tf_op jit(solution)/shard_map/all_to_all | solution.py:635
  322.9 6.8 %collective-permute-start.3 = (bf16[512,512]{1,0:T(8,128)(2,1)}, bf16[512,512]{1,0:T(8,128)(2,1)}, u32[]{:S(2)}, u32[]{:S(2)}) collective-permute-start(bf16[512,512]{1,0:T(8,128)(2,1)} %bitcast.29), channel_id=1, source_target_pairs={{0,1},{1,0},{2,3},{3,2},{4,5},{5,4},{6,7},{7,6},{8,9},{9,8},{10,11... | collective-permute-start | bytes 1572872 | tf_op jit(solution)/shard_map/ppermute | solution.py:594
  327.3 38.6 %collective-permute-start.1 = (bf16[784,512]{1,0:T(8,128)(2,1)}, bf16[784,512]{1,0:T(8,128)(2,1)S(1)}, u32[]{:S(2)}, u32[]{:S(2)}) collective-permute-start(bf16[784,512]{1,0:T(8,128)(2,1)} %row_sums.1), channel_id=1, source_target_pairs={{0,16},{16,0},{1,17},{17,1},{2,18},{18,2},{3,19},{19,3},{4,20},{20... | collective-permute-start | bytes 2408456 | tf_op jit(solution)/shard_map/ppermute | solution.py:654
  327.6 46.7 %collective-permute-start.5 = (bf16[768,512]{1,0:T(8,128)(2,1)}, bf16[768,512]{1,0:T(8,128)(2,1)}, u32[]{:S(2)}, u32[]{:S(2)}) collective-permute-start(bf16[768,512]{1,0:T(8,128)(2,1)} %bitcast.27), channel_id=1, source_target_pairs={{0,1},{1,0},{2,3},{3,2},{4,5},{5,4},{6,7},{7,6},{8,9},{9,8},{10,11... | collective-permute-start | bytes 2359304 | tf_op jit(solution)/shard_map/ppermute | solution.py:594
  334.6 39.7 %copy-start.11 = (bf16[16,48,512]{2,1,0:T(8,128)(2,1)S(1)}, bf16[16,48,512]{2,1,0:T(8,128)(2,1)}, u32[]{:S(2)}) copy-start(bf16[16,48,512]{2,1,0:T(8,128)(2,1)} %all_to_all.58) | copy-start | bytes 2359300
  350.6 15.4 %copy-start.1 = (bf16[16,96,512]{2,1,0:T(8,128)(2,1)}, bf16[16,96,512]{2,1,0:T(8,128)(2,1)S(1)}, u32[]{:S(2)}) copy-start(bf16[16,96,512]{2,1,0:T(8,128)(2,1)S(1)} %all-to-all-done.3) | copy-start | bytes 4718596
  (17 other events, 105.6 us)

commit v2 on v1

v2 whole, which is shorter than its diff:
```python
import functools
import math

import jax
import jax.numpy as jnp
from jax import lax
from jax.experimental import pallas as pl
from jax.experimental.pallas import tpu as pltpu
from jax.sharding import Mesh
from jax.sharding import PartitionSpec as P


D = 512
H = 8
NB = 32

EPSILON = 1e-06
ROW_RATE = 0.2
LEARN_RATE = 0.01
BETA_ONE = 0.9
BETA_TWO = 0.95
ADAM_EPSILON = 1e-08
WEIGHT_DECAY = 0.1

SWAP = [(0, 1), (1, 0)]
BLK = 256
F32 = jnp.float32
BF16 = jnp.bfloat16
HIGH = lax.Precision.HIGHEST
PARAMS = pltpu.CompilerParams(vmem_limit_bytes=60 * 1024 * 1024)
NT = (((1,), (1,)), ((), ()))
TN = (((0,), (0,)), ((), ()))


def dot(left, right):
    return jnp.dot(left, right, preferred_element_type=F32)


def dot_nt(left, right):
    return lax.dot_general(left, right, NT, preferred_element_type=F32)


def dot_tn(left, right):
    return lax.dot_general(left, right, TN, preferred_element_type=F32)


def iota(shape, dim):
    return lax.broadcasted_iota(jnp.int32, shape, dim)


def one_hot(mask):
    return jnp.where(mask, 1.0, 0.0).astype(BF16)


def at(block):
    return pl.ds(pl.multiple_of(block * BLK, BLK), BLK)


def root_mean(mean_square):
    return jnp.sqrt(mean_square + EPSILON)


def mean_last(values):
    return jnp.mean(values, -1, keepdims=True)


def sds(*shape, dtype=BF16):
    return jax.ShapeDtypeStruct(shape, dtype)


def adam_update(weight, gradient, first, second, decay):
    first_new = BETA_ONE * first + (1.0 - BETA_ONE) * gradient
    second_new = BETA_TWO * second + (1.0 - BETA_TWO) * gradient * gradient
    update = -LEARN_RATE * (first_new / (jnp.sqrt(second_new) + ADAM_EPSILON) + decay * weight)
    return (update, first_new, second_new)


def slots_kernel(devices, capacity, half_ref, ownc_ref, ownr_ref, rows_ref, slotc_ref, slotr_ref, ids_ref):
    requests = ownc_ref.shape[0]
    peers = devices // 2
    shift = half_ref[0] * peers
    relc = ownc_ref[...] - shift
    relc = jnp.where(relc < 0, relc + devices, relc)
    relr = ownr_ref[...] - shift
    relr = jnp.where(relr < 0, relr + devices, relr)
    lower = one_hot(iota((BLK, BLK), 0) > iota((BLK, BLK), 1))
    upper = one_hot(iota((BLK, BLK), 0) < iota((BLK, BLK), 1))
    run_c = jnp.zeros((1, devices), F32)
    run_r = jnp.zeros((devices, 1), F32)
    acc_hi = jnp.zeros((peers, 2 * capacity), F32)
    acc_lo = jnp.zeros((peers, 2 * capacity), F32)
    for block in range(requests // BLK):
        part = slice(block * BLK, (block + 1) * BLK)
        rc = relc[part]
        hits = jnp.where(rc == iota((BLK, devices), 1), 1.0, 0.0)
        before = dot(lower, hits.astype(BF16)) + run_c
        rank = jnp.sum(before * hits, 1, keepdims=True).astype(jnp.int32)
        run_c = run_c + jnp.sum(hits, 0, keepdims=True)
        slotc_ref[part, :] = rc * capacity + rank
        rr = relr[:, part]
        hits_r = jnp.where(rr == iota((devices, BLK), 0), 1.0, 0.0)
        before_r = dot(hits_r.astype(BF16), upper) + run_r
        rank_r = jnp.sum(before_r * hits_r, 0, keepdims=True).astype(jnp.int32)
        run_r = run_r + jnp.sum(hits_r, 1, keepdims=True)
        slotr_ref[:, part] = rr * capacity + rank_r
        far = rc >= peers
        where = one_hot(iota((BLK, 2 * capacity), 1) == rank + jnp.where(far, capacity, 0))
        near_peer = jnp.where(rr >= peers, rr - peers, rr)
        mine = near_peer == iota((peers, BLK), 0)
        rows = rows_ref[:, part]
        hi = rows // 32
        lo = rows - hi * 32
        acc_hi = acc_hi + dot(jnp.where(mine, hi.astype(F32), 0.0).astype(BF16), where)
        acc_lo = acc_lo + dot(jnp.where(mine, lo.astype(F32), 0.0).astype(BF16), where)
    ids_ref[...] = (acc_hi * 32.0 + acc_lo).astype(jnp.int32)


def request_slots(half, owners, item_rows, devices, capacity):
    requests = item_rows.shape[0]
    vmem = pl.BlockSpec(memory_space=pltpu.VMEM)
    return pl.pallas_call(
        functools.partial(slots_kernel, devices, capacity),
        out_shape=(
            sds(requests, 1, dtype=jnp.int32),
            sds(1, requests, dtype=jnp.int32),
            sds(devices // 2, 2 * capacity, dtype=jnp.int32),
        ),
        in_specs=[pl.BlockSpec(memory_space=pltpu.SMEM)] + [vmem] * 3,
        out_specs=[vmem] * 3,
        compiler_params=PARAMS,
        name="request_slots",
    )(half, owners.reshape(requests, 1), owners.reshape(1, requests), item_rows.reshape(1, requests))


def serve_kernel(ids_ref, table_ref, out_ref):
    rows = table_ref.shape[0]
    for block in range(out_ref.shape[0] // BLK):
        part = slice(block * BLK, (block + 1) * BLK)
        hits = one_hot(ids_ref[part, :] == iota((BLK, rows), 1))
        out_ref[part, :] = dot(hits, table_ref[...]).astype(BF16)


def serve(ids, table):
    return pl.pallas_call(
        serve_kernel,
        out_shape=sds(ids.shape[0], table.shape[1]),
        compiler_params=PARAMS,
        name="serve",
    )(ids, table)


def place_kernel(slotc_ref, got_ref, out_ref):
    slots = got_ref.shape[0]
    for block in range(out_ref.shape[0] // BLK):
        part = slice(block * BLK, (block + 1) * BLK)
        hits = one_hot(slotc_ref[part, :] == iota((BLK, slots), 1))
        out_ref[part, :] = dot(hits, got_ref[...]).astype(BF16)


def place(slotc, got):
    return pl.pallas_call(
        place_kernel,
        out_shape=sds(slotc.shape[0], got.shape[1]),
        compiler_params=PARAMS,
        name="place",
    )(slotc, got)


def step_kernel(
    total_tokens,
    len_ref,
    own_ref,
    far_ref,
    slotc_ref,
    slotr_ref,
    w_ref,
    wo_ref,
    gains_ref,
    tb_ref,
    bucketr_ref,
    bucketc_ref,
    out_ref,
    rows_ref,
    n1_ref,
    dp_ref,
    dout_ref,
    dbias_ref,
    stats_ref,
    dgain_ref,
    xs,
    neg,
    gate,
    deriv_ref,
    att,
    v_ref,
    q_ref,
    k_ref,
    baug,
    do_ref,
    abuf,
    sbuf,
    dnacc,
    dwo,
    carry,
    qt,
    dt,
    kt,
    vt,
    dkb,
):
    seq_len = n1_ref.shape[0]
    requests = slotc_ref.shape[0]
    negs = requests - seq_len
    slots = far_ref.shape[0]
    blocks = seq_len // BLK
    length = len_ref[0]
    inv_len = 1.0 / (jnp.zeros((1, 1), jnp.int32) + length).astype(F32)

    def fetch(block):
        hits = one_hot(slotc_ref[at(block), :] - slots == iota((BLK, slots), 1))
        return own_ref[at(block), :].astype(F32) + dot(hits, far_ref[...])

    xs[pl.ds(seq_len, 8), :] = jnp.zeros((8, D), F32)
    tb = 0.5 * tb_ref[...]
    tb_hi = tb.astype(BF16)
    tb_lo = (tb - tb_hi.astype(F32)).astype(BF16)
    head = iota((H, D), 0)
    spot = head // 2 * 128 + jnp.where(head % 2 == 0, 64, 0)
    lane_of = iota((H, D), 1)
    terms = dot_tn(tb_hi, one_hot(lane_of == spot)) + dot_tn(tb_lo, one_hot(lane_of == spot + 1))
    terms = terms.astype(BF16)

    def project(block, sum_x):
        rows = at(block)
        x = fetch(block)
        xs[rows, :] = x
        baug[rows, :] = dot(one_hot(bucketc_ref[rows, :] == iota((BLK, NB), 1)), terms).astype(BF16)
        mean_sq = mean_last(x * x)
        pos = block * BLK + iota((BLK, 1), 0)
        live = pos < length
        n1 = (x * lax.rsqrt(mean_sq + EPSILON) * gains_ref[0:1, :]).astype(BF16)
        n1_ref[rows, :] = n1
        for part in range(4):
            half_pre = dot(n1, w_ref[:, part * D : (part + 1) * D])
            th = jnp.tanh(half_pre)
            bend = half_pre * th
            act = half_pre + bend
            deriv_ref[rows, part * D : (part + 1) * D] = ((1.0 + th) * (1.0 + half_pre - bend)).astype(BF16)
            if part == 0:
                gate[rows, :] = act
            elif part == 1:
                v_ref[rows, :] = jnp.where(live, act, 0.0).astype(BF16)
            elif part == 2:
                q_ref[rows, :] = (act * (0.5 * (D // H) ** -0.5)).astype(BF16)
            else:
                k_ref[rows, :] = act.astype(BF16)
        return sum_x + jnp.sum(jnp.where(live, root_mean(mean_sq), 0.0), keepdims=True)

    sum_x = lax.fori_loop(0, blocks, project, jnp.zeros((1, 1), F32))

    def fetch_neg(block, _):
        neg[at(block), :] = fetch(blocks + block).astype(BF16)
        return 0

    lax.fori_loop(0, negs // BLK, fetch_neg, 0)

    lower = iota((BLK, BLK), 0) >= iota((BLK, BLK), 1)
    lane = iota((1, 128), 1)
    sides = [one_hot(lane < 64), one_hot(lane >= 64)]
    marks = [one_hot(lane // 2 == 32), one_hot(lane // 2 == 0)]

    def attend(pair, _):
        lanes = pl.ds(pl.multiple_of(pair * 128, 128), 128)
        bias = baug[:, lanes]
        keys = [k_ref[:, lanes] * sides[hh] + bias * sides[1 - hh] for hh in range(2)]
        vals = [v_ref[:, lanes] * sides[hh] for hh in range(2)]
        for qb in range(blocks):
            qs = slice(qb * BLK, (qb + 1) * BLK)
            total = jnp.zeros((BLK, 128), F32)
            for hh in range(2):
                query = q_ref[qs, lanes] * sides[hh] + marks[hh]
                for kb in range(qb + 1):
                    span = slice(kb * BLK, (kb + 1) * BLK)
                    half_s = dot_nt(query, keys[hh][span])
                    th = jnp.tanh(half_s)
                    bend = half_s * th
                    score = half_s + bend
                    deriv = (1.0 + th) * (1.0 + half_s - bend)
                    if kb == qb:
                        score = jnp.where(lower, score, 0.0)
                        deriv = jnp.where(lower, deriv, 0.0)
                    low = score.astype(BF16)
                    tile = qb * (qb + 1) // 2 + kb
                    abuf[2 * pair + hh, tile] = low
                    sbuf[2 * pair + hh, tile] = deriv.astype(BF16)
                    total = total + dot(low, vals[hh][span])
            att[qs, lanes] = total * inv_len
        return 0

    lax.fori_loop(0, H // 2, attend, 0)

    scale = 2.0 / math.sqrt(D)
    dnacc[...] = jnp.zeros_like(dnacc)
    dwo[...] = jnp.zeros_like(dwo)
    carry[...] = jnp.zeros_like(carry)
    first_row = iota((BLK, 1), 0) == 0
    last_row = iota((BLK, 1), 0) == BLK - 1

    def middle(block, sums):
        sum_loss, sum_o, sum_b, dg1, dg2 = sums
        rows = at(block)
        x = xs[rows, :]
        pos = block * BLK + iota((BLK, 1), 0)
        live = pos < length
        valid = pos < length - 1
        o = att[rows, :]
        u = gate[rows, :]
        ms_o = mean_last(o * o)
        r2 = lax.rsqrt(ms_o + EPSILON)
        n2 = o * r2 * gains_ref[1:2, :]
        g = (n2 * u).astype(BF16)
        branch = dot(g, wo_ref[...])
        ms_b = mean_last(branch * branch)
        mixed = x + branch
        r3 = lax.rsqrt(mean_last(mixed * mixed) + EPSILON)
        final = (mixed * r3 * gains_ref[2:3, :]).astype(BF16)
        final_f = final.astype(F32)
        after = xs[pl.ds(pl.multiple_of(block * BLK + BLK, 8), 8), :][0:1, :]
        nxt = jnp.where(last_row, after, pltpu.roll(x, BLK - 1, 0))
        target = jnp.sum(final_f * nxt, -1, keepdims=True) * scale
        logits = dot_nt(final, neg[...]) * scale
        top = jnp.maximum(jnp.max(logits, -1, keepdims=True), target)
        powers = jnp.exp(logits - top)
        near = jnp.exp(target - top)
        total = near + jnp.sum(powers, -1, keepdims=True)
        lse = top + jnp.log(total)
        weight = jnp.where(valid, 1.0 / total_tokens, 0.0)
        share = weight / total
        dt_ = (share * near - weight) * scale
        dz = (share * powers).astype(BF16)
        dfin = dt_ * nxt + scale * dot(dz, neg[...])
        dnacc[...] += dot_tn(dz, final)
        dnext = dt_ * final_f
        shifted = jnp.where(first_row, carry[0:1, :], pltpu.roll(dnext, 1, 0))
        carry[...] = jnp.broadcast_to(dnext[BLK - 1 : BLK, :], carry.shape)
        unit3 = mixed * r3
        dg2 = dg2 + jnp.sum(dfin * unit3, 0, keepdims=True)
        scaled = dfin * gains_ref[2:3, :]
        dy = r3 * (scaled - unit3 * mean_last(scaled * unit3))
        att[rows, :] = dy + shifted
        db = dy.astype(BF16)
        dwo[...] += dot_tn(g, db)
        dg = dot_nt(db, wo_ref[...])
        dp_ref[rows, 0:D] = (0.5 * dg * n2 * deriv_ref[rows, 0:D].astype(F32)).astype(BF16)
        dn2 = dg * u
        unit2 = o * r2
        dg1 = dg1 + jnp.sum(dn2 * unit2, 0, keepdims=True)
        scaled2 = dn2 * gains_ref[1:2, :]
        do = (r2 * (0.5 * inv_len)) * (scaled2 - unit2 * mean_last(scaled2 * unit2))
        do_ref[rows, :] = do.astype(BF16)
        return (
            sum_loss + jnp.sum(jnp.where(valid, lse - target, 0.0), keepdims=True),
            sum_o + jnp.sum(jnp.where(live, root_mean(ms_o), 0.0), keepdims=True),
            sum_b + jnp.sum(jnp.where(live, root_mean(ms_b), 0.0), keepdims=True),
            dg1,
            dg2,
        )

    zero = jnp.zeros((1, 1), F32)
    zrow = jnp.zeros((1, D), F32)
    sum_loss, sum_o, sum_b, dg1, dg2 = lax.fori_loop(0, blocks, middle, (zero, zero, zero, zrow, zrow))
    rows_ref[seq_len:requests, :] = (dnacc[...] * scale).astype(BF16)
    dout_ref[...] = dwo[...].astype(BF16)
    which = iota((8, 128), 0)
    stats = jnp.where(which == 0, sum_loss, 0.0) + jnp.where(which == 1, sum_x, 0.0)
    stats_ref[...] = stats + jnp.where(which == 2, sum_o, 0.0) + jnp.where(which == 3, sum_b, 0.0)

    ones = one_hot(iota((16, seq_len), 0) == 0)
    alive = iota((seq_len, 1), 0) < length

    def attend_back(pair, _):
        lanes = pl.ds(pl.multiple_of(pair * 128, 128), 128)
        keys = [k_ref[:, lanes] * side for side in sides]
        vals = [v_ref[:, lanes] * side for side in sides]
        grads = do_ref[:, lanes]
        qtr = q_ref[:, lanes].astype(F32).T.astype(BF16)
        dtr = grads.astype(F32).T.astype(BF16)
        for hh in range(2):
            qt[hh, 0:64, :] = qtr[hh * 64 : hh * 64 + 64, :]
            qt[hh, 64:80, :] = ones
            dt[hh] = dtr[hh * 64 : hh * 64 + 64, :]
        kt[...] = jnp.zeros_like(kt)
        vt[...] = jnp.zeros_like(vt)
        dql = pl.ds(pl.multiple_of(2 * D + pair * 128, 128), 128)
        for qb in range(blocks):
            qs = slice(qb * BLK, (qb + 1) * BLK)
            dq = jnp.zeros((BLK, 128), F32)
            for hh in range(2):
                for kb in range(qb + 1):
                    span = slice(kb * BLK, (kb + 1) * BLK)
                    tile = qb * (qb + 1) // 2 + kb
                    slope = sbuf[2 * pair + hh, tile].astype(F32)
                    ds = (dot_nt(grads[qs], vals[hh][span]) * slope).astype(BF16)
                    dq = dq + dot(ds, keys[hh][span])
                    kt[hh, :, span] += dot(qt[hh, :, qs], ds)
                    vt[hh, :, span] += dot(dt[hh, :, qs], abuf[2 * pair + hh, tile])
            dq = dq * (0.5 * (D // H) ** -0.5)
            dp_ref[qs, dql] = (dq * deriv_ref[qs, dql].astype(F32)).astype(BF16)
        dkl = pl.ds(pl.multiple_of(3 * D + pair * 128, 128), 128)
        dvl = pl.ds(pl.multiple_of(D + pair * 128, 128), 128)
        dk = jnp.concatenate([kt[0, 0:64, :], kt[1, 0:64, :]], 0).T
        dv = jnp.concatenate([vt[0], vt[1]], 0).T
        dp_ref[:, dkl] = (dk * deriv_ref[:, dkl].astype(F32)).astype(BF16)
        dp_ref[:, dvl] = (jnp.where(alive, dv, 0.0) * deriv_ref[:, dvl].astype(F32)).astype(BF16)
        for hh in range(2):
            dkb[pl.ds(2 * pair + hh, 1), :] = kt[hh, 64:65, :]
        return 0

    lax.fori_loop(0, H // 2, attend_back, 0)
    buckets = jnp.where(bucketr_ref[...] == iota((NB, seq_len), 0), 1.0, 0.0)
    dbias_ref[...] = lax.dot_general(dkb[...], buckets, NT, precision=HIGH, preferred_element_type=F32)

    def tail(block, dg0):
        rows = at(block)
        x = xs[rows, :]
        r1 = lax.rsqrt(mean_last(x * x) + EPSILON)
        unit1 = x * r1
        dn1 = dot_nt(dp_ref[rows, :], w_ref[...])
        dg0 = dg0 + jnp.sum(dn1 * unit1, 0, keepdims=True)
        scaled = dn1 * (2.0 * gains_ref[0:1, :])
        dx = r1 * (scaled - unit1 * mean_last(scaled * unit1)) + att[rows, :]
        rows_ref[rows, :] = dx.astype(BF16)
        return dg0

    dg0 = 2.0 * lax.fori_loop(0, blocks, tail, zrow)
    row = iota((8, D), 0)
    gsum = jnp.where(row == 0, dg0, 0.0) + jnp.where(row == 1, dg1, 0.0)
    dgain_ref[...] = gsum + jnp.where(row == 2, dg2, 0.0)

    def put(block, _):
        slot = slots + block * BLK + iota((BLK, 1), 0)
        out_ref[at(block), :] = dot(one_hot(slotr_ref[...] == slot), rows_ref[...]).astype(BF16)
        return 0

    lax.fori_loop(0, slots // BLK, put, 0)


def step(length, own, far, slotc, slotr, w, wo, gains, time_bias, buckets, total_tokens):
    seq_len = buckets.shape[1]
    requests = slotc.shape[0]
    negs = requests - seq_len
    slots = far.shape[0]
    vmem = pl.BlockSpec(memory_space=pltpu.VMEM)
    blocks = seq_len // BLK
    tiles = blocks * (blocks + 1) // 2
    outs = (
        sds(slots, D),
        sds(requests, D),
        sds(seq_len, D),
        sds(seq_len, 4 * D),
        sds(D, D),
        sds(H, NB, dtype=F32),
        sds(8, 128, dtype=F32),
        sds(8, D, dtype=F32),
    )
    return pl.pallas_call(
        functools.partial(step_kernel, total_tokens),
        out_shape=outs,
        in_specs=[pl.BlockSpec(memory_space=pltpu.SMEM)] + [vmem] * 10,
        out_specs=[vmem] * len(outs),
        scratch_shapes=[
            pltpu.VMEM((seq_len + 8, D), F32),
            pltpu.VMEM((negs, D), BF16),
            pltpu.VMEM((seq_len, D), F32),
            pltpu.VMEM((seq_len, 4 * D), BF16),
            pltpu.VMEM((seq_len, D), F32),
            pltpu.VMEM((seq_len, D), BF16),
            pltpu.VMEM((seq_len, D), BF16),
            pltpu.VMEM((seq_len, D), BF16),
            pltpu.VMEM((seq_len, D), BF16),
            pltpu.VMEM((seq_len, D), BF16),
            pltpu.VMEM((H, tiles, BLK, BLK), BF16),
            pltpu.VMEM((H, tiles, BLK, BLK), BF16),
            pltpu.VMEM((negs, D), F32),
            pltpu.VMEM((D, D), F32),
            pltpu.VMEM((8, D), F32),
            pltpu.VMEM((2, 80, seq_len), BF16),
            pltpu.VMEM((2, 64, seq_len), BF16),
            pltpu.VMEM((2, 80, seq_len), F32),
            pltpu.VMEM((2, 64, seq_len), F32),
            pltpu.VMEM((H, seq_len), F32),
        ],
        compiler_params=PARAMS,
        cost_estimate=pl.CostEstimate(flops=50_000_000_000, bytes_accessed=15_000_000, transcendentals=0),
        name="step",
    )(length, own, far, slotc, slotr, w, wo, gains, time_bias, buckets, buckets.reshape(seq_len, 1))


def spread_kernel(slotr_ref, rows_ref, out_ref):
    def put(block, _):
        slot = block * BLK + iota((BLK, 1), 0)
        out_ref[at(block), :] = dot(one_hot(slotr_ref[...] == slot), rows_ref[...]).astype(BF16)
        return 0

    lax.fori_loop(0, out_ref.shape[0] // BLK, put, 0)


def spread(slotr, rows, slots):
    return pl.pallas_call(
        spread_kernel,
        out_shape=sds(slots, D),
        compiler_params=PARAMS,
        name="spread",
    )(slotr, rows)


def weight_kernel(n1_ref, dp_ref, out_ref, turned):
    @pl.when(pl.program_id(0) == 0)
    def _():
        turned[...] = n1_ref[...].astype(F32).T.astype(BF16)

    out_ref[...] = dot(turned[...], dp_ref[...]).astype(BF16)


def weight_grad(n1, dp):
    parts = dp.shape[1] // D
    seq_len = n1.shape[0]
    return pl.pallas_call(
        weight_kernel,
        grid=(parts,),
        out_shape=sds(dp.shape[1], D),
        in_specs=[pl.BlockSpec((seq_len, D), lambda i: (0, 0)), pl.BlockSpec((seq_len, D), lambda i: (0, i))],
        out_specs=pl.BlockSpec((D, D), lambda i: (i, 0)),
        scratch_shapes=[pltpu.VMEM((D, seq_len), BF16)],
        compiler_params=PARAMS,
        name="weight_grad",
    )(n1, dp)


def gather_kernel(ids_ref, got_ref, out_ref):
    rows, slots = (out_ref.shape[0], got_ref.shape[0])
    hits = one_hot(ids_ref[...] == iota((rows, slots), 0))
    out_ref[...] = dot(hits, got_ref[...]).astype(BF16)


def row_sums(ids, got, rows):
    return pl.pallas_call(
        gather_kernel,
        out_shape=sds(rows, got.shape[1]),
        compiler_params=PARAMS,
        name="row_sums",
    )(ids, got)


def update_kernel(ids_ref, got_ref, far_ref, table_ref, acc_ref, table_out, acc_out):
    rows, slots = (table_ref.shape[0], got_ref.shape[0])
    hits = one_hot(ids_ref[...] == iota((rows, slots), 0))
    sums = dot(hits, got_ref[...]) + far_ref[...].astype(F32)
    acc = acc_ref[...] + mean_last(sums * sums)
    acc_out[...] = acc
    table_out[...] = table_ref[...] - ROW_RATE * sums * lax.rsqrt(acc)


def update_rows(ids, got, far, table, row_acc):
    rows = table.shape[0]
    new_table, new_acc = pl.pallas_call(
        update_kernel,
        out_shape=(sds(*table.shape, dtype=F32), sds(rows, 1, dtype=F32)),
        compiler_params=PARAMS,
        name="update_rows",
    )(ids, got, far, table, row_acc.reshape(rows, 1))
    return new_table, new_acc.reshape(rows)


def sum_chips(grad, axes):
    pair = axes[-1]
    chips = axes[:-1]
    rows, width = grad.shape
    core = lax.axis_index(pair)
    half = rows // 2
    keep = lax.dynamic_slice_in_dim(grad, core * half, half, 0)
    give = lax.dynamic_slice_in_dim(grad, (1 - core) * half, half, 0)
    part = keep.astype(F32) + lax.ppermute(give, pair, SWAP).astype(F32)
    part = part.astype(BF16).reshape((2,) * len(chips) + (half >> len(chips), width))
    for dim in reversed(range(len(chips))):
        here = lax.axis_index(chips[dim])
        give = lax.dynamic_index_in_dim(part, 1 - here, dim, keepdims=True)
        keep = lax.dynamic_index_in_dim(part, here, dim, keepdims=True)
        got = lax.ppermute(give, chips[dim], SWAP)
        part = (keep.astype(F32) + got.astype(F32)).astype(BF16)
    return part.reshape(half >> len(chips), width)


def share_chips(part, extra, axes):
    pair = axes[-1]
    chips = axes[:-1]
    count = lax.axis_size(chips)
    rows, width = part.shape
    packed = jnp.concatenate([part, extra], 0)[None]
    got = lax.all_to_all(jnp.broadcast_to(packed, (count,) + packed.shape[1:]), chips, 0, 0, tiled=True)
    whole = got[:, :rows].reshape(count * rows, width)
    other = lax.ppermute(whole, pair, SWAP)
    core = lax.axis_index(pair)
    dense = jnp.where(core == 0, jnp.concatenate([whole, other], 0), jnp.concatenate([other, whole], 0))
    return dense, got[:, rows:]


def per_device(
    axes,
    table,
    row_acc,
    uvqk_weight,
    out_weight,
    time_bias,
    gains,
    uvqk_m,
    uvqk_v,
    out_m,
    out_v,
    bias_m,
    bias_v,
    gain_m,
    gain_v,
    lengths,
    time_buckets,
    item_rows,
    row_owner,
):
    every = axes
    near = axes[1:]
    devices = lax.axis_size(every)
    peers = devices // 2
    requests = item_rows.shape[0]
    capacity = max(2, 2 * requests // devices)
    rows = table.shape[0]
    slots = peers * capacity
    total_tokens = float(time_buckets.size * devices)
    half = lax.axis_index(axes[0]).reshape(1)

    def exchange(values):
        return lax.all_to_all(values.reshape(peers, capacity, D), near, 0, 0, tiled=True).reshape(slots, D)

    table_low = table.astype(BF16)
    table_far = lax.ppermute(table_low, axes[0], SWAP)
    slotc, slotr, ids = request_slots(half, row_owner, item_rows, devices, capacity)
    ids = lax.all_to_all(ids, near, 0, 0, tiled=True)
    ids_own = ids[:, :capacity]
    ids_far = ids[:, capacity:]
    serve_own = serve(ids_own.reshape(slots, 1), table_low)
    got_own = exchange(serve_own)
    serve_far = serve(ids_far.reshape(slots, 1), table_far)
    got_far = exchange(serve_far)
    own = place(slotc, got_own)

    w_low = (0.5 * uvqk_weight).astype(BF16)
    wo_low = out_weight.astype(BF16)
    send_far, row_grads, n1, dp, dout, dbias, stats, dgain = step(
        lengths, own, got_far, slotc, slotr, w_low, wo_low, gains, time_bias, time_buckets, total_tokens
    )
    back_far = exchange(send_far)
    send_own = spread(slotr, row_grads, slots)
    dense = jnp.concatenate([dout, weight_grad(n1, dp)], 0)
    sums_far = row_sums(ids_far.reshape(1, slots), back_far, rows)
    sums_far = lax.ppermute(sums_far, axes[0], SWAP)
    back_own = exchange(send_own)
    new_table, new_acc = update_rows(ids_own.reshape(1, slots), back_own, sums_far, table, row_acc)

    small = jnp.concatenate(
        [
            dbias.reshape(-1),
            dgain[:3].reshape(-1),
            stats[:4, 0],
            jnp.zeros((2048 - H * NB - 3 * D - 4,), F32),
        ]
    ).reshape(4, D)
    small = small + lax.ppermute(small, axes[-1], SWAP)
    small_hi = lax.reduce_precision(small, 8, 7)
    small_lo = (small - small_hi).astype(BF16)
    small_hi = small_hi.astype(BF16)
    part = sum_chips(dense, axes)
    dense, small = share_chips(part, jnp.concatenate([small_hi, small_lo], 0), axes)
    small = jnp.sum(small.astype(F32), 0)
    small = (small[:4] + small[4:]).reshape(-1)
    sum_bias = small[: H * NB].reshape(H, NB)
    sum_gains = small[H * NB : H * NB + 3 * D].reshape(3, D)
    sums = small[H * NB + 3 * D : H * NB + 3 * D + 4] / total_tokens
    summary = jnp.stack([sums[0], sums[1], sums[3]])
    attention_rms = sums[2:3]

    sum_out = dense[:D].astype(F32)
    sum_uvqk = jnp.concatenate([dense[i * D : i * D + D] for i in range(1, 5)], 1).astype(F32)
    uvqk_step, uvqk_m_new, uvqk_v_new = adam_update(
        uvqk_weight, sum_uvqk, uvqk_m, uvqk_v, WEIGHT_DECAY
    )
    out_step, out_m_new, out_v_new = adam_update(out_weight, sum_out, out_m, out_v, WEIGHT_DECAY)
    bias_step, bias_m_new, bias_v_new = adam_update(time_bias, sum_bias, bias_m, bias_v, 0.0)
    gain_step, gain_m_new, gain_v_new = adam_update(gains, sum_gains, gain_m, gain_v, 0.0)
    return (
        new_table,
        new_acc,
        uvqk_step,
        uvqk_m_new,
        uvqk_v_new,
        out_step,
        out_m_new,
        out_v_new,
        bias_step,
        bias_m_new,
        bias_v_new,
        gain_step,
        gain_m_new,
        gain_v_new,
        summary,
        attention_rms,
    )


def solution(mesh):
    sizes = (mesh.shape["dp"], mesh.shape["mp"])
    bits = [size.bit_length() - 1 for size in sizes]
    axes = tuple(f"d{i}" for i in range(bits[0])) + tuple(f"m{i}" for i in range(bits[1]))
    fine = Mesh(mesh.devices.reshape((2,) * len(axes)), axes)
    split = P(axes)
    whole = P()

    def body(*args):
        return per_device(axes, *args)

    return jax.shard_map(
        body,
        mesh=fine,
        in_specs=(split, split) + (whole,) * 12 + (split,) * 4,
        out_specs=(split, split) + (whole,) * 14,
        check_vma=False,
    )
```

time: 386 us -> 344 us (0.89)
  blocking collectives: 43.8 us -> 0 us
  waiting for transfers between devices: 133 us -> 155 us
  Pallas kernels: 110 us -> 96.7 us
  other arithmetic: 32.1 us -> 24.4 us
    ppermute x6 -> x9, waiting for transfers between devices: 46.5 us -> 132 us  [the longest x1 56.4 us: per_device(): sums_far = lax.ppermute(sums_far, axes[0], SWAP)]
    all_to_all x8 -> x6, waiting for transfers between devices: 86.9 us -> 23.5 us  [the longest x4 19 us: exchange(): lax.all_to_all(values.reshape(peers, capacity, D), near, 0, 0, tiled=True)]
    all_to_all x2 -> x0, blocking collectives: 43.8 us -> none  [sum_dense(): lax.all_to_all(jnp.broadcast_to(mine[None], parts.shape), CHIPS, 0, 0, ti...]
    pallas_call x4 -> x3, Pallas kernels: 82.9 us -> 69 us  [the longest x1 56.5 us: step(): pl.pallas_call(functools.partial(step_kernel, total_tokens), out_shape=ou...]
    ppermute x6 -> x9, starting transfers between devices: 3.41 us -> 13 us  [the longest x4 7.35 us: sum_chips(): got = lax.ppermute(give, chips[dim], SWAP)]
    all_to_all x8 -> x6, starting transfers between devices: 40.7 us -> 33.6 us  [the longest x4 21.4 us: exchange(): lax.all_to_all(values.reshape(peers, capacity, D), near, 0, 0, tiled=True)]
  transfers between devices with their start and end apart: 14 -> 15, of which waited for: 9 -> 9; matrix products, arithmetic and copies ran while one was open for 7% -> 6% of each run, Pallas kernels for 17% -> 9%
where the time goes in v2:
time: 344 us; the launch traced here: 343 us
  waiting for transfers between devices  155 us (45%)
  Pallas kernels  96.7 us (28%)
  starting transfers between devices  46.7 us (14%)
  other arithmetic  24.4 us (7%)
  local copies, waits for them, and re-layouts  18.7 us (5%)
    pallas_call x1, Pallas kernels, step(): pl.pallas_call(functools.partial(step_kernel, total_tokens), out_shape=ou...  56.5 us
    ppermute x1, waiting for transfers between devices, per_device(): sums_far = lax.ppermute(sums_far, axes[0], SWAP)  56.4 us
    ppermute x4, waiting for transfers between devices, sum_chips(): got = lax.ppermute(give, chips[dim], SWAP)  44 us
    ppermute x1, waiting for transfers between devices, per_device(): table_far = lax.ppermute(table_low, axes[0], SWAP)  31.1 us
    all_to_all x4, starting transfers between devices, exchange(): lax.all_to_all(values.reshape(peers, capacity, D), near, 0, 0, tiled=True)  21.4 us
    all_to_all x4, waiting for transfers between devices, exchange(): lax.all_to_all(values.reshape(peers, capacity, D), near, 0, 0, tiled=True)  19 us
    pallas_call x2, Pallas kernels, serve(): pl.pallas_call(serve_kernel, out_shape=sds(ids.shape[0], table.shape[1]),...  8.8 us
    mul x4, other arithmetic, adam_update(): -LEARN_RATE  8.79 us
  transfers between devices with their start and end apart: 15, of which 9 were waited for; matrix products, arithmetic and copies ran while one was open for 6% of the time, Pallas kernels for 9%

profile of v2, /device:TPU:0, one launch (start us, length us, event | category | flops | bytes accessed | tf_op | source)
XLA Modules:
  0.0 343.2 jit_solution(7726284842237597071)
XLA Ops:
  3.9 3.9 %request_slots.1 = (s32[1536,1]{1,0:T(8,128)}, s32[1,1536]{1,0:T(1,128)}, s32[16,192]{1,0:T(8,128)}) custom-call(s32[1]{0:T(128)} %bitcast.half_ref, s32[1536,1]{1,0:T(8,128)} %copy.40.ownc_ref, s32[1,1536]{1,0:T(1,128)} %bitcast.35, s32[1,1536]{1,0:T(1,128)} %reshape.118.rows_ref), custom_call_target="tpu_custom_call" | custom-call | tf_op jit(solution)/shard_map/request_slots/pallas_call | solution.py:121
  9.2 6.3 %all-to-all-start = ((s32[16,1,192]{2,1,0:T(1,128)}), s32[16,1,192]{2,1,0:T(1,128)S(1)}, u32[]{:S(2)}, u32[]{:S(2)}) async-start(s32[16,1,192]{2,1,0:T(1,128)} %copy.41), calls=%async_computation | async-start | bytes 32768 | tf_op jit(solution)/shard_map/all_to_all | solution.py:646
  16.5 4.6 %all-to-all-done = s32[16,1,192]{2,1,0:T(1,128)S(1)} async-done(((s32[16,1,192]{2,1,0:T(1,128)}), s32[16,1,192]{2,1,0:T(1,128)S(1)}, u32[]{:S(2)}, u32[]{:S(2)}) %all-to-all-start) | async-done | bytes 12320 | tf_op jit(solution)/shard_map/all_to_all | solution.py:646
  22.7 4.4 %serve.2 = bf16[1536,512]{1,0:T(8,128)(2,1)} custom-call(s32[1536,1]{1,0:T(8,128)} %reshape.142.ids_ref, bf16[784,512]{1,0:T(8,128)(2,1)} %convert_element_type.69.table_ref), custom_call_target="tpu_custom_call" | custom-call | tf_op jit(solution)/shard_map/serve/pallas_call | solution.py:144
  27.1 3.7 %all-to-all-start.1 = ((bf16[16,96,512]{2,1,0:T(8,128)(2,1)}), bf16[16,96,512]{2,1,0:T(8,128)(2,1)S(1)}, u32[]{:S(2)}, u32[]{:S(2)}) async-start(bf16[16,96,512]{2,1,0:T(8,128)(2,1)} %bitcast.23), calls=%async_computation.1 | async-start | bytes 3145728 | tf_op jit(solution)/shard_map/all_to_all | solution.py:641
  35.1 31.1 %collective-permute-done.table_ref = bf16[784,512]{1,0:T(8,128)(2,1)S(1)} collective-permute-done((bf16[784,512]{1,0:T(8,128)(2,1)S(1)}, bf16[784,512]{1,0:T(8,128)(2,1)S(1)}, u32[]{:S(2)}, u32[]{:S(2)}) %collective-permute-start) | collective-permute-done | bytes 802848 | tf_op jit(solution)/shard_map/ppermute | solution.py:644
  67.1 4.4 %serve.3 = bf16[1536,512]{1,0:T(8,128)(2,1)} custom-call(s32[1536,1]{1,0:T(8,128)} %reshape.143.ids_ref, bf16[784,512]{1,0:T(8,128)(2,1)} %copy-done.13), custom_call_target="tpu_custom_call" | custom-call | tf_op jit(solution)/shard_map/serve/pallas_call | solution.py:144
  71.4 8.9 %all-to-all-start.2 = ((bf16[16,96,512]{2,1,0:T(8,128)(2,1)}), bf16[16,96,512]{2,1,0:T(8,128)(2,1)}, u32[]{:S(2)}, u32[]{:S(2)}) async-start(bf16[16,96,512]{2,1,0:T(8,128)(2,1)} %bitcast.24), calls=%async_computation.2 | async-start | bytes 3145728 | tf_op jit(solution)/shard_map/all_to_all | solution.py:641
  82.9 4.0 %multiply_convert_fusion.w_ref = bf16[512,2048]{1,0:T(8,128)(2,1)} fusion(f32[512,2048]{1,0:T(8,128)} %param.20), kind=kLoop, calls=%fused_computation.5 | loop fusion | flops 2097152 | bytes 6291456 | tf_op jit(solution)/shard_map/convert_element_type | solution.py:655
  86.9 5.5 %place.1.own_ref = bf16[1536,512]{1,0:T(8,128)(2,1)} custom-call(s32[1536,1]{1,0:T(8,128)} %get-tuple-element.31.slotc_ref, bf16[1536,512]{1,0:T(8,128)(2,1)} %bitcast.26), custom_call_target="tpu_custom_call" | custom-call | tf_op jit(solution)/shard_map/place/pallas_call | solution.py:161
  92.4 10.7 %all-to-all-done.2 = bf16[16,96,512]{2,1,0:T(8,128)(2,1)} async-done(((bf16[16,96,512]{2,1,0:T(8,128)(2,1)}), bf16[16,96,512]{2,1,0:T(8,128)(2,1)}, u32[]{:S(2)}, u32[]{:S(2)}) %all-to-all-start.2) | async-done | bytes 1572896 | tf_op jit(solution)/shard_map/all_to_all | solution.py:641
  103.1 56.5 %step.1 = (bf16[1536,512]{1,0:T(8,128)(2,1)}, bf16[1536,512]{1,0:T(8,128)(2,1)}, bf16[1024,512]{1,0:T(8,128)(2,1)}, bf16[1024,2048]{1,0:T(8,128)(2,1)}, bf16[512...) custom-call(s32[1]{0:T(128)S(6)} %copy.50.len_ref, bf16[1536,512]{1,0:T(8,128)(2,1)} %place.1.own_ref, ...), custom_call_target="tpu_custom_call" | custom-call | flops 49999998976 | bytes 15000000 | tf_op jit(solution)/shard_map/step/pallas_call | solution.py:466
  159.6 4.4 %all-to-all-start.4 = ((bf16[16,96,512]{2,1,0:T(8,128)(2,1)}), bf16[16,96,512]{2,1,0:T(8,128)(2,1)}, u32[]{:S(2)}, u32[]{:S(2)}) async-start(bf16[16,96,512]{2,1,0:T(8,128)(2,1)} %bitcast.31), calls=%async_computation.4 | async-start | bytes 3145728 | tf_op jit(solution)/shard_map/all_to_all | solution.py:641
  164.1 6.4 %weight_grad.1 = bf16[2048,512]{1,0:T(8,128)(2,1)} custom-call(bf16[1024,512]{1,0:T(8,128)(2,1)} %get-tuple-element.37.n1_ref, bf16[1024,2048]{1,0:T(8,128)(2,1)} %get-tuple-element.38.dp_ref), custom_call_target="tpu_custom_call" | custom-call | tf_op jit(solution)/shard_map/weight_grad/pallas_call | solution.py:528
  172.5 6.2 %spread.1 = bf16[1536,512]{1,0:T(8,128)(2,1)} custom-call(s32[1,1536]{1,0:T(1,128)} %get-tuple-element.30.slotr_ref, bf16[1536,512]{1,0:T(8,128)(2,1)} %get-tuple-element.32.rows_ref), custom_call_target="tpu_custom_call" | custom-call | tf_op jit(solution)/shard_map/spread/pallas_call | solution.py:509
  178.6 8.2 %all-to-all-done.4 = bf16[16,96,512]{2,1,0:T(8,128)(2,1)} async-done(((bf16[16,96,512]{2,1,0:T(8,128)(2,1)}), bf16[16,96,512]{2,1,0:T(8,128)(2,1)}, u32[]{:S(2)}, u32[]{:S(2)}) %all-to-all-start.4) | async-done | bytes 1572896 | tf_op jit(solution)/shard_map/all_to_all | solution.py:641
  186.8 4.4 %all-to-all-start.3 = ((bf16[16,96,512]{2,1,0:T(8,128)(2,1)}), bf16[16,96,512]{2,1,0:T(8,128)(2,1)}, u32[]{:S(2)}, u32[]{:S(2)}) async-start(bf16[16,96,512]{2,1,0:T(8,128)(2,1)} %bitcast.25), calls=%async_computation.3 | async-start | bytes 3145728 | tf_op jit(solution)/shard_map/all_to_all | solution.py:641
  195.4 29.6 %collective-permute-done.3 = bf16[2,2,2,1,80,512]{5,4,3,2,1,0:T(8,128)(2,1)S(1)} collective-permute-done((bf16[2,2,2,1,80,512]{5,4,3,2,1,0:T(8,128)(2,1)S(1)}, bf16[2,2,2,1,80,512]{5,4,3,2,1,0:T(8,128)(2,1)S(1)}, u32[]{:S(2)}, u32[]{:S(2)}) %collective-permute-start.3) | collective-permute-done | bytes 655392 | tf_op jit(solution)/shard_map/ppermute | solution.py:589
  226.9 7.7 %collective-permute-done.4 = bf16[2,2,1,1,80,512]{5,4,3,2,1,0:T(8,128)(2,1)S(1)} collective-permute-done((bf16[2,2,1,1,80,512]{5,4,3,2,1,0:T(8,128)(2,1)S(1)}, bf16[2,2,1,1,80,512]{5,4,3,2,1,0:T(8,128)(2,1)S(1)}, u32[]{:S(2)}, u32[]{:S(2)}) %collective-permute-start.4) | collective-permute-done | bytes 327712 | tf_op jit(solution)/shard_map/ppermute | solution.py:589
  247.0 5.9 %all-to-all-start.5 = ((bf16[16,88,512]{2,1,0:T(8,128)(2,1)}), bf16[16,88,512]{2,1,0:T(8,128)(2,1)S(1)}, u32[]{:S(2)}, u32[]{:S(2)}) async-start(bf16[16,88,512]{2,1,0:T(8,128)(2,1)} %broadcast_in_dim.10), calls=%async_computation.5 | async-start | bytes 2883584 | tf_op jit(solution)/shard_map/all_to_all | solution.py:600
  253.6 3.7 %row_sums.1 = bf16[784,512]{1,0:T(8,128)(2,1)} custom-call(s32[1,1536]{1,0:T(1,128)} %reshape.129.ids_ref, bf16[1536,512]{1,0:T(8,128)(2,1)} %bitcast.11.got_ref), custom_call_target="tpu_custom_call" | custom-call | tf_op jit(solution)/shard_map/row_sums/pallas_call | solution.py:547
  261.7 56.4 %collective-permute-done.1.far_ref = bf16[784,512]{1,0:T(8,128)(2,1)S(1)} collective-permute-done((bf16[784,512]{1,0:T(8,128)(2,1)}, bf16[784,512]{1,0:T(8,128)(2,1)S(1)}, u32[]{:S(2)}, u32[]{:S(2)}) %collective-permute-start.1) | collective-permute-done | bytes 802848 | tf_op jit(solution)/shard_map/ppermute | solution.py:664
  319.0 5.7 %update_rows.1 = (f32[784,512]{1,0:T(8,128)}, f32[784,1]{1,0:T(8,128)}) custom-call(s32[1,1536]{1,0:T(1,128)} %reshape.119.ids_ref, bf16[1536,512]{1,0:T(8,128)(2,1)} %bitcast.9.got_ref, bf16[784,512]{1,0:T(8,128)(2,1)} %copy-done.12, f32[784,512]{1,0:T(8,128)} %table_ref.1, f32[784,1]{1,0:T(8,128)} %reshape.144.acc_ref), custom_call_target="tpu_custom_call" | custom-call | tf_op jit(solution)/shard_map/update_rows/pallas_call | solution.py:566
  337.7 5.4 %add_multiply_fusion = (f32[512,2048]{1,0:T(8,128)}, f32[512,2048]{1,0:T(8,128)}, f32[512,2048]{1,0:T(8,128)}) fusion(f32[512,2048]{1,0:T(8,128)S(1)} %copy-done.1, bf16[512,512]{1,0:T(8,128)(2,1)S(1)} %get-tuple-element.55, bf16[512,512]{1,0:T(8,128)(2,1)S(1)} %get-tuple-element.56, bf16[512,512]{1,0:T(8,128)(2,1)S(1)} %get-tuple-element.57, ...), kind=kLoop, calls=%fused_computation.4 | loop fusion | flops 20971520 | bytes 27262976 | tf_op jit(solution)/shard_map/mul | solution.py:74
  (117 shorter events, 53.3 us)
Async XLA Ops:
  0.6 14.9 %copy-start.2 = (f32[784,512]{1,0:T(8,128)S(1)}, f32[784,512]{1,0:T(8,128)}, u32[]{:S(2)}) copy-start(f32[784,512]{1,0:T(8,128)} %table_ref.1) | copy-start | bytes 4816900
  9.2 11.9 %all-to-all-start = ((s32[16,1,192]{2,1,0:T(1,128)}), s32[16,1,192]{2,1,0:T(1,128)S(1)}, u32[]{:S(2)}, u32[]{:S(2)}) async-start(s32[16,1,192]{2,1,0:T(1,128)} %copy.41), calls=%async_computation | async-start | bytes 32768 | tf_op jit(solution)/shard_map/all_to_all | solution.py:646
  27.1 44.3 %all-to-all-start.1 = ((bf16[16,96,512]{2,1,0:T(8,128)(2,1)}), bf16[16,96,512]{2,1,0:T(8,128)(2,1)S(1)}, u32[]{:S(2)}, u32[]{:S(2)}) async-start(bf16[16,96,512]{2,1,0:T(8,128)(2,1)} %bitcast.23), calls=%async_computation.1 | async-start | bytes 3145728 | tf_op jit(solution)/shard_map/all_to_all | solution.py:641
  30.9 35.3 %collective-permute-start = (bf16[784,512]{1,0:T(8,128)(2,1)S(1)}, bf16[784,512]{1,0:T(8,128)(2,1)S(1)}, u32[]{:S(2)}, u32[]{:S(2)}) collective-permute-start(bf16[784,512]{1,0:T(8,128)(2,1)S(1)} %copy-done.8), channel_id=1, source_target_pairs={{0,16},{16,0},{1,17},{17,1},{2,18},{18,2},{3,19},{19,3},{4,20},{20... | collective-permute-start | bytes 2408456 | tf_op jit(solution)/shard_map/ppermute | solution.py:644
  35.1 45.9 %copy-start.17 = (s32[1,1024]{1,0:T(1,128)S(1)}, s32[1,1024]{1,0:T(1,128)}, u32[]{:S(2)}) copy-start(s32[1,1024]{1,0:T(1,128)} %bucketr_ref.1) | copy-start | bytes 12292
  71.4 10.6 %copy-start.4 = (f32[512,512]{1,0:T(8,128)S(1)}, f32[512,512]{1,0:T(8,128)}, u32[]{:S(2)}) copy-start(f32[512,512]{1,0:T(8,128)} %param.21) | copy-start | bytes 3145732
  71.4 11.5 %copy-start.3 = (bf16[16,96,512]{2,1,0:T(8,128)(2,1)}, bf16[16,96,512]{2,1,0:T(8,128)(2,1)S(1)}, u32[]{:S(2)}) copy-start(bf16[16,96,512]{2,1,0:T(8,128)(2,1)S(1)} %all-to-all-done.1) | copy-start | bytes 4718596
  71.4 31.7 %all-to-all-start.2 = ((bf16[16,96,512]{2,1,0:T(8,128)(2,1)}), bf16[16,96,512]{2,1,0:T(8,128)(2,1)}, u32[]{:S(2)}, u32[]{:S(2)}) async-start(bf16[16,96,512]{2,1,0:T(8,128)(2,1)} %bitcast.24), calls=%async_computation.2 | async-start | bytes 3145728 | tf_op jit(solution)/shard_map/all_to_all | solution.py:641
  159.6 27.2 %all-to-all-start.4 = ((bf16[16,96,512]{2,1,0:T(8,128)(2,1)}), bf16[16,96,512]{2,1,0:T(8,128)(2,1)}, u32[]{:S(2)}, u32[]{:S(2)}) async-start(bf16[16,96,512]{2,1,0:T(8,128)(2,1)} %bitcast.31), calls=%async_computation.4 | async-start | bytes 3145728 | tf_op jit(solution)/shard_map/all_to_all | solution.py:641
  172.3 18.9 %collective-permute-start.2 = (bf16[1280,512]{1,0:T(8,128)(2,1)S(1)}, bf16[1280,512]{1,0:T(8,128)(2,1)}, u32[]{:S(2)}, u32[]{:S(2)}) collective-permute-start(bf16[1280,512]{1,0:T(8,128)(2,1)S(1)} %fusion.2), channel_id=1, source_target_pairs={{0,1},{1,0},{2,3},{3,2},{4,5},{5,4},{6,7},{7,6},{8,9},{9,8},{10,11... | collective-permute-start | bytes 3932168 | tf_op jit(solution)/shard_map/ppermute | solution.py:583
  172.5 18.8 %copy-start = (bf16[2048,512]{1,0:T(8,128)(2,1)S(1)}, bf16[2048,512]{1,0:T(8,128)(2,1)}, u32[]{:S(2)}) copy-start(bf16[2048,512]{1,0:T(8,128)(2,1)} %weight_grad.1) | copy-start | bytes 6291460
  186.8 59.0 %all-to-all-start.3 = ((bf16[16,96,512]{2,1,0:T(8,128)(2,1)}), bf16[16,96,512]{2,1,0:T(8,128)(2,1)}, u32[]{:S(2)}, u32[]{:S(2)}) async-start(bf16[16,96,512]{2,1,0:T(8,128)(2,1)} %bitcast.25), calls=%async_computation.3 | async-start | bytes 3145728 | tf_op jit(solution)/shard_map/all_to_all | solution.py:641
  193.5 43.2 %copy-start.22 = (f32[8,32]{1,0:T(8,128)S(1)}, f32[8,32]{1,0:T(8,128)}, u32[]{:S(2)}) copy-start(f32[8,32]{1,0:T(8,128)} %get-tuple-element.39) | copy-start | bytes 3076
  193.5 43.3 %copy-start.23 = (f32[8,512]{1,0:T(8,128)S(1)}, f32[8,512]{1,0:T(8,128)}, u32[]{:S(2)}) copy-start(f32[8,512]{1,0:T(8,128)} %get-tuple-element.40) | copy-start | bytes 49156
  193.5 43.3 %copy-start.24 = (f32[8,128]{1,0:T(8,128)S(1)}, f32[8,128]{1,0:T(8,128)}, u32[]{:S(2)}) copy-start(f32[8,128]{1,0:T(8,128)} %get-tuple-element.41) | copy-start | bytes 12292
  193.6 31.5 %collective-permute-start.3 = (bf16[2,2,2,1,80,512]{5,4,3,2,1,0:T(8,128)(2,1)S(1)}, bf16[2,2,2,1,80,512]{5,4,3,2,1,0:T(8,128)(2,1)S(1)}, u32[]{:S(2)}, u32[]{:S(2)}) collective-permute-start(bf16[2,2,2,1,80,512]{5,4,3,2,1,0:T(8,128)(2,1)S(1)} %constant_dynamic-slice_fusion.3), channel_id=1, source_target_pairs={{0,2},{2,0},{1,3},{3,1},{4,6},{6,4},{5,7},{7,5},{8,10},{10,8},{9,1... | collective-permute-start | bytes 1966088 | tf_op jit(solution)/shard_map/ppermute | solution.py:589
  225.3 9.2 %collective-permute-start.4 = (bf16[2,2,1,1,80,512]{5,4,3,2,1,0:T(8,128)(2,1)S(1)}, bf16[2,2,1,1,80,512]{5,4,3,2,1,0:T(8,128)(2,1)S(1)}, u32[]{:S(2)}, u32[]{:S(2)}) collective-permute-start(bf16[2,2,1,1,80,512]{5,4,3,2,1,0:T(8,128)(2,1)S(1)} %constant_dynamic-slice_fusion.2), channel_id=1, source_target_pairs={{0,4},{4,0},{1,5},{5,1},{2,6},{6,2},{3,7},{7,3},{8,12},{12,8},{9,1... | collective-permute-start | bytes 983048 | tf_op jit(solution)/shard_map/ppermute | solution.py:589
  234.7 5.6 %collective-permute-start.5 = (bf16[2,1,1,1,80,512]{5,4,3,2,1,0:T(8,128)(2,1)S(1)}, bf16[2,1,1,1,80,512]{5,4,3,2,1,0:T(8,128)(2,1)S(1)}, u32[]{:S(2)}, u32[]{:S(2)}) collective-permute-start(bf16[2,1,1,1,80,512]{5,4,3,2,1,0:T(8,128)(2,1)S(1)} %constant_dynamic-slice_fusion.1), channel_id=1, source_target_pairs={{0,8},{8,0},{1,9},{9,1},{2,10},{10,2},{3,11},{11,3},{4,12},{12,4},... | collective-permute-start | bytes 491528 | tf_op jit(solution)/shard_map/ppermute | solution.py:589
  237.0 5.3 %collective-permute-start.7 = (f32[4,512]{1,0:T(4,128)S(1)}, f32[4,512]{1,0:T(4,128)S(1)}, u32[]{:S(2)}, u32[]{:S(2)}) collective-permute-start(f32[4,512]{1,0:T(4,128)S(1)} %reshape.138), channel_id=1, source_target_pairs={{0,1},{1,0},{2,3},{3,2},{4,5},{5,4},{6,7},{7,6},{8,9},{9,8},{10,11... | collective-permute-start | bytes 24584 | tf_op jit(solution)/shard_map/ppermute | solution.py:676
  240.3 5.4 %collective-permute-start.6 = (bf16[1,1,1,1,80,512]{5,4,3,2,1,0:T(8,128)(2,1)S(1)}, bf16[1,1,1,1,80,512]{5,4,3,2,1,0:T(8,128)(2,1)S(1)}, u32[]{:S(2)}, u32[]{:S(2)}) collective-permute-start(bf16[1,1,1,1,80,512]{5,4,3,2,1,0:T(8,128)(2,1)S(1)} %constant_dynamic-slice_fusion), channel_id=1, source_target_pairs={{0,16},{16,0},{1,17},{17,1},{2,18},{18,2},{3,19},{19,3},{4,20},{20... | collective-permute-start | bytes 245768 | tf_op jit(solution)/shard_map/ppermute | solution.py:589
  247.0 13.1 %copy-start.18 = (f32[784]{0:T(1024)S(1)}, f32[784]{0:T(1024)}, u32[]{:S(2)}) copy-start(f32[784]{0:T(1024)} %param.19) | copy-start | bytes 9412
  247.0 79.6 %all-to-all-start.5 = ((bf16[16,88,512]{2,1,0:T(8,128)(2,1)}), bf16[16,88,512]{2,1,0:T(8,128)(2,1)S(1)}, u32[]{:S(2)}, u32[]{:S(2)}) async-start(bf16[16,88,512]{2,1,0:T(8,128)(2,1)} %broadcast_in_dim.10), calls=%async_computation.5 | async-start | bytes 2883584 | tf_op jit(solution)/shard_map/all_to_all | solution.py:600
  257.3 60.8 %collective-permute-start.1 = (bf16[784,512]{1,0:T(8,128)(2,1)}, bf16[784,512]{1,0:T(8,128)(2,1)S(1)}, u32[]{:S(2)}, u32[]{:S(2)}) collective-permute-start(bf16[784,512]{1,0:T(8,128)(2,1)} %row_sums.1), channel_id=1, source_target_pairs={{0,16},{16,0},{1,17},{17,1},{2,18},{18,2},{3,19},{19,3},{4,20},{20... | collective-permute-start | bytes 2408456 | tf_op jit(solution)/shard_map/ppermute | solution.py:664
  326.8 3.3 collective-permute-start.8
  (16 other events, 62.8 us)

commit v3 on v2

--- a/solution.py
+++ b/solution.py
@@ -27,7 +27,8 @@
 F32 = jnp.float32
 BF16 = jnp.bfloat16
 HIGH = lax.Precision.HIGHEST
-PARAMS = pltpu.CompilerParams(vmem_limit_bytes=60 * 1024 * 1024)
+PARAMS = pltpu.CompilerParams(vmem_limit_bytes=16 * 1024 * 1024)
+BIG_PARAMS = pltpu.CompilerParams(vmem_limit_bytes=63 * 1024 * 1024)
 NT = (((1,), (1,)), ((), ()))
 TN = (((0,), (0,)), ((), ()))
 
@@ -75,44 +76,42 @@
     return (update, first_new, second_new)
 
 
-def slots_kernel(devices, capacity, half_ref, ownc_ref, ownr_ref, rows_ref, slotc_ref, slotr_ref, ids_ref):
-    requests = ownc_ref.shape[0]
+def upright(row, size, offset=0):
+    spot = iota((size, row.shape[1]), 1) == iota((size, row.shape[1]), 0) + offset
+    return jnp.sum(jnp.where(spot, row, 0.0), 1, keepdims=True)
+
+
+def slots_kernel(devices, capacity, half_ref, owner_ref, rows_ref, slotc_ref, slotr_ref, ids_ref):
+    requests = owner_ref.shape[1]
     peers = devices // 2
-    shift = half_ref[0] * peers
-    relc = ownc_ref[...] - shift
-    relc = jnp.where(relc < 0, relc + devices, relc)
-    relr = ownr_ref[...] - shift
-    relr = jnp.where(relr < 0, relr + devices, relr)
-    lower = one_hot(iota((BLK, BLK), 0) > iota((BLK, BLK), 1))
+    wide = rows_ref.shape[1]
+    relative = owner_ref[...] - half_ref[0] * peers
+    relative = jnp.where(relative < 0, relative + devices, relative)
     upper = one_hot(iota((BLK, BLK), 0) < iota((BLK, BLK), 1))
-    run_c = jnp.zeros((1, devices), F32)
-    run_r = jnp.zeros((devices, 1), F32)
+    run = jnp.zeros((devices, 1), F32)
     acc_hi = jnp.zeros((peers, 2 * capacity), F32)
     acc_lo = jnp.zeros((peers, 2 * capacity), F32)
     for block in range(requests // BLK):
         part = slice(block * BLK, (block + 1) * BLK)
-        rc = relc[part]
-        hits = jnp.where(rc == iota((BLK, devices), 1), 1.0, 0.0)
-        before = dot(lower, hits.astype(BF16)) + run_c
-        rank = jnp.sum(before * hits, 1, keepdims=True).astype(jnp.int32)
-        run_c = run_c + jnp.sum(hits, 0, keepdims=True)
-        slotc_ref[part, :] = rc * capacity + rank
-        rr = relr[:, part]
-        hits_r = jnp.where(rr == iota((devices, BLK), 0), 1.0, 0.0)
-        before_r = dot(hits_r.astype(BF16), upper) + run_r
-        rank_r = jnp.sum(before_r * hits_r, 0, keepdims=True).astype(jnp.int32)
-        run_r = run_r + jnp.sum(hits_r, 1, keepdims=True)
-        slotr_ref[:, part] = rr * capacity + rank_r
-        far = rc >= peers
-        where = one_hot(iota((BLK, 2 * capacity), 1) == rank + jnp.where(far, capacity, 0))
-        near_peer = jnp.where(rr >= peers, rr - peers, rr)
-        mine = near_peer == iota((peers, BLK), 0)
-        rows = rows_ref[:, part]
+        owner = relative[:, part]
+        hits = jnp.where(owner == iota((devices, BLK), 0), 1.0, 0.0)
+        before = dot(hits.astype(BF16), upper) + run
+        rank = jnp.sum(before * hits, 0, keepdims=True)
+        run = run + jnp.sum(hits, 1, keepdims=True)
+        slot = owner.astype(F32) * capacity + rank
+        slotr_ref[:, part] = slot.astype(jnp.int32)
+        slotc_ref[part, :] = upright(slot, BLK).astype(jnp.int32)
+        far = owner >= peers
+        place_at = upright(rank + jnp.where(far, 1.0 * capacity, 0.0), BLK)
+        where = one_hot(iota((BLK, 2 * capacity), 1) == place_at.astype(jnp.int32))
+        mine = jnp.where(far, owner - peers, owner) == iota((peers, BLK), 0)
+        rows = [rows_ref[i : i + 1, :] for i in range(block * BLK // wide, (block + 1) * BLK // wide)]
+        rows = jnp.concatenate(rows, 1)
         hi = rows // 32
         lo = rows - hi * 32
         acc_hi = acc_hi + dot(jnp.where(mine, hi.astype(F32), 0.0).astype(BF16), where)
         acc_lo = acc_lo + dot(jnp.where(mine, lo.astype(F32), 0.0).astype(BF16), where)
-    ids_ref[...] = (acc_hi * 32.0 + acc_lo).astype(jnp.int32)
+    ids_ref[:, 0, :] = (acc_hi * 32.0 + acc_lo).astype(jnp.int32)
 
 
 def request_slots(half, owners, item_rows, devices, capacity):
@@ -123,30 +122,42 @@
         out_shape=(
             sds(requests, 1, dtype=jnp.int32),
             sds(1, requests, dtype=jnp.int32),
-            sds(devices // 2, 2 * capacity, dtype=jnp.int32),
+            sds(devices // 2, 1, 2 * capacity, dtype=jnp.int32),
         ),
-        in_specs=[pl.BlockSpec(memory_space=pltpu.SMEM)] + [vmem] * 3,
+        in_specs=[pl.BlockSpec(memory_space=pltpu.SMEM)] + [vmem] * 2,
         out_specs=[vmem] * 3,
-        compiler_params=PARAMS,
+        compiler_params=BIG_PARAMS,
         name="request_slots",
-    )(half, owners.reshape(requests, 1), owners.reshape(1, requests), item_rows.reshape(1, requests))
-
-
-def serve_kernel(ids_ref, table_ref, out_ref):
-    rows = table_ref.shape[0]
-    for block in range(out_ref.shape[0] // BLK):
-        part = slice(block * BLK, (block + 1) * BLK)
-        hits = one_hot(ids_ref[part, :] == iota((BLK, rows), 1))
-        out_ref[part, :] = dot(hits, table_ref[...]).astype(BF16)
-
-
-def serve(ids, table):
+    )(half, owners.reshape(1, requests), item_rows.reshape(requests // 128, 128))
+
+
+def serve_kernel(offset, ids_ref, *refs):
+    *table_refs, out_ref, hits = refs
+    rows = table_refs[0].shape[0]
+    table = table_refs[0][...]
+    for other in table_refs[1:]:
+        table = table + other[...]
+    peers = ids_ref.shape[0]
+    capacity = out_ref.shape[0] // peers
+    for peer in range(peers):
+        ids = upright(ids_ref[peer].astype(F32), capacity, offset).astype(jnp.int32)
+        hits[peer * capacity : (peer + 1) * capacity, :] = one_hot(ids == iota((capacity, rows), 1))
+    size = out_ref.shape[0] // 3
+    for block in range(3):
+        part = slice(block * size, (block + 1) * size)
+        out_ref[part, :] = dot(hits[part, :], table).astype(BF16)
+
+
+def serve(ids, tables, offset):
+    slots = ids.shape[0] * (ids.shape[2] // 2)
+    rows, width = tables[0].shape
     return pl.pallas_call(
-        serve_kernel,
-        out_shape=sds(ids.shape[0], table.shape[1]),
+        functools.partial(serve_kernel, offset),
+        out_shape=sds(slots, width),
+        scratch_shapes=[pltpu.VMEM((slots, rows), BF16)],
         compiler_params=PARAMS,
         name="serve",
-    )(ids, table)
+    )(ids, *tables)
 
 
 def place_kernel(slotc_ref, got_ref, out_ref):
@@ -169,6 +180,7 @@
 def step_kernel(
     total_tokens,
     len_ref,
+    core_ref,
     own_ref,
     far_ref,
     slotc_ref,
@@ -181,12 +193,13 @@
     bucketc_ref,
     out_ref,
     rows_ref,
-    n1_ref,
-    dp_ref,
-    dout_ref,
+    keep_ref,
+    give_ref,
     dbias_ref,
     stats_ref,
     dgain_ref,
+    n1_ref,
+    dp_ref,
     xs,
     neg,
     gate,
@@ -209,7 +222,7 @@
     dkb,
 ):
     seq_len = n1_ref.shape[0]
-    requests = slotc_ref.shape[0]
+    requests = rows_ref.shape[0]
     negs = requests - seq_len
     slots = far_ref.shape[0]
     blocks = seq_len // BLK
@@ -370,7 +383,6 @@
     zrow = jnp.zeros((1, D), F32)
     sum_loss, sum_o, sum_b, dg1, dg2 = lax.fori_loop(0, blocks, middle, (zero, zero, zero, zrow, zrow))
     rows_ref[seq_len:requests, :] = (dnacc[...] * scale).astype(BF16)
-    dout_ref[...] = dwo[...].astype(BF16)
     which = iota((8, 128), 0)
     stats = jnp.where(which == 0, sum_loss, 0.0) + jnp.where(which == 1, sum_x, 0.0)
     stats_ref[...] = stats + jnp.where(which == 2, sum_o, 0.0) + jnp.where(which == 3, sum_b, 0.0)
@@ -444,8 +456,29 @@
 
     lax.fori_loop(0, slots // BLK, put, 0)
 
-
-def step(length, own, far, slotc, slotr, w, wo, gains, time_bias, buckets, total_tokens):
+    half = keep_ref.shape[0] // BLK
+
+    def write(block, values):
+        rows = slice(block % half * BLK, (block % half + 1) * BLK)
+
+        @pl.when(core_ref[0] == block // half)
+        def _():
+            keep_ref[rows, :] = values
+
+        @pl.when(core_ref[0] != block // half)
+        def _():
+            give_ref[rows, :] = values
+
+    for side in range(D // BLK):
+        rows = slice(side * BLK, (side + 1) * BLK)
+        write(side, dwo[rows, :].astype(BF16))
+        turned = n1_ref[:, rows].astype(F32).T.astype(BF16)
+        for part in range(4):
+            grad = dot(turned, dp_ref[:, part * D : (part + 1) * D])
+            write((part + 1) * (D // BLK) + side, grad.astype(BF16))
+
+
+def step(length, core, own, far, slotc, slotr, w, wo, gains, time_bias, buckets, total_tokens):
     seq_len = buckets.shape[1]
     requests = slotc.shape[0]
     negs = requests - seq_len
@@ -456,9 +489,8 @@
     outs = (
         sds(slots, D),
         sds(requests, D),
-        sds(seq_len, D),
-        sds(seq_len, 4 * D),
-        sds(D, D),
+        sds(5 * D // 2, D),
+        sds(5 * D // 2, D),
         sds(H, NB, dtype=F32),
         sds(8, 128, dtype=F32),
         sds(8, D, dtype=F32),
@@ -466,9 +498,11 @@
     return pl.pallas_call(
         functools.partial(step_kernel, total_tokens),
         out_shape=outs,
-        in_specs=[pl.BlockSpec(memory_space=pltpu.SMEM)] + [vmem] * 10,
+        in_specs=[pl.BlockSpec(memory_space=pltpu.SMEM)] * 2 + [vmem] * 10,
         out_specs=[vmem] * len(outs),
         scratch_shapes=[
+            pltpu.VMEM((seq_len, D), BF16),
+            pltpu.VMEM((seq_len, 4 * D), BF16),
             pltpu.VMEM((seq_len + 8, D), F32),
             pltpu.VMEM((negs, D), BF16),
             pltpu.VMEM((seq_len, D), F32),
@@ -490,10 +524,10 @@
             pltpu.VMEM((2, 64, seq_len), F32),
             pltpu.VMEM((H, seq_len), F32),
         ],
-        compiler_params=PARAMS,
+        compiler_params=BIG_PARAMS,
         cost_estimate=pl.CostEstimate(flops=50_000_000_000, bytes_accessed=15_000_000, transcendentals=0),
         name="step",
-    )(length, own, far, slotc, slotr, w, wo, gains, time_bias, buckets, buckets.reshape(seq_len, 1))
+    )(length, core, own, far, slotc, slotr, w, wo, gains, time_bias, buckets, buckets.reshape(seq_len, 1))
 
 
 def spread_kernel(slotr_ref, rows_ref, out_ref):
@@ -512,29 +546,6 @@
         compiler_params=PARAMS,
         name="spread",
     )(slotr, rows)
-
-
-def weight_kernel(n1_ref, dp_ref, out_ref, turned):
-    @pl.when(pl.program_id(0) == 0)
-    def _():
-        turned[...] = n1_ref[...].astype(F32).T.astype(BF16)
-
-    out_ref[...] = dot(turned[...], dp_ref[...]).astype(BF16)
-
-
-def weight_grad(n1, dp):
-    parts = dp.shape[1] // D
-    seq_len = n1.shape[0]
-    return pl.pallas_call(
-        weight_kernel,
-        grid=(parts,),
-        out_shape=sds(dp.shape[1], D),
-        in_specs=[pl.BlockSpec((seq_len, D), lambda i: (0, 0)), pl.BlockSpec((seq_len, D), lambda i: (0, i))],
-        out_specs=pl.BlockSpec((D, D), lambda i: (i, 0)),
-        scratch_shapes=[pltpu.VMEM((D, seq_len), BF16)],
-        compiler_params=PARAMS,
-        name="weight_grad",
-    )(n1, dp)
 
 
 def gather_kernel(ids_ref, got_ref, out_ref):
@@ -572,37 +583,132 @@
     return new_table, new_acc.reshape(rows)
 
 
-def sum_chips(grad, axes):
-    pair = axes[-1]
-    chips = axes[:-1]
-    rows, width = grad.shape
-    core = lax.axis_index(pair)
-    half = rows // 2
-    keep = lax.dynamic_slice_in_dim(grad, core * half, half, 0)
-    give = lax.dynamic_slice_in_dim(grad, (1 - core) * half, half, 0)
-    part = keep.astype(F32) + lax.ppermute(give, pair, SWAP).astype(F32)
-    part = part.astype(BF16).reshape((2,) * len(chips) + (half >> len(chips), width))
-    for dim in reversed(range(len(chips))):
-        here = lax.axis_index(chips[dim])
-        give = lax.dynamic_index_in_dim(part, 1 - here, dim, keepdims=True)
-        keep = lax.dynamic_index_in_dim(part, here, dim, keepdims=True)
-        got = lax.ppermute(give, chips[dim], SWAP)
-        part = (keep.astype(F32) + got.astype(F32)).astype(BF16)
-    return part.reshape(half >> len(chips), width)
-
-
-def share_chips(part, extra, axes):
-    pair = axes[-1]
-    chips = axes[:-1]
-    count = lax.axis_size(chips)
+def pick(array, index, dim):
+    return lax.dynamic_index_in_dim(array, index, dim, keepdims=False)
+
+
+def swap(values, axis):
+    return lax.ppermute(values, axis, SWAP)
+
+
+def add(left, right):
+    return (left.astype(F32) + right.astype(F32)).astype(BF16)
+
+
+def turn(values, axes, stage):
+    pairs = []
+    for place in range(8):
+        core = place & 1
+        flip = 4 if core == stage else 2
+        pairs.append((place, place ^ flip))
+    return lax.ppermute(values, axes, pairs)
+
+
+def sum_chips(keep, got, order, pair):
+    rows, width = keep.shape
+    one = lax.axis_index(pair) == 0
+    here, there = (lax.axis_index(order[0]), lax.axis_index(order[1]))
+    outer = jnp.where(one, here, there)
+    inner = jnp.where(one, there, here)
+    plane = order[:2] + (pair,)
+    terms = [values.reshape(2, 2, rows // 4, width) for values in (keep, got)]
+    got = turn(add(*[pick(v, 1 - outer, 0) for v in terms]), plane, 0)
+    terms = [add(*[pick(v, outer, 0) for v in terms]), got]
+    got = turn(add(*[pick(v, 1 - inner, 0) for v in terms]), plane, 1)
+    part = add(add(*[pick(v, inner, 0) for v in terms]), got)
+    for axis in order[2:]:
+        part = part.reshape(2, part.shape[0] // 2, width)
+        here = lax.axis_index(axis)
+        got = swap(pick(part, 1 - here, 0), axis)
+        part = add(pick(part, here, 0), got)
+    return part
+
+
+def join(values, got, first):
+    return jnp.stack([jnp.where(first, values, got), jnp.where(first, got, values)])
+
+
+def share_chips(part, extra, order, pair):
     rows, width = part.shape
-    packed = jnp.concatenate([part, extra], 0)[None]
-    got = lax.all_to_all(jnp.broadcast_to(packed, (count,) + packed.shape[1:]), chips, 0, 0, tiled=True)
-    whole = got[:, :rows].reshape(count * rows, width)
-    other = lax.ppermute(whole, pair, SWAP)
-    core = lax.axis_index(pair)
-    dense = jnp.where(core == 0, jnp.concatenate([whole, other], 0), jnp.concatenate([other, whole], 0))
-    return dense, got[:, rows:]
+    packed = jnp.concatenate([part, extra], 0)
+    for axis in reversed(order[2:]):
+        packed = join(packed, swap(packed, axis), lax.axis_index(axis) == 0)
+    one = lax.axis_index(pair) == 0
+    here, there = (lax.axis_index(order[0]), lax.axis_index(order[1]))
+    plane = order[:2] + (pair,)
+    packed = packed.reshape(-1, rows + extra.shape[0], width)
+    inner, outer = (jnp.where(one, there, here), jnp.where(one, here, there))
+    packed = join(packed, turn(packed, plane, 1), inner == 0)
+    packed = join(packed, turn(packed, plane, 0), outer == 0)
+    whole = packed.reshape(-1, rows + extra.shape[0], width)
+    return whole[:, :rows].reshape(-1, width), whole[:, rows:]
+
+
+def adam_kernel(core_ref, mine_ref, other_ref, *refs):
+    sources, targets, inside_, outside, sem_in, sem_out = (refs[:6], refs[6:12], refs[12:18], refs[18:24], *refs[24:])
+    chunks = sem_in.shape[0]
+    size = D // chunks
+    half = mine_ref.shape[0] // size
+    parts = 1 + sources[0].shape[1] // D
+
+    def copy(chunk, k, incoming):
+        rows = pl.ds(pl.multiple_of(chunk * size, size), size)
+        if incoming:
+            return pltpu.make_async_copy(sources[k].at[rows], inside_[k].at[rows], sem_in.at[chunk, k])
+        return pltpu.make_async_copy(outside[k].at[rows], targets[k].at[rows], sem_out.at[chunk, k])
+
+    def begin(chunk, _):
+        for k in range(6):
+            copy(chunk, k, True).start()
+        return 0
+
+    lax.fori_loop(0, chunks, begin, 0)
+
+    def compute(chunk, _):
+        for k in range(6):
+            copy(chunk, k, True).wait()
+        rows = pl.ds(pl.multiple_of(chunk * size, size), size)
+        for part in range(parts):
+            spot = part * chunks + chunk
+            from_ = pl.ds(pl.multiple_of(lax.rem(spot, half) * size, size), size)
+            own = spot // half == core_ref[0]
+            grad = jnp.where(own, mine_ref[from_, :].astype(F32), other_ref[from_, :].astype(F32))
+            first = 0 if part else 3
+            columns = slice((part - 1) * D, part * D) if part else slice(None)
+            w, m, v = (inside_[first + k][rows, columns] for k in range(3))
+            for k, value in enumerate(adam_update(w, grad, m, v, WEIGHT_DECAY)):
+                outside[first + k][rows, columns] = value
+        for k in range(6):
+            copy(chunk, k, False).start()
+        return 0
+
+    lax.fori_loop(0, chunks, compute, 0)
+
+    def finish(chunk, _):
+        for k in range(6):
+            copy(chunk, k, False).wait()
+        return 0
+
+    lax.fori_loop(0, chunks, finish, 0)
+
+
+def adam(core, mine, other, uvqk, out):
+    chunks = 8
+    vmem = pl.BlockSpec(memory_space=pltpu.VMEM)
+    hbm = pl.BlockSpec(memory_space=pl.ANY)
+    shapes = [uvqk[0].shape] * 3 + [out[0].shape] * 3
+    buffers = [pltpu.VMEM(shape, F32) for shape in shapes]
+    return pl.pallas_call(
+        adam_kernel,
+        out_shape=[sds(*shape, dtype=F32) for shape in shapes],
+        in_specs=[pl.BlockSpec(memory_space=pltpu.SMEM), vmem, vmem] + [hbm] * 6,
+        out_specs=[hbm] * 6,
+        scratch_shapes=buffers
+        + buffers
+        + [pltpu.SemaphoreType.DMA((chunks, 6)), pltpu.SemaphoreType.DMA((chunks, 6))],
+        compiler_params=BIG_PARAMS,
+        name="adam",
+    )(core, mine, other, *uvqk, *out)
 
 
 def per_device(
@@ -636,30 +742,36 @@
     slots = peers * capacity
     total_tokens = float(time_buckets.size * devices)
     half = lax.axis_index(axes[0]).reshape(1)
+    core = lax.axis_index(axes[-1]).reshape(1)
 
     def exchange(values):
         return lax.all_to_all(values.reshape(peers, capacity, D), near, 0, 0, tiled=True).reshape(slots, D)
 
     table_low = table.astype(BF16)
-    table_far = lax.ppermute(table_low, axes[0], SWAP)
     slotc, slotr, ids = request_slots(half, row_owner, item_rows, devices, capacity)
     ids = lax.all_to_all(ids, near, 0, 0, tiled=True)
-    ids_own = ids[:, :capacity]
-    ids_far = ids[:, capacity:]
-    serve_own = serve(ids_own.reshape(slots, 1), table_low)
+    ids_own = ids[:, 0, :capacity]
+    ids_far = ids[:, 0, capacity:]
+    outer = lax.ppermute(table_low, axes[:2], [(0, 2), (3, 1)])
+    inner = lax.ppermute(table_low, axes[:2], [(1, 3), (2, 0)])
+    serve_own = serve(ids, [table_low], 0)
     got_own = exchange(serve_own)
-    serve_far = serve(ids_far.reshape(slots, 1), table_far)
+    serve_far = serve(ids, [outer, inner], capacity)
     got_far = exchange(serve_far)
     own = place(slotc, got_own)
 
     w_low = (0.5 * uvqk_weight).astype(BF16)
     wo_low = out_weight.astype(BF16)
-    send_far, row_grads, n1, dp, dout, dbias, stats, dgain = step(
-        lengths, own, got_far, slotc, slotr, w_low, wo_low, gains, time_bias, time_buckets, total_tokens
+    send_far, row_grads, keep, give, dbias, stats, dgain = step(
+        lengths, core, own, got_far, slotc, slotr, w_low, wo_low, gains, time_bias, time_buckets, total_tokens
     )
     back_far = exchange(send_far)
     send_own = spread(slotr, row_grads, slots)
-    dense = jnp.concatenate([dout, weight_grad(n1, dp)], 0)
+    got = swap(give, axes[-1])
+    order = axes[-3:-1] + axes[-4::-1]
+    unit = 8 << len(order)
+    pad = -keep.shape[0] % unit
+    part = sum_chips(*[jnp.pad(v, ((0, pad), (0, 0))) for v in (keep, got)], order, axes[-1])
     sums_far = row_sums(ids_far.reshape(1, slots), back_far, rows)
     sums_far = lax.ppermute(sums_far, axes[0], SWAP)
     back_own = exchange(send_own)
@@ -677,8 +789,9 @@
     small_hi = lax.reduce_precision(small, 8, 7)
     small_lo = (small - small_hi).astype(BF16)
     small_hi = small_hi.astype(BF16)
-    part = sum_chips(dense, axes)
-    dense, small = share_chips(part, jnp.concatenate([small_hi, small_lo], 0), axes)
+    mine, small = share_chips(part, jnp.concatenate([small_hi, small_lo], 0), order, axes[-1])
+    mine = mine[: keep.shape[0]]
+    other = swap(mine, axes[-1])
     small = jnp.sum(small.astype(F32), 0)
     small = (small[:4] + small[4:]).reshape(-1)
     sum_bias = small[: H * NB].reshape(H, NB)
@@ -687,12 +800,9 @@
     summary = jnp.stack([sums[0], sums[1], sums[3]])
     attention_rms = sums[2:3]
 
-    sum_out = dense[:D].astype(F32)
-    sum_uvqk = jnp.concatenate([dense[i * D : i * D + D] for i in range(1, 5)], 1).astype(F32)
-    uvqk_step, uvqk_m_new, uvqk_v_new = adam_update(
-        uvqk_weight, sum_uvqk, uvqk_m, uvqk_v, WEIGHT_DECAY
+    uvqk_step, uvqk_m_new, uvqk_v_new, out_step, out_m_new, out_v_new = adam(
+        core, mine, other, (uvqk_weight, uvqk_m, uvqk_v), (out_weight, out_m, out_v)
     )
-    out_step, out_m_new, out_v_new = adam_update(out_weight, sum_out, out_m, out_v, WEIGHT_DECAY)
     bias_step, bias_m_new, bias_v_new = adam_update(time_bias, sum_bias, bias_m, bias_v, 0.0)
     gain_step, gain_m_new, gain_v_new = adam_update(gains, sum_gains, gain_m, gain_v, 0.0)
     return (

time: 344 us -> 310 us (0.901)
  waiting for transfers between devices: 155 us -> 130 us
  local copies, waits for them, and re-layouts: 18.7 us -> 9.28 us
    ppermute x1, waiting for transfers between devices: 56.4 us -> 26.9 us  [per_device(): sums_far = lax.ppermute(sums_far, axes[0], SWAP)]
    ppermute x7 -> x12, waiting for transfers between devices: 75.1 us -> 86.7 us  [the longest x1 33.3 us: per_device(): inner = lax.ppermute(table_low, axes[:2], [(1, 3), (2, 0)])]
    ppermute x7 -> x12, starting transfers between devices: 10.2 us -> 20.6 us  [the longest x6 7.42 us: swap(): return lax.ppermute(values, axis, SWAP)]
    mul x4 -> x2, other arithmetic: 8.79 us -> 1.24 us  [adam_update(): -LEARN_RATE]
    another operation x0 -> x8, other arithmetic: none -> 7 us  [join(): jnp.stack([jnp.where(first, values, got), jnp.where(first, got, values)])]
    all_to_all x4, waiting for transfers between devices: 19 us -> 12.2 us  [exchange(): lax.all_to_all(values.reshape(peers, capacity, D), near, 0, 0, tiled=True)]
    all_to_all x1 -> x0, starting transfers between devices: 5.88 us -> none  [share_chips(): lax.all_to_all(jnp.broadcast_to(packed, (count,) + packed.shape[1:]), chi...]
    reshape x5 -> x0, local copies, waits for them, and re-layouts: 5.87 us -> none  [the longest x1 1.55 us: per_device(): serve_own = serve(ids_own.reshape(slots, 1), table_low)]
  transfers between devices with their start and end apart: 15 -> 19, of which waited for: 9 -> 9; matrix products, arithmetic and copies ran while one was open for 6% -> 9% of each run, Pallas kernels for 9% -> 5%
where the time goes in v3:
time: 310 us; the launch traced here: 309 us
  waiting for transfers between devices  130 us (42%)
  Pallas kernels  96.4 us (31%)
  starting transfers between devices  46.9 us (15%)
  other arithmetic  24.7 us (8%)
  local copies, waits for them, and re-layouts  9.28 us (3%)
    pallas_call x1, Pallas kernels, step(): pl.pallas_call(functools.partial(step_kernel, total_tokens), out_shape=ou...  59.8 us
    ppermute x1, waiting for transfers between devices, per_device(): inner = lax.ppermute(table_low, axes[:2], [(1, 3), (2, 0)])  33.3 us
    ppermute x4, waiting for transfers between devices, turn(): return lax.ppermute(values, axes, pairs)  29.5 us
    ppermute x1, waiting for transfers between devices, per_device(): sums_far = lax.ppermute(sums_far, axes[0], SWAP)  26.9 us
    ppermute x6, waiting for transfers between devices, swap(): return lax.ppermute(values, axis, SWAP)  23.9 us
    all_to_all x4, starting transfers between devices, exchange(): lax.all_to_all(values.reshape(peers, capacity, D), near, 0, 0, tiled=True)  17.1 us
    pallas_call x1, Pallas kernels, adam(): pl.pallas_call(adam_kernel, out_shape=[sds(*shape, dtype=F32) for shape i...  14.2 us
    all_to_all x4, waiting for transfers between devices, exchange(): lax.all_to_all(values.reshape(peers, capacity, D), near, 0, 0, tiled=True)  12.2 us
  transfers between devices with their start and end apart: 19, of which 9 were waited for; matrix products, arithmetic and copies ran while one was open for 9% of the time, Pallas kernels for 5%

profile of v3, /device:TPU:0, one launch (start us, length us, event | category | flops | bytes accessed | tf_op | source)
XLA Modules:
  0.0 309.0 jit_solution(10765607062999872342)
XLA Ops:
  0.7 3.2 %request_slots.1 = (s32[1536,1]{1,0:T(8,128)}, s32[1,1536]{1,0:T(1,128)}, s32[16,1,192]{2,1,0:T(1,128)}) custom-call(s32[1]{0:T(128)} %bitcast.half_ref, s32[1,1536]{1,0:T(1,128)} %bitcast.84, s32[12,128]{1,0:T(8,128)} %bitcast.83), custom_call_target="tpu_custom_call" | custom-call | tf_op jit(solution)/shard_map/request_slots/pallas_call | solution.py:120
  3.8 6.3 %all-to-all-start = ((s32[16,1,192]{2,1,0:T(1,128)}), s32[16,1,192]{2,1,0:T(1,128)S(1)}, u32[]{:S(2)}, u32[]{:S(2)}) async-start(s32[16,1,192]{2,1,0:T(1,128)} %get-tuple-element.34), calls=%async_computation | async-start | bytes 32768 | tf_op jit(solution)/shard_map/all_to_all | solution.py:752
  11.7 4.0 %all-to-all-done.ids_ref = s32[16,1,192]{2,1,0:T(1,128)S(1)} async-done(((s32[16,1,192]{2,1,0:T(1,128)}), s32[16,1,192]{2,1,0:T(1,128)S(1)}, u32[]{:S(2)}, u32[]{:S(2)}) %all-to-all-start) | async-done | bytes 12320 | tf_op jit(solution)/shard_map/all_to_all | solution.py:752
  15.7 3.1 serve.2
  18.8 3.7 %all-to-all-start.1 = ((bf16[16,96,512]{2,1,0:T(8,128)(2,1)}), bf16[16,96,512]{2,1,0:T(8,128)(2,1)S(1)}, u32[]{:S(2)}, u32[]{:S(2)}) async-start(bf16[16,96,512]{2,1,0:T(8,128)(2,1)} %bitcast.4), calls=%async_computation.1 | async-start | bytes 3145728 | tf_op jit(solution)/shard_map/all_to_all | solution.py:748
  23.8 5.5 %collective-permute-start = (bf16[784,512]{1,0:T(8,128)(2,1)S(1)}, bf16[784,512]{1,0:T(8,128)(2,1)S(1)}, u32[]{:S(2)}, u32[]{:S(2)}) collective-permute-start(bf16[784,512]{1,0:T(8,128)(2,1)S(1)} %convert_element_type.112.refs_0_), channel_id=1, source_target_pairs={{0,16},{24,8},{1,17},{25,9},{2,18},{26,10},{3,19},{27,11},{4,20},{... | collective-permute-start | bytes 2408456 | tf_op jit(solution)/shard_map/ppermute | solution.py:755
  29.3 33.3 %collective-permute-done.1.refs_1_ = bf16[784,512]{1,0:T(8,128)(2,1)S(1)} collective-permute-done((bf16[784,512]{1,0:T(8,128)(2,1)S(1)}, bf16[784,512]{1,0:T(8,128)(2,1)S(1)}, u32[]{:S(2)}, u32[]{:S(2)}) %collective-permute-start.1) | collective-permute-done | bytes 802848 | tf_op jit(solution)/shard_map/ppermute | solution.py:756
  62.6 3.1 %serve.3 = bf16[1536,512]{1,0:T(8,128)(2,1)} custom-call(s32[16,1,192]{2,1,0:T(1,128)S(1)} %all-to-all-done.ids_ref, bf16[784,512]{1,0:T(8,128)(2,1)S(1)} %collective-permute-done.refs_0_, bf16[784,512]{1,0:T(8,128)(2,1)S(1)} %collective-permute-done.1.refs_1_), custom_call_target="tpu_custom_call" | custom-call | tf_op jit(solution)/shard_map/serve/pallas_call | solution.py:154
  65.7 4.7 %all-to-all-start.2 = ((bf16[16,96,512]{2,1,0:T(8,128)(2,1)}), bf16[16,96,512]{2,1,0:T(8,128)(2,1)}, u32[]{:S(2)}, u32[]{:S(2)}) async-start(bf16[16,96,512]{2,1,0:T(8,128)(2,1)} %bitcast.6), calls=%async_computation.2 | async-start | bytes 3145728 | tf_op jit(solution)/shard_map/all_to_all | solution.py:748
  73.0 4.1 %multiply_convert_fusion.w_ref = bf16[512,2048]{1,0:T(8,128)(2,1)} fusion(f32[512,2048]{1,0:T(8,128)} %refs_0_.1), kind=kLoop, calls=%fused_computation | loop fusion | flops 2097152 | bytes 6291456 | tf_op jit(solution)/shard_map/convert_element_type | solution.py:763
  80.9 12.2 %all-to-all-done.2 = bf16[16,96,512]{2,1,0:T(8,128)(2,1)} async-done(((bf16[16,96,512]{2,1,0:T(8,128)(2,1)}), bf16[16,96,512]{2,1,0:T(8,128)(2,1)}, u32[]{:S(2)}, u32[]{:S(2)}) %all-to-all-start.2) | async-done | bytes 1572896 | tf_op jit(solution)/shard_map/all_to_all | solution.py:748
  93.1 59.8 %step.1 = (bf16[1536,512]{1,0:T(8,128)(2,1)}, bf16[1536,512]{1,0:T(8,128)(2,1)}, bf16[1280,512]{1,0:T(8,128)(2,1)}, bf16[1280,512]{1,0:T(8,128)(2,1)}, f32[8,32]...) custom-call(s32[1]{0:T(128)S(6)} %copy.37.len_ref, s32[1]{0:T(128)} %bitcast.3.core_ref, bf16[1536,512]{1,0:T(8,128)(2,1)} %copy-done.4, ...), custom_call_target="tpu_custom_call" | custom-call | flops 49999998976 | bytes 15000000 | tf_op jit(solution)/shard_map/step/pallas_call | solution.py:498
  153.0 3.9 %all-to-all-start.4 = ((bf16[16,96,512]{2,1,0:T(8,128)(2,1)}), bf16[16,96,512]{2,1,0:T(8,128)(2,1)S(1)}, u32[]{:S(2)}, u32[]{:S(2)}) async-start(bf16[16,96,512]{2,1,0:T(8,128)(2,1)} %bitcast.75), calls=%async_computation.4 | async-start | bytes 3145728 | tf_op jit(solution)/shard_map/all_to_all | solution.py:748
  161.4 22.8 %collective-permute-done.4 = bf16[2,320,512]{2,1,0:T(8,128)(2,1)} collective-permute-done((bf16[2,320,512]{2,1,0:T(8,128)(2,1)}, bf16[2,320,512]{2,1,0:T(8,128)(2,1)}, u32[]{:S(2)}, u32[]{:S(2)}) %collective-permute-start.4) | collective-permute-done | bytes 655392 | tf_op jit(solution)/shard_map/ppermute | solution.py:604
  187.2 6.3 %collective-permute-done.5 = bf16[320,512]{1,0:T(8,128)(2,1)} collective-permute-done((bf16[320,512]{1,0:T(8,128)(2,1)}, bf16[320,512]{1,0:T(8,128)(2,1)}, u32[]{:S(2)}, u32[]{:S(2)}) %collective-permute-start.5) | collective-permute-done | bytes 327712 | tf_op jit(solution)/shard_map/ppermute | solution.py:604
  196.9 3.4 %spread.1 = bf16[1536,512]{1,0:T(8,128)(2,1)S(1)} custom-call(s32[1,1536]{1,0:T(1,128)S(1)} %copy-done.7, bf16[1536,512]{1,0:T(8,128)(2,1)S(1)} %copy-done.3), custom_call_target="tpu_custom_call" | custom-call | tf_op jit(solution)/shard_map/spread/pallas_call | solution.py:543
  202.8 3.2 %collective-permute-start.7 = (bf16[80,512]{1,0:T(8,128)(2,1)S(1)}, bf16[80,512]{1,0:T(8,128)(2,1)S(1)}, u32[]{:S(2)}, u32[]{:S(2)}) collective-permute-start(bf16[80,512]{1,0:T(8,128)(2,1)S(1)} %dynamic-slice_bitcast_fusion.1), channel_id=1, source_target_pairs={{0,16},{16,0},{1,17},{17,1},{2,18},{18,2},{3,19},{19,3},{4,20},{20... | collective-permute-start | bytes 245768 | tf_op jit(solution)/shard_map/ppermute | solution.py:591
  206.0 4.8 %all-to-all-start.3 = ((bf16[16,96,512]{2,1,0:T(8,128)(2,1)}), bf16[16,96,512]{2,1,0:T(8,128)(2,1)S(1)}, u32[]{:S(2)}, u32[]{:S(2)}) async-start(bf16[16,96,512]{2,1,0:T(8,128)(2,1)} %bitcast.69), calls=%async_computation.3 | async-start | bytes 3145728 | tf_op jit(solution)/shard_map/all_to_all | solution.py:748
  211.9 19.2 %collective-permute-done.9 = bf16[88,512]{1,0:T(8,128)(2,1)S(1)} collective-permute-done((bf16[88,512]{1,0:T(8,128)(2,1)S(1)}, bf16[88,512]{1,0:T(8,128)(2,1)S(1)}, u32[]{:S(2)}, u32[]{:S(2)}) %collective-permute-start.9) | collective-permute-done | bytes 90144 | tf_op jit(solution)/shard_map/ppermute | solution.py:591
  233.0 4.7 %collective-permute-done.10 = bf16[2,88,512]{2,1,0:T(8,128)(2,1)} collective-permute-done((bf16[2,88,512]{2,1,0:T(8,128)(2,1)S(1)}, bf16[2,88,512]{2,1,0:T(8,128)(2,1)}, u32[]{:S(2)}, u32[]{:S(2)}) %collective-permute-start.10) | collective-permute-done | bytes 180256 | tf_op jit(solution)/shard_map/ppermute | solution.py:591
  244.5 2.8 collective-permute-start.2
  253.4 26.9 %collective-permute-done.2.far_ref = bf16[784,512]{1,0:T(8,128)(2,1)} collective-permute-done((bf16[784,512]{1,0:T(8,128)(2,1)}, bf16[784,512]{1,0:T(8,128)(2,1)}, u32[]{:S(2)}, u32[]{:S(2)}) %collective-permute-start.2) | collective-permute-done | bytes 802848 | tf_op jit(solution)/shard_map/ppermute | solution.py:776
  281.4 4.6 %update_rows.1 = (f32[784,512]{1,0:T(8,128)}, f32[784,1]{1,0:T(8,128)S(1)}) custom-call(s32[1,1536]{1,0:T(1,128)S(1)} %reshape_squeeze.6.ids_ref, bf16[1536,512]{1,0:T(8,128)(2,1)S(1)} %bitcast.67, bf16[784,512]{1,0:T(8,128)(2,1)} %collective-permute-done.2.far_ref, f32[784,512]{1,0:T(8,128)S(1)} %copy-done, f32[784,1]{1,0:T(8,128)S(1)} %copy-done.2), custom_call_target="tpu_custom_call" | custom-call | tf_op jit(solution)/shard_map/update_rows/pallas_call | solution.py:577
  294.6 14.2 %adam.1 = (f32[512,2048]{1,0:T(8,128)}, f32[512,2048]{1,0:T(8,128)}, f32[512,2048]{1,0:T(8,128)}, f32[512,512]{1,0:T(8,128)}, f32[512,512]{1,0:T(8,128)}, /*index=5*/f32[512,512]{1,0:T(8,128)}) custom-call(s32[1]{0:T(128)} %bitcast.3.core_ref, bf16[1280,512]{1,0:T(8,128)(2,1)} %bitcast.74, bf16[1280,512]{1,0:T(8,128)(2,1)} %collective-permute-done.13.other_ref, ...), custom_call_target="tpu_custom_call" | custom-call | tf_op jit(solution)/shard_map/adam/pallas_call | solution.py:701
  (115 shorter events, 47.1 us)
Async XLA Ops:
  3.8 11.9 %all-to-all-start = ((s32[16,1,192]{2,1,0:T(1,128)}), s32[16,1,192]{2,1,0:T(1,128)S(1)}, u32[]{:S(2)}, u32[]{:S(2)}) async-start(s32[16,1,192]{2,1,0:T(1,128)} %get-tuple-element.34), calls=%async_computation | async-start | bytes 32768 | tf_op jit(solution)/shard_map/all_to_all | solution.py:752
  18.8 47.0 %all-to-all-start.1 = ((bf16[16,96,512]{2,1,0:T(8,128)(2,1)}), bf16[16,96,512]{2,1,0:T(8,128)(2,1)S(1)}, u32[]{:S(2)}, u32[]{:S(2)}) async-start(bf16[16,96,512]{2,1,0:T(8,128)(2,1)} %bitcast.4), calls=%async_computation.1 | async-start | bytes 3145728 | tf_op jit(solution)/shard_map/all_to_all | solution.py:748
  22.5 40.1 %collective-permute-start.1 = (bf16[784,512]{1,0:T(8,128)(2,1)S(1)}, bf16[784,512]{1,0:T(8,128)(2,1)S(1)}, u32[]{:S(2)}, u32[]{:S(2)}) collective-permute-start(bf16[784,512]{1,0:T(8,128)(2,1)S(1)} %convert_element_type.112.refs_0_), channel_id=1, source_target_pairs={{8,24},{16,0},{9,25},{17,1},{10,26},{18,2},{11,27},{19,3},{12,28},... | collective-permute-start | bytes 2408456 | tf_op jit(solution)/shard_map/ppermute | solution.py:756
  23.8 38.8 %collective-permute-start = (bf16[784,512]{1,0:T(8,128)(2,1)S(1)}, bf16[784,512]{1,0:T(8,128)(2,1)S(1)}, u32[]{:S(2)}, u32[]{:S(2)}) collective-permute-start(bf16[784,512]{1,0:T(8,128)(2,1)S(1)} %convert_element_type.112.refs_0_), channel_id=1, source_target_pairs={{0,16},{24,8},{1,17},{25,9},{2,18},{26,10},{3,19},{27,11},{4,20},{... | collective-permute-start | bytes 2408456 | tf_op jit(solution)/shard_map/ppermute | solution.py:755
  65.7 6.4 %copy-start.9 = (f32[512,512]{1,0:T(8,128)S(1)}, f32[512,512]{1,0:T(8,128)}, u32[]{:S(2)}) copy-start(f32[512,512]{1,0:T(8,128)} %refs_3_.1) | copy-start | bytes 3145732
  65.7 27.3 %all-to-all-start.2 = ((bf16[16,96,512]{2,1,0:T(8,128)(2,1)}), bf16[16,96,512]{2,1,0:T(8,128)(2,1)}, u32[]{:S(2)}, u32[]{:S(2)}) async-start(bf16[16,96,512]{2,1,0:T(8,128)(2,1)} %bitcast.6), calls=%async_computation.2 | async-start | bytes 3145728 | tf_op jit(solution)/shard_map/all_to_all | solution.py:748
  152.9 3.9 %collective-permute-start.3 = (bf16[1280,512]{1,0:T(8,128)(2,1)}, bf16[1280,512]{1,0:T(8,128)(2,1)}, u32[]{:S(2)}, u32[]{:S(2)}) collective-permute-start(bf16[1280,512]{1,0:T(8,128)(2,1)} %get-tuple-element.42), channel_id=1, source_target_pairs={{0,1},{1,0},{2,3},{3,2},{4,5},{5,4},{6,7},{7,6},{8,9},{9,8},{10,11... | collective-permute-start | bytes 3932168 | tf_op jit(solution)/shard_map/ppermute | solution.py:591
  153.0 53.0 %all-to-all-start.4 = ((bf16[16,96,512]{2,1,0:T(8,128)(2,1)}), bf16[16,96,512]{2,1,0:T(8,128)(2,1)S(1)}, u32[]{:S(2)}, u32[]{:S(2)}) async-start(bf16[16,96,512]{2,1,0:T(8,128)(2,1)} %bitcast.75), calls=%async_computation.4 | async-start | bytes 3145728 | tf_op jit(solution)/shard_map/all_to_all | solution.py:748
  159.6 37.3 %copy-start.3 = (bf16[1536,512]{1,0:T(8,128)(2,1)S(1)}, bf16[1536,512]{1,0:T(8,128)(2,1)}, u32[]{:S(2)}) copy-start(bf16[1536,512]{1,0:T(8,128)(2,1)} %get-tuple-element.37.rows_ref) | copy-start | bytes 4718596
  159.6 37.3 %copy-start.7 = (s32[1,1536]{1,0:T(1,128)S(1)}, s32[1,1536]{1,0:T(1,128)}, u32[]{:S(2)}) copy-start(s32[1,1536]{1,0:T(1,128)} %get-tuple-element.35.slotr_ref) | copy-start | bytes 18436
  159.6 24.6 %collective-permute-start.4 = (bf16[2,320,512]{2,1,0:T(8,128)(2,1)}, bf16[2,320,512]{2,1,0:T(8,128)(2,1)}, u32[]{:S(2)}, u32[]{:S(2)}) collective-permute-start(bf16[2,320,512]{2,1,0:T(8,128)(2,1)} %get-tuple-element.61), channel_id=1, source_target_pairs={{0,4},{1,3},{2,6},{3,1},{4,0},{5,7},{6,2},{7,5},{8,12},{9,11},{10,... | collective-permute-start | bytes 1966088 | tf_op jit(solution)/shard_map/ppermute | solution.py:604
  186.1 7.4 %collective-permute-start.5 = (bf16[320,512]{1,0:T(8,128)(2,1)}, bf16[320,512]{1,0:T(8,128)(2,1)}, u32[]{:S(2)}, u32[]{:S(2)}) collective-permute-start(bf16[320,512]{1,0:T(8,128)(2,1)} %fusion.5), channel_id=1, source_target_pairs={{0,2},{1,5},{2,0},{3,7},{4,6},{5,1},{6,4},{7,3},{8,10},{9,13},{10,... | collective-permute-start | bytes 983048 | tf_op jit(solution)/shard_map/ppermute | solution.py:604
  195.5 6.3 %collective-permute-start.6 = (bf16[160,512]{1,0:T(8,128)(2,1)S(1)}, bf16[160,512]{1,0:T(8,128)(2,1)S(1)}, u32[]{:S(2)}, u32[]{:S(2)}) collective-permute-start(bf16[160,512]{1,0:T(8,128)(2,1)S(1)} %dynamic-slice_bitcast_fusion), channel_id=1, source_target_pairs={{0,8},{8,0},{1,9},{9,1},{2,10},{10,2},{3,11},{11,3},{4,12},{12,4},... | collective-permute-start | bytes 491528 | tf_op jit(solution)/shard_map/ppermute | solution.py:591
  201.8 9.1 %collective-permute-start.8 = (f32[4,512]{1,0:T(4,128)S(1)}, f32[4,512]{1,0:T(4,128)S(1)}, u32[]{:S(2)}, u32[]{:S(2)}) collective-permute-start(f32[4,512]{1,0:T(4,128)S(1)} %reshape.165), channel_id=1, source_target_pairs={{0,1},{1,0},{2,3},{3,2},{4,5},{5,4},{6,7},{7,6},{8,9},{9,8},{10,11... | collective-permute-start | bytes 24584 | tf_op jit(solution)/shard_map/ppermute | solution.py:788
  202.8 8.1 %collective-permute-start.7 = (bf16[80,512]{1,0:T(8,128)(2,1)S(1)}, bf16[80,512]{1,0:T(8,128)(2,1)S(1)}, u32[]{:S(2)}, u32[]{:S(2)}) collective-permute-start(bf16[80,512]{1,0:T(8,128)(2,1)S(1)} %dynamic-slice_bitcast_fusion.1), channel_id=1, source_target_pairs={{0,16},{16,0},{1,17},{17,1},{2,18},{18,2},{3,19},{19,3},{4,20},{20... | collective-permute-start | bytes 245768 | tf_op jit(solution)/shard_map/ppermute | solution.py:591
  206.0 47.5 %all-to-all-start.3 = ((bf16[16,96,512]{2,1,0:T(8,128)(2,1)}), bf16[16,96,512]{2,1,0:T(8,128)(2,1)S(1)}, u32[]{:S(2)}, u32[]{:S(2)}) async-start(bf16[16,96,512]{2,1,0:T(8,128)(2,1)} %bitcast.69), calls=%async_computation.3 | async-start | bytes 3145728 | tf_op jit(solution)/shard_map/all_to_all | solution.py:748
  210.9 20.2 %collective-permute-start.9 = (bf16[88,512]{1,0:T(8,128)(2,1)S(1)}, bf16[88,512]{1,0:T(8,128)(2,1)S(1)}, u32[]{:S(2)}, u32[]{:S(2)}) collective-permute-start(bf16[88,512]{1,0:T(8,128)(2,1)S(1)} %pad_maximum_fusion.4), channel_id=1, source_target_pairs={{0,16},{16,0},{1,17},{17,1},{2,18},{18,2},{3,19},{19,3},{4,20},{20... | collective-permute-start | bytes 270344 | tf_op jit(solution)/shard_map/ppermute | solution.py:591
  231.2 6.6 %collective-permute-start.10 = (bf16[2,88,512]{2,1,0:T(8,128)(2,1)S(1)}, bf16[2,88,512]{2,1,0:T(8,128)(2,1)}, u32[]{:S(2)}, u32[]{:S(2)}) collective-permute-start(bf16[2,88,512]{2,1,0:T(8,128)(2,1)S(1)} %pad_maximum_fusion.3), channel_id=1, source_target_pairs={{0,8},{8,0},{1,9},{9,1},{2,10},{10,2},{3,11},{11,3},{4,12},{12,4},... | collective-permute-start | bytes 540680 | tf_op jit(solution)/shard_map/ppermute | solution.py:591
  239.5 8.2 %collective-permute-start.11 = (bf16[4,88,512]{2,1,0:T(8,128)(2,1)}, bf16[4,88,512]{2,1,0:T(8,128)(2,1)}, u32[]{:S(2)}, u32[]{:S(2)}) collective-permute-start(bf16[4,88,512]{2,1,0:T(8,128)(2,1)} %bitcast.30), channel_id=1, source_target_pairs={{0,2},{1,5},{2,0},{3,7},{4,6},{5,1},{6,4},{7,3},{8,10},{9,13},{10,... | collective-permute-start | bytes 1081352 | tf_op jit(solution)/shard_map/ppermute | solution.py:604
  244.5 8.0 %copy-start.16 = (f32[784]{0:T(1024)S(1)}, f32[784]{0:T(1024)}, u32[]{:S(2)}) copy-start(f32[784]{0:T(1024)} %param.19) | copy-start | bytes 9412
  244.5 35.9 %copy-start = (f32[784,512]{1,0:T(8,128)S(1)}, f32[784,512]{1,0:T(8,128)}, u32[]{:S(2)}) copy-start(f32[784,512]{1,0:T(8,128)} %table_ref.1) | copy-start | bytes 4816900
  244.5 35.9 %collective-permute-start.2 = (bf16[784,512]{1,0:T(8,128)(2,1)}, bf16[784,512]{1,0:T(8,128)(2,1)}, u32[]{:S(2)}, u32[]{:S(2)}) collective-permute-start(bf16[784,512]{1,0:T(8,128)(2,1)} %row_sums.1), channel_id=1, source_target_pairs={{0,16},{16,0},{1,17},{17,1},{2,18},{18,2},{3,19},{19,3},{4,20},{20... | collective-permute-start | bytes 2408456 | tf_op jit(solution)/shard_map/ppermute | solution.py:776
  251.5 37.0 %collective-permute-start.12 = (bf16[2,4,88,512]{3,2,1,0:T(8,128)(2,1)}, bf16[2,4,88,512]{3,2,1,0:T(8,128)(2,1)}, u32[]{:S(2)}, u32[]{:S(2)}) collective-permute-start(bf16[2,4,88,512]{3,2,1,0:T(8,128)(2,1)} %pad_maximum_fusion.1), channel_id=1, source_target_pairs={{0,4},{1,3},{2,6},{3,1},{4,0},{5,7},{6,2},{7,5},{8,12},{9,11},{10,... | collective-permute-start | bytes 2162696 | tf_op jit(solution)/shard_map/ppermute | solution.py:604
  291.3 3.2 %collective-permute-start.13 = (bf16[1280,512]{1,0:T(8,128)(2,1)S(1)}, bf16[1280,512]{1,0:T(8,128)(2,1)}, u32[]{:S(2)}, u32[]{:S(2)}) collective-permute-start(bf16[1280,512]{1,0:T(8,128)(2,1)S(1)} %bitcast.73), channel_id=1, source_target_pairs={{0,1},{1,0},{2,3},{3,2},{4,5},{5,4},{6,7},{7,6},{8,9},{9,8},{10,11... | collective-permute-start | bytes 3932168 | tf_op jit(solution)/shard_map/ppermute | solution.py:591
  (18 other events, 54.9 us)

commit v4 on v3

--- a/solution.py
+++ b/solution.py
@@ -184,15 +184,13 @@
     own_ref,
     far_ref,
     slotc_ref,
-    slotr_ref,
-    w_ref,
-    wo_ref,
+    w_hbm,
+    wo_hbm,
     gains_ref,
     tb_ref,
     bucketr_ref,
     bucketc_ref,
-    out_ref,
-    rows_ref,
+    rows_out,
     keep_ref,
     give_ref,
     dbias_ref,
@@ -220,6 +218,10 @@
     kt,
     vt,
     dkb,
+    w_ref,
+    wo_ref,
+    rows_ref,
+    sems,
 ):
     seq_len = n1_ref.shape[0]
     requests = rows_ref.shape[0]
@@ -228,6 +230,11 @@
     blocks = seq_len // BLK
     length = len_ref[0]
     inv_len = 1.0 / (jnp.zeros((1, 1), jnp.int32) + length).astype(F32)
+    copy_w = pltpu.make_async_copy(w_hbm, w_ref, sems.at[0])
+    copy_wo = pltpu.make_async_copy(wo_hbm, wo_ref, sems.at[1])
+    copy_rows = pltpu.make_async_copy(rows_ref, rows_out, sems.at[2])
+    copy_w.start()
+    copy_wo.start()
 
     def fetch(block):
         hits = one_hot(slotc_ref[at(block), :] - slots == iota((BLK, slots), 1))
@@ -242,6 +249,12 @@
     lane_of = iota((H, D), 1)
     terms = dot_tn(tb_hi, one_hot(lane_of == spot)) + dot_tn(tb_lo, one_hot(lane_of == spot + 1))
     terms = terms.astype(BF16)
+
+    def fetch_neg(block, _):
+        neg[at(block), :] = fetch(blocks + block).astype(BF16)
+        return 0
+
+    lax.fori_loop(0, negs // BLK, fetch_neg, 0)
 
     def project(block, sum_x):
         rows = at(block)
@@ -269,13 +282,13 @@
                 k_ref[rows, :] = act.astype(BF16)
         return sum_x + jnp.sum(jnp.where(live, root_mean(mean_sq), 0.0), keepdims=True)
 
+    copy_w.wait()
+    copy_wo.wait()
     sum_x = lax.fori_loop(0, blocks, project, jnp.zeros((1, 1), F32))
 
-    def fetch_neg(block, _):
-        neg[at(block), :] = fetch(blocks + block).astype(BF16)
-        return 0
-
-    lax.fori_loop(0, negs // BLK, fetch_neg, 0)
+    def tile_rows(kb, qb):
+        start = (kb * blocks - kb * (kb - 1) // 2 + qb - kb) * BLK
+        return slice(start, start + BLK)
 
     lower = iota((BLK, BLK), 0) >= iota((BLK, BLK), 1)
     lane = iota((1, 128), 1)
@@ -303,10 +316,13 @@
                         score = jnp.where(lower, score, 0.0)
                         deriv = jnp.where(lower, deriv, 0.0)
                     low = score.astype(BF16)
-                    tile = qb * (qb + 1) // 2 + kb
-                    abuf[2 * pair + hh, tile] = low
-                    sbuf[2 * pair + hh, tile] = deriv.astype(BF16)
-                    total = total + dot(low, vals[hh][span])
+                    spot = tile_rows(kb, qb)
+                    abuf[2 * pair + hh, spot, :] = low
+                    sbuf[2 * pair + hh, spot, :] = deriv.astype(BF16)
+            for hh in range(2):
+                for kb in range(qb + 1):
+                    span = slice(kb * BLK, (kb + 1) * BLK)
+                    total = total + dot(abuf[2 * pair + hh, tile_rows(kb, qb), :], vals[hh][span])
             att[qs, lanes] = total * inv_len
         return 0
 
@@ -401,8 +417,6 @@
             qt[hh, 0:64, :] = qtr[hh * 64 : hh * 64 + 64, :]
             qt[hh, 64:80, :] = ones
             dt[hh] = dtr[hh * 64 : hh * 64 + 64, :]
-        kt[...] = jnp.zeros_like(kt)
-        vt[...] = jnp.zeros_like(vt)
         dql = pl.ds(pl.multiple_of(2 * D + pair * 128, 128), 128)
         for qb in range(blocks):
             qs = slice(qb * BLK, (qb + 1) * BLK)
@@ -410,14 +424,20 @@
             for hh in range(2):
                 for kb in range(qb + 1):
                     span = slice(kb * BLK, (kb + 1) * BLK)
-                    tile = qb * (qb + 1) // 2 + kb
-                    slope = sbuf[2 * pair + hh, tile].astype(F32)
+                    spot = tile_rows(kb, qb)
+                    slope = sbuf[2 * pair + hh, spot, :].astype(F32)
                     ds = (dot_nt(grads[qs], vals[hh][span]) * slope).astype(BF16)
-                    dq = dq + dot(ds, keys[hh][span])
-                    kt[hh, :, span] += dot(qt[hh, :, qs], ds)
-                    vt[hh, :, span] += dot(dt[hh, :, qs], abuf[2 * pair + hh, tile])
+                    sbuf[2 * pair + hh, spot, :] = ds
+                for kb in range(qb + 1):
+                    dq = dq + dot(sbuf[2 * pair + hh, tile_rows(kb, qb), :], keys[hh][kb * BLK : (kb + 1) * BLK])
             dq = dq * (0.5 * (D // H) ** -0.5)
             dp_ref[qs, dql] = (dq * deriv_ref[qs, dql].astype(F32)).astype(BF16)
+        for hh in range(2):
+            for kb in range(blocks):
+                span = slice(kb * BLK, (kb + 1) * BLK)
+                column = slice(tile_rows(kb, kb).start, tile_rows(kb, blocks - 1).stop)
+                kt[hh, :, span] = dot(qt[hh, :, kb * BLK :], sbuf[2 * pair + hh, column, :])
+                vt[hh, :, span] = dot(dt[hh, :, kb * BLK :], abuf[2 * pair + hh, column, :])
         dkl = pl.ds(pl.multiple_of(3 * D + pair * 128, 128), 128)
         dvl = pl.ds(pl.multiple_of(D + pair * 128, 128), 128)
         dk = jnp.concatenate([kt[0, 0:64, :], kt[1, 0:64, :]], 0).T
@@ -449,12 +469,7 @@
     gsum = jnp.where(row == 0, dg0, 0.0) + jnp.where(row == 1, dg1, 0.0)
     dgain_ref[...] = gsum + jnp.where(row == 2, dg2, 0.0)
 
-    def put(block, _):
-        slot = slots + block * BLK + iota((BLK, 1), 0)
-        out_ref[at(block), :] = dot(one_hot(slotr_ref[...] == slot), rows_ref[...]).astype(BF16)
-        return 0
-
-    lax.fori_loop(0, slots // BLK, put, 0)
+    copy_rows.start()
 
     half = keep_ref.shape[0] // BLK
 
@@ -476,18 +491,18 @@
         for part in range(4):
             grad = dot(turned, dp_ref[:, part * D : (part + 1) * D])
             write((part + 1) * (D // BLK) + side, grad.astype(BF16))
-
-
-def step(length, core, own, far, slotc, slotr, w, wo, gains, time_bias, buckets, total_tokens):
+    copy_rows.wait()
+
+
+def step(length, core, own, far, slotc, w, wo, gains, time_bias, buckets, total_tokens):
     seq_len = buckets.shape[1]
     requests = slotc.shape[0]
     negs = requests - seq_len
-    slots = far.shape[0]
+    hbm = pl.BlockSpec(memory_space=pl.ANY)
     vmem = pl.BlockSpec(memory_space=pltpu.VMEM)
     blocks = seq_len // BLK
     tiles = blocks * (blocks + 1) // 2
     outs = (
-        sds(slots, D),
         sds(requests, D),
         sds(5 * D // 2, D),
         sds(5 * D // 2, D),
@@ -498,8 +513,8 @@
     return pl.pallas_call(
         functools.partial(step_kernel, total_tokens),
         out_shape=outs,
-        in_specs=[pl.BlockSpec(memory_space=pltpu.SMEM)] * 2 + [vmem] * 10,
-        out_specs=[vmem] * len(outs),
+        in_specs=[pl.BlockSpec(memory_space=pltpu.SMEM)] * 2 + [vmem] * 3 + [hbm] * 2 + [vmem] * 4,
+        out_specs=[hbm] + [vmem] * (len(outs) - 1),
         scratch_shapes=[
             pltpu.VMEM((seq_len, D), BF16),
             pltpu.VMEM((seq_len, 4 * D), BF16),
@@ -513,8 +528,8 @@
             pltpu.VMEM((seq_len, D), BF16),
             pltpu.VMEM((seq_len, D), BF16),
             pltpu.VMEM((seq_len, D), BF16),
-            pltpu.VMEM((H, tiles, BLK, BLK), BF16),
-            pltpu.VMEM((H, tiles, BLK, BLK), BF16),
+            pltpu.VMEM((H, tiles * BLK, BLK), BF16),
+            pltpu.VMEM((H, tiles * BLK, BLK), BF16),
             pltpu.VMEM((negs, D), F32),
             pltpu.VMEM((D, D), F32),
             pltpu.VMEM((8, D), F32),
@@ -523,27 +538,35 @@
             pltpu.VMEM((2, 80, seq_len), F32),
             pltpu.VMEM((2, 64, seq_len), F32),
             pltpu.VMEM((H, seq_len), F32),
+            pltpu.VMEM(w.shape, BF16),
+            pltpu.VMEM(wo.shape, BF16),
+            pltpu.VMEM((requests, D), BF16),
+            pltpu.SemaphoreType.DMA((3,)),
         ],
         compiler_params=BIG_PARAMS,
         cost_estimate=pl.CostEstimate(flops=50_000_000_000, bytes_accessed=15_000_000, transcendentals=0),
         name="step",
-    )(length, core, own, far, slotc, slotr, w, wo, gains, time_bias, buckets, buckets.reshape(seq_len, 1))
-
-
-def spread_kernel(slotr_ref, rows_ref, out_ref):
+    )(length, core, own, far, slotc, w, wo, gains, time_bias, buckets, buckets.reshape(seq_len, 1))
+
+
+def spread_kernel(slotr_ref, rows_ref, far_ref, own_ref):
+    slots = far_ref.shape[0]
+
     def put(block, _):
         slot = block * BLK + iota((BLK, 1), 0)
-        out_ref[at(block), :] = dot(one_hot(slotr_ref[...] == slot), rows_ref[...]).astype(BF16)
+        far_ref[at(block), :] = dot(one_hot(slotr_ref[...] - slots == slot), rows_ref[...]).astype(BF16)
+        own_ref[at(block), :] = dot(one_hot(slotr_ref[...] == slot), rows_ref[...]).astype(BF16)
         return 0
 
-    lax.fori_loop(0, out_ref.shape[0] // BLK, put, 0)
+    lax.fori_loop(0, slots // BLK, put, 0)
 
 
 def spread(slotr, rows, slots):
     return pl.pallas_call(
         spread_kernel,
-        out_shape=sds(slots, D),
+        out_shape=(sds(slots, D), sds(slots, D)),
         compiler_params=PARAMS,
+        cost_estimate=pl.CostEstimate(flops=5_000_000_000, bytes_accessed=6_000_000, transcendentals=0),
         name="spread",
     )(slotr, rows)
 
@@ -762,11 +785,11 @@
 
     w_low = (0.5 * uvqk_weight).astype(BF16)
     wo_low = out_weight.astype(BF16)
-    send_far, row_grads, keep, give, dbias, stats, dgain = step(
-        lengths, core, own, got_far, slotc, slotr, w_low, wo_low, gains, time_bias, time_buckets, total_tokens
+    row_grads, keep, give, dbias, stats, dgain = step(
+        lengths, core, own, got_far, slotc, w_low, wo_low, gains, time_bias, time_buckets, total_tokens
     )
+    send_far, send_own = spread(slotr, row_grads, slots)
     back_far = exchange(send_far)
-    send_own = spread(slotr, row_grads, slots)
     got = swap(give, axes[-1])
     order = axes[-3:-1] + axes[-4::-1]
     unit = 8 << len(order)

time: 310 us -> 305 us (0.984)
  Pallas kernels: 96.4 us -> 89.2 us
  waiting for transfers between devices: 130 us -> 134 us
    pallas_call x1, Pallas kernels: 59.8 us -> 49.5 us  [step(): pl.pallas_call(functools.partial(step_kernel, total_tokens), out_shape=ou...]
    ppermute x6, waiting for transfers between devices: 23.9 us -> 28.5 us  [swap(): return lax.ppermute(values, axis, SWAP)]
    pallas_call x1, Pallas kernels: 3.43 us -> 6.6 us  [spread(): pl.pallas_call(spread_kernel, out_shape=(sds(slots, D), sds(slots, D)), c...]
    unnamed x47 -> x43, local copies, waits for them, and re-layouts: 5.94 us -> 6.61 us
  transfers between devices with their start and end apart: 19 -> 19, of which waited for: 9 -> 10; matrix products, arithmetic and copies ran while one was open for 9% -> 8% of each run, Pallas kernels for 5% -> 6%
where the time goes in v4:
time: 305 us; the launch traced here: 304 us
  waiting for transfers between devices  134 us (44%)
  Pallas kernels  89.2 us (29%)
  starting transfers between devices  47.6 us (16%)
  other arithmetic  22 us (7%)
  local copies, waits for them, and re-layouts  9.95 us (3%)
    pallas_call x1, Pallas kernels, step(): pl.pallas_call(functools.partial(step_kernel, total_tokens), out_shape=ou...  49.5 us
    ppermute x1, waiting for transfers between devices, per_device(): inner = lax.ppermute(table_low, axes[:2], [(1, 3), (2, 0)])  33.3 us
    ppermute x4, waiting for transfers between devices, turn(): return lax.ppermute(values, axes, pairs)  28.8 us
    ppermute x6, waiting for transfers between devices, swap(): return lax.ppermute(values, axis, SWAP)  28.5 us
    ppermute x1, waiting for transfers between devices, per_device(): sums_far = lax.ppermute(sums_far, axes[0], SWAP)  27 us
    all_to_all x4, starting transfers between devices, exchange(): lax.all_to_all(values.reshape(peers, capacity, D), near, 0, 0, tiled=True)  18.5 us
    pallas_call x1, Pallas kernels, adam(): pl.pallas_call(adam_kernel, out_shape=[sds(*shape, dtype=F32) for shape i...  14.2 us
    all_to_all x4, waiting for transfers between devices, exchange(): lax.all_to_all(values.reshape(peers, capacity, D), near, 0, 0, tiled=True)  12.2 us
  transfers between devices with their start and end apart: 19, of which 10 were waited for; matrix products, arithmetic and copies ran while one was open for 8% of the time, Pallas kernels for 6%

profile of v4, /device:TPU:0, one launch (start us, length us, event | category | flops | bytes accessed | tf_op | source)
XLA Modules:
  0.0 304.5 jit_solution(15786273564847065924)
XLA Ops:
  0.7 3.2 %request_slots.1 = (s32[1536,1]{1,0:T(8,128)}, s32[1,1536]{1,0:T(1,128)}, s32[16,1,192]{2,1,0:T(1,128)}) custom-call(s32[1]{0:T(128)} %bitcast.half_ref, s32[1,1536]{1,0:T(1,128)} %bitcast.83, s32[12,128]{1,0:T(8,128)} %bitcast.82), custom_call_target="tpu_custom_call" | custom-call | tf_op jit(solution)/shard_map/request_slots/pallas_call | solution.py:120
  3.8 6.3 %all-to-all-start = ((s32[16,1,192]{2,1,0:T(1,128)}), s32[16,1,192]{2,1,0:T(1,128)S(1)}, u32[]{:S(2)}, u32[]{:S(2)}) async-start(s32[16,1,192]{2,1,0:T(1,128)} %get-tuple-element.35), calls=%async_computation | async-start | bytes 32768 | tf_op jit(solution)/shard_map/all_to_all | solution.py:775
  11.7 4.0 %all-to-all-done.ids_ref = s32[16,1,192]{2,1,0:T(1,128)S(1)} async-done(((s32[16,1,192]{2,1,0:T(1,128)}), s32[16,1,192]{2,1,0:T(1,128)S(1)}, u32[]{:S(2)}, u32[]{:S(2)}) %all-to-all-start) | async-done | bytes 12320 | tf_op jit(solution)/shard_map/all_to_all | solution.py:775
  15.7 3.1 %serve.2 = bf16[1536,512]{1,0:T(8,128)(2,1)} custom-call(s32[16,1,192]{2,1,0:T(1,128)S(1)} %all-to-all-done.ids_ref, bf16[784,512]{1,0:T(8,128)(2,1)S(1)} %convert_element_type.112.refs_0_), custom_call_target="tpu_custom_call" | custom-call | tf_op jit(solution)/shard_map/serve/pallas_call | solution.py:154
  18.8 3.7 %all-to-all-start.1 = ((bf16[16,96,512]{2,1,0:T(8,128)(2,1)}), bf16[16,96,512]{2,1,0:T(8,128)(2,1)S(1)}, u32[]{:S(2)}, u32[]{:S(2)}) async-start(bf16[16,96,512]{2,1,0:T(8,128)(2,1)} %bitcast.4), calls=%async_computation.1 | async-start | bytes 3145728 | tf_op jit(solution)/shard_map/all_to_all | solution.py:771
  23.8 5.5 %collective-permute-start = (bf16[784,512]{1,0:T(8,128)(2,1)S(1)}, bf16[784,512]{1,0:T(8,128)(2,1)S(1)}, u32[]{:S(2)}, u32[]{:S(2)}) collective-permute-start(bf16[784,512]{1,0:T(8,128)(2,1)S(1)} %convert_element_type.112.refs_0_), channel_id=1, source_target_pairs={{0,16},{24,8},{1,17},{25,9},{2,18},{26,10},{3,19},{27,11},{4,20},{... | collective-permute-start | bytes 2408456 | tf_op jit(solution)/shard_map/ppermute | solution.py:778
  29.3 33.3 %collective-permute-done.1.refs_1_ = bf16[784,512]{1,0:T(8,128)(2,1)S(1)} collective-permute-done((bf16[784,512]{1,0:T(8,128)(2,1)S(1)}, bf16[784,512]{1,0:T(8,128)(2,1)S(1)}, u32[]{:S(2)}, u32[]{:S(2)}) %collective-permute-start.1) | collective-permute-done | bytes 802848 | tf_op jit(solution)/shard_map/ppermute | solution.py:779
  62.6 3.1 %serve.3 = bf16[1536,512]{1,0:T(8,128)(2,1)} custom-call(s32[16,1,192]{2,1,0:T(1,128)S(1)} %all-to-all-done.ids_ref, bf16[784,512]{1,0:T(8,128)(2,1)S(1)} %collective-permute-done.refs_0_, bf16[784,512]{1,0:T(8,128)(2,1)S(1)} %collective-permute-done.1.refs_1_), custom_call_target="tpu_custom_call" | custom-call | tf_op jit(solution)/shard_map/serve/pallas_call | solution.py:154
  65.7 4.7 %all-to-all-start.2 = ((bf16[16,96,512]{2,1,0:T(8,128)(2,1)}), bf16[16,96,512]{2,1,0:T(8,128)(2,1)}, u32[]{:S(2)}, u32[]{:S(2)}) async-start(bf16[16,96,512]{2,1,0:T(8,128)(2,1)} %bitcast.6), calls=%async_computation.2 | async-start | bytes 3145728 | tf_op jit(solution)/shard_map/all_to_all | solution.py:771
  73.0 4.1 %multiply_convert_fusion.w_hbm = bf16[512,2048]{1,0:T(8,128)(2,1)} fusion(f32[512,2048]{1,0:T(8,128)} %refs_0_.1), kind=kLoop, calls=%fused_computation | loop fusion | flops 2097152 | bytes 6291456 | tf_op jit(solution)/shard_map/convert_element_type | solution.py:786
  80.9 12.2 %all-to-all-done.2 = bf16[16,96,512]{2,1,0:T(8,128)(2,1)} async-done(((bf16[16,96,512]{2,1,0:T(8,128)(2,1)}), bf16[16,96,512]{2,1,0:T(8,128)(2,1)}, u32[]{:S(2)}, u32[]{:S(2)}) %all-to-all-start.2) | async-done | bytes 1572896 | tf_op jit(solution)/shard_map/all_to_all | solution.py:771
  93.1 49.5 %step.1 = (bf16[1536,512]{1,0:T(8,128)(2,1)}, bf16[1280,512]{1,0:T(8,128)(2,1)}, bf16[1280,512]{1,0:T(8,128)(2,1)}, f32[8,32]{1,0:T(8,128)}, f32[8,128]{1,0:T(8,128)}, /*index=5*/f32[8,512]{1,0:T(8,128)}) custom-call(s32[1]{0:T(128)S(6)} %copy.37.len_ref, s32[1]{0:T(128)} %bitcast.3.core_ref, bf16[1536,512]{1,0:T(8,128)(2,1)} %copy-done.3, ...), custom_call_target="tpu_custom_call" | custom-call | flops 49999998976 | bytes 15000000 | tf_op jit(solution)/shard_map/step/pallas_call | solution.py:513
  144.1 6.6 %spread.1 = (bf16[1536,512]{1,0:T(8,128)(2,1)}, bf16[1536,512]{1,0:T(8,128)(2,1)S(1)}) custom-call(s32[1,1536]{1,0:T(1,128)S(1)} %copy-done.6, bf16[1536,512]{1,0:T(8,128)(2,1)S(1)} %copy-done.7), custom_call_target="tpu_custom_call" | custom-call | flops 5000000000 | bytes 6000000 | tf_op jit(solution)/shard_map/spread/pallas_call | solution.py:565
  151.8 3.7 %all-to-all-start.4 = ((bf16[16,96,512]{2,1,0:T(8,128)(2,1)}), bf16[16,96,512]{2,1,0:T(8,128)(2,1)S(1)}, u32[]{:S(2)}, u32[]{:S(2)}) async-start(bf16[16,96,512]{2,1,0:T(8,128)(2,1)} %bitcast.11), calls=%async_computation.4 | async-start | bytes 3145728 | tf_op jit(solution)/shard_map/all_to_all | solution.py:771
  160.4 22.5 %collective-permute-done.4 = bf16[2,320,512]{2,1,0:T(8,128)(2,1)S(1)} collective-permute-done((bf16[2,320,512]{2,1,0:T(8,128)(2,1)}, bf16[2,320,512]{2,1,0:T(8,128)(2,1)S(1)}, u32[]{:S(2)}, u32[]{:S(2)}) %collective-permute-start.4) | collective-permute-done | bytes 655392 | tf_op jit(solution)/shard_map/ppermute | solution.py:627
  184.1 6.1 %collective-permute-done.5 = bf16[320,512]{1,0:T(8,128)(2,1)} collective-permute-done((bf16[320,512]{1,0:T(8,128)(2,1)S(1)}, bf16[320,512]{1,0:T(8,128)(2,1)}, u32[]{:S(2)}, u32[]{:S(2)}) %collective-permute-start.5) | collective-permute-done | bytes 327712 | tf_op jit(solution)/shard_map/ppermute | solution.py:627
  193.1 3.6 %collective-permute-done.6 = bf16[160,512]{1,0:T(8,128)(2,1)S(1)} collective-permute-done((bf16[160,512]{1,0:T(8,128)(2,1)S(1)}, bf16[160,512]{1,0:T(8,128)(2,1)S(1)}, u32[]{:S(2)}, u32[]{:S(2)}) %collective-permute-start.6) | collective-permute-done | bytes 163872 | tf_op jit(solution)/shard_map/ppermute | solution.py:614
  196.8 3.2 %collective-permute-start.7 = (bf16[80,512]{1,0:T(8,128)(2,1)S(1)}, bf16[80,512]{1,0:T(8,128)(2,1)S(1)}, u32[]{:S(2)}, u32[]{:S(2)}) collective-permute-start(bf16[80,512]{1,0:T(8,128)(2,1)S(1)} %dynamic-slice_bitcast_fusion.1), channel_id=1, source_target_pairs={{0,16},{16,0},{1,17},{17,1},{2,18},{18,2},{3,19},{19,3},{4,20},{20... | collective-permute-start | bytes 245768 | tf_op jit(solution)/shard_map/ppermute | solution.py:614
  200.0 6.4 %all-to-all-start.3 = ((bf16[16,96,512]{2,1,0:T(8,128)(2,1)}), bf16[16,96,512]{2,1,0:T(8,128)(2,1)S(1)}, u32[]{:S(2)}, u32[]{:S(2)}) async-start(bf16[16,96,512]{2,1,0:T(8,128)(2,1)} %bitcast.70), calls=%async_computation.3 | async-start | bytes 3145728 | tf_op jit(solution)/shard_map/all_to_all | solution.py:771
  206.5 20.1 %collective-permute-done.9 = bf16[88,512]{1,0:T(8,128)(2,1)S(1)} collective-permute-done((bf16[88,512]{1,0:T(8,128)(2,1)S(1)}, bf16[88,512]{1,0:T(8,128)(2,1)S(1)}, u32[]{:S(2)}, u32[]{:S(2)}) %collective-permute-start.9) | collective-permute-done | bytes 90144 | tf_op jit(solution)/shard_map/ppermute | solution.py:614
  228.5 4.8 %collective-permute-done.10 = bf16[2,88,512]{2,1,0:T(8,128)(2,1)} collective-permute-done((bf16[2,88,512]{2,1,0:T(8,128)(2,1)S(1)}, bf16[2,88,512]{2,1,0:T(8,128)(2,1)}, u32[]{:S(2)}, u32[]{:S(2)}) %collective-permute-start.10) | collective-permute-done | bytes 180256 | tf_op jit(solution)/shard_map/ppermute | solution.py:614
  248.9 27.0 %collective-permute-done.2.far_ref = bf16[784,512]{1,0:T(8,128)(2,1)} collective-permute-done((bf16[784,512]{1,0:T(8,128)(2,1)}, bf16[784,512]{1,0:T(8,128)(2,1)}, u32[]{:S(2)}, u32[]{:S(2)}) %collective-permute-start.2) | collective-permute-done | bytes 802848 | tf_op jit(solution)/shard_map/ppermute | solution.py:799
  276.9 4.6 %update_rows.1 = (f32[784,512]{1,0:T(8,128)}, f32[784,1]{1,0:T(8,128)S(1)}) custom-call(s32[1,1536]{1,0:T(1,128)S(1)} %reshape_squeeze.6.ids_ref, bf16[1536,512]{1,0:T(8,128)(2,1)S(1)} %bitcast.67, bf16[784,512]{1,0:T(8,128)(2,1)} %collective-permute-done.2.far_ref, f32[784,512]{1,0:T(8,128)S(1)} %copy-done, f32[784,1]{1,0:T(8,128)S(1)} %copy-done.1), custom_call_target="tpu_custom_call" | custom-call | tf_op jit(solution)/shard_map/update_rows/pallas_call | solution.py:600
  290.1 14.2 %adam.1 = (f32[512,2048]{1,0:T(8,128)}, f32[512,2048]{1,0:T(8,128)}, f32[512,2048]{1,0:T(8,128)}, f32[512,512]{1,0:T(8,128)}, f32[512,512]{1,0:T(8,128)}, /*index=5*/f32[512,512]{1,0:T(8,128)}) custom-call(s32[1]{0:T(128)} %bitcast.3.core_ref, bf16[1280,512]{1,0:T(8,128)(2,1)} %bitcast.74, bf16[1280,512]{1,0:T(8,128)(2,1)} %collective-permute-done.13.other_ref, ...), custom_call_target="tpu_custom_call" | custom-call | tf_op jit(solution)/shard_map/adam/pallas_call | solution.py:724
  (111 shorter events, 47.1 us)
Async XLA Ops:
  3.8 11.9 %all-to-all-start = ((s32[16,1,192]{2,1,0:T(1,128)}), s32[16,1,192]{2,1,0:T(1,128)S(1)}, u32[]{:S(2)}, u32[]{:S(2)}) async-start(s32[16,1,192]{2,1,0:T(1,128)} %get-tuple-element.35), calls=%async_computation | async-start | bytes 32768 | tf_op jit(solution)/shard_map/all_to_all | solution.py:775
  18.8 47.0 %all-to-all-start.1 = ((bf16[16,96,512]{2,1,0:T(8,128)(2,1)}), bf16[16,96,512]{2,1,0:T(8,128)(2,1)S(1)}, u32[]{:S(2)}, u32[]{:S(2)}) async-start(bf16[16,96,512]{2,1,0:T(8,128)(2,1)} %bitcast.4), calls=%async_computation.1 | async-start | bytes 3145728 | tf_op jit(solution)/shard_map/all_to_all | solution.py:771
  22.5 40.1 %collective-permute-start.1 = (bf16[784,512]{1,0:T(8,128)(2,1)S(1)}, bf16[784,512]{1,0:T(8,128)(2,1)S(1)}, u32[]{:S(2)}, u32[]{:S(2)}) collective-permute-start(bf16[784,512]{1,0:T(8,128)(2,1)S(1)} %convert_element_type.112.refs_0_), channel_id=1, source_target_pairs={{8,24},{16,0},{9,25},{17,1},{10,26},{18,2},{11,27},{19,3},{12,28},... | collective-permute-start | bytes 2408456 | tf_op jit(solution)/shard_map/ppermute | solution.py:779
  23.8 38.8 %collective-permute-start = (bf16[784,512]{1,0:T(8,128)(2,1)S(1)}, bf16[784,512]{1,0:T(8,128)(2,1)S(1)}, u32[]{:S(2)}, u32[]{:S(2)}) collective-permute-start(bf16[784,512]{1,0:T(8,128)(2,1)S(1)} %convert_element_type.112.refs_0_), channel_id=1, source_target_pairs={{0,16},{24,8},{1,17},{25,9},{2,18},{26,10},{3,19},{27,11},{4,20},{... | collective-permute-start | bytes 2408456 | tf_op jit(solution)/shard_map/ppermute | solution.py:778
  65.7 27.3 %all-to-all-start.2 = ((bf16[16,96,512]{2,1,0:T(8,128)(2,1)}), bf16[16,96,512]{2,1,0:T(8,128)(2,1)}, u32[]{:S(2)}, u32[]{:S(2)}) async-start(bf16[16,96,512]{2,1,0:T(8,128)(2,1)} %bitcast.6), calls=%async_computation.2 | async-start | bytes 3145728 | tf_op jit(solution)/shard_map/all_to_all | solution.py:771
  93.1 49.6 %copy-start.6 = (s32[1,1536]{1,0:T(1,128)S(1)}, s32[1,1536]{1,0:T(1,128)}, u32[]{:S(2)}) copy-start(s32[1,1536]{1,0:T(1,128)} %get-tuple-element.36.slotr_ref) | copy-start | bytes 18436
  142.6 13.0 %collective-permute-start.3 = (bf16[1280,512]{1,0:T(8,128)(2,1)}, bf16[1280,512]{1,0:T(8,128)(2,1)}, u32[]{:S(2)}, u32[]{:S(2)}) collective-permute-start(bf16[1280,512]{1,0:T(8,128)(2,1)} %get-tuple-element.44), channel_id=1, source_target_pairs={{0,1},{1,0},{2,3},{3,2},{4,5},{5,4},{6,7},{7,6},{8,9},{9,8},{10,11... | collective-permute-start | bytes 3932168 | tf_op jit(solution)/shard_map/ppermute | solution.py:614
  151.8 48.1 %all-to-all-start.4 = ((bf16[16,96,512]{2,1,0:T(8,128)(2,1)}), bf16[16,96,512]{2,1,0:T(8,128)(2,1)S(1)}, u32[]{:S(2)}, u32[]{:S(2)}) async-start(bf16[16,96,512]{2,1,0:T(8,128)(2,1)} %bitcast.11), calls=%async_computation.4 | async-start | bytes 3145728 | tf_op jit(solution)/shard_map/all_to_all | solution.py:771
  158.5 34.2 %copy-start.18 = (f32[8,32]{1,0:T(8,128)S(1)}, f32[8,32]{1,0:T(8,128)}, u32[]{:S(2)}) copy-start(f32[8,32]{1,0:T(8,128)} %get-tuple-element.45) | copy-start | bytes 3076
  158.5 34.3 %copy-start.19 = (f32[8,512]{1,0:T(8,128)S(1)}, f32[8,512]{1,0:T(8,128)}, u32[]{:S(2)}) copy-start(f32[8,512]{1,0:T(8,128)} %get-tuple-element.46) | copy-start | bytes 49156
  158.5 34.3 %copy-start.20 = (f32[8,128]{1,0:T(8,128)S(1)}, f32[8,128]{1,0:T(8,128)}, u32[]{:S(2)}) copy-start(f32[8,128]{1,0:T(8,128)} %get-tuple-element.47) | copy-start | bytes 12292
  158.5 24.3 %collective-permute-start.4 = (bf16[2,320,512]{2,1,0:T(8,128)(2,1)}, bf16[2,320,512]{2,1,0:T(8,128)(2,1)S(1)}, u32[]{:S(2)}, u32[]{:S(2)}) collective-permute-start(bf16[2,320,512]{2,1,0:T(8,128)(2,1)} %get-tuple-element.63), channel_id=1, source_target_pairs={{0,4},{1,3},{2,6},{3,1},{4,0},{5,7},{6,2},{7,5},{8,12},{9,11},{10,... | collective-permute-start | bytes 1966088 | tf_op jit(solution)/shard_map/ppermute | solution.py:627
  182.9 7.2 %collective-permute-start.5 = (bf16[320,512]{1,0:T(8,128)(2,1)S(1)}, bf16[320,512]{1,0:T(8,128)(2,1)}, u32[]{:S(2)}, u32[]{:S(2)}) collective-permute-start(bf16[320,512]{1,0:T(8,128)(2,1)S(1)} %fusion.5), channel_id=1, source_target_pairs={{0,2},{1,5},{2,0},{3,7},{4,6},{5,1},{6,4},{7,3},{8,10},{9,13},{10,... | collective-permute-start | bytes 983048 | tf_op jit(solution)/shard_map/ppermute | solution.py:627
  191.3 5.4 %collective-permute-start.6 = (bf16[160,512]{1,0:T(8,128)(2,1)S(1)}, bf16[160,512]{1,0:T(8,128)(2,1)S(1)}, u32[]{:S(2)}, u32[]{:S(2)}) collective-permute-start(bf16[160,512]{1,0:T(8,128)(2,1)S(1)} %dynamic-slice_bitcast_fusion), channel_id=1, source_target_pairs={{0,8},{8,0},{1,9},{9,1},{2,10},{10,2},{3,11},{11,3},{4,12},{12,4},... | collective-permute-start | bytes 491528 | tf_op jit(solution)/shard_map/ppermute | solution.py:614
  193.0 13.3 %collective-permute-start.8 = (f32[4,512]{1,0:T(4,128)S(1)}, f32[4,512]{1,0:T(4,128)S(1)}, u32[]{:S(2)}, u32[]{:S(2)}) collective-permute-start(f32[4,512]{1,0:T(4,128)S(1)} %reshape.165), channel_id=1, source_target_pairs={{0,1},{1,0},{2,3},{3,2},{4,5},{5,4},{6,7},{7,6},{8,9},{9,8},{10,11... | collective-permute-start | bytes 24584 | tf_op jit(solution)/shard_map/ppermute | solution.py:811
  196.8 9.6 %collective-permute-start.7 = (bf16[80,512]{1,0:T(8,128)(2,1)S(1)}, bf16[80,512]{1,0:T(8,128)(2,1)S(1)}, u32[]{:S(2)}, u32[]{:S(2)}) collective-permute-start(bf16[80,512]{1,0:T(8,128)(2,1)S(1)} %dynamic-slice_bitcast_fusion.1), channel_id=1, source_target_pairs={{0,16},{16,0},{1,17},{17,1},{2,18},{18,2},{3,19},{19,3},{4,20},{20... | collective-permute-start | bytes 245768 | tf_op jit(solution)/shard_map/ppermute | solution.py:614
  200.0 48.9 %all-to-all-start.3 = ((bf16[16,96,512]{2,1,0:T(8,128)(2,1)}), bf16[16,96,512]{2,1,0:T(8,128)(2,1)S(1)}, u32[]{:S(2)}, u32[]{:S(2)}) async-start(bf16[16,96,512]{2,1,0:T(8,128)(2,1)} %bitcast.70), calls=%async_computation.3 | async-start | bytes 3145728 | tf_op jit(solution)/shard_map/all_to_all | solution.py:771
  206.4 20.2 %collective-permute-start.9 = (bf16[88,512]{1,0:T(8,128)(2,1)S(1)}, bf16[88,512]{1,0:T(8,128)(2,1)S(1)}, u32[]{:S(2)}, u32[]{:S(2)}) collective-permute-start(bf16[88,512]{1,0:T(8,128)(2,1)S(1)} %pad_maximum_fusion.4), channel_id=1, source_target_pairs={{0,16},{16,0},{1,17},{17,1},{2,18},{18,2},{3,19},{19,3},{4,20},{20... | collective-permute-start | bytes 270344 | tf_op jit(solution)/shard_map/ppermute | solution.py:614
  226.7 6.6 %collective-permute-start.10 = (bf16[2,88,512]{2,1,0:T(8,128)(2,1)S(1)}, bf16[2,88,512]{2,1,0:T(8,128)(2,1)}, u32[]{:S(2)}, u32[]{:S(2)}) collective-permute-start(bf16[2,88,512]{2,1,0:T(8,128)(2,1)S(1)} %pad_maximum_fusion.3), channel_id=1, source_target_pairs={{0,8},{8,0},{1,9},{9,1},{2,10},{10,2},{3,11},{11,3},{4,12},{12,4},... | collective-permute-start | bytes 540680 | tf_op jit(solution)/shard_map/ppermute | solution.py:614
  235.0 8.2 %collective-permute-start.11 = (bf16[4,88,512]{2,1,0:T(8,128)(2,1)}, bf16[4,88,512]{2,1,0:T(8,128)(2,1)}, u32[]{:S(2)}, u32[]{:S(2)}) collective-permute-start(bf16[4,88,512]{2,1,0:T(8,128)(2,1)} %bitcast.30), channel_id=1, source_target_pairs={{0,2},{1,5},{2,0},{3,7},{4,6},{5,1},{6,4},{7,3},{8,10},{9,13},{10,... | collective-permute-start | bytes 1081352 | tf_op jit(solution)/shard_map/ppermute | solution.py:627
  239.9 36.0 %copy-start = (f32[784,512]{1,0:T(8,128)S(1)}, f32[784,512]{1,0:T(8,128)}, u32[]{:S(2)}) copy-start(f32[784,512]{1,0:T(8,128)} %table_ref.1) | copy-start | bytes 4816900
  239.9 36.0 %collective-permute-start.2 = (bf16[784,512]{1,0:T(8,128)(2,1)}, bf16[784,512]{1,0:T(8,128)(2,1)}, u32[]{:S(2)}, u32[]{:S(2)}) collective-permute-start(bf16[784,512]{1,0:T(8,128)(2,1)} %row_sums.1), channel_id=1, source_target_pairs={{0,16},{16,0},{1,17},{17,1},{2,18},{18,2},{3,19},{19,3},{4,20},{20... | collective-permute-start | bytes 2408456 | tf_op jit(solution)/shard_map/ppermute | solution.py:799
  246.9 37.1 %collective-permute-start.12 = (bf16[2,4,88,512]{3,2,1,0:T(8,128)(2,1)}, bf16[2,4,88,512]{3,2,1,0:T(8,128)(2,1)}, u32[]{:S(2)}, u32[]{:S(2)}) collective-permute-start(bf16[2,4,88,512]{3,2,1,0:T(8,128)(2,1)} %pad_maximum_fusion.1), channel_id=1, source_target_pairs={{0,4},{1,3},{2,6},{3,1},{4,0},{5,7},{6,2},{7,5},{8,12},{9,11},{10,... | collective-permute-start | bytes 2162696 | tf_op jit(solution)/shard_map/ppermute | solution.py:627
  286.9 3.2 %collective-permute-start.13 = (bf16[1280,512]{1,0:T(8,128)(2,1)S(1)}, bf16[1280,512]{1,0:T(8,128)(2,1)}, u32[]{:S(2)}, u32[]{:S(2)}) collective-permute-start(bf16[1280,512]{1,0:T(8,128)(2,1)S(1)} %bitcast.73), channel_id=1, source_target_pairs={{0,1},{1,0},{2,3},{3,2},{4,5},{5,4},{6,7},{7,6},{8,9},{9,8},{10,11... | collective-permute-start | bytes 3932168 | tf_op jit(solution)/shard_map/ppermute | solution.py:614
  (16 other events, 52.0 us)
